TPU v7x, 32 devices: a whole 2x2x4 slice. The times are simulated.
32 devices in a mesh: dp: 16 (over z, y, x), tensor: 2 (over core).
Axes of the slice: x: 2, y: 2, z: 4, core: 2. Of those that a mesh axis runs over, the one named last changes fastest.
Arguments:
- tokens: bfloat16 [16, 2, 128, 1152], P('dp', 'tensor'), may hold values from -6 to 6
- cond: bfloat16 [1, 1152], replicated, may hold values from -6 to 6
- out_grad: bfloat16 [16, 2, 128, 1152], P(None, 'tensor', 'dp'), may hold values from -6 to 6
- w_qkv: bfloat16 [2, 1152, 3, 1152], P(None, 'dp', None, 'tensor'), may hold values from -0.1875 to 0.1875
- w_out: bfloat16 [2, 1152, 1152], P(None, 'tensor', 'dp'), may hold values from -0.75 to 0.75
- w_fc1: bfloat16 [2, 1152, 4608], P(None, 'dp', 'tensor'), may hold values from -0.1875 to 0.1875
- w_fc2: bfloat16 [2, 4608, 1152], P(None, 'tensor', 'dp'), may hold values from -0.125 to 0.125
- w_ada: bfloat16 [2, 1152, 6, 1152], P(None, ('dp', 'tensor')), may hold values from -0.1875 to 0.1875
- b_ada: bfloat16 [2, 6, 1152], P(None, None, ('dp', 'tensor')), may hold values from -3 to 3
- b_proj: bfloat16 [2, 4, 1152], P(None, None, ('dp', 'tensor')), may hold values from -3 to 3
- b_fc1: bfloat16 [2, 4608], P(None, ('dp', 'tensor')), may hold values from -3 to 3
Outputs:
- output: bfloat16 [16, 2, 128, 1152], P(None, 'tensor', 'dp')
- tokens_grad: float32 [16, 2, 128, 1152], P('dp', 'tensor')
- cond_grad: float32 [1, 1152], P(None, ('dp', 'tensor'))
- w_qkv_grad: float32 [2, 1152, 3, 1152], P(None, 'dp', None, 'tensor')
- w_out_grad: float32 [2, 1152, 1152], P(None, 'tensor', 'dp')
- w_fc1_grad: float32 [2, 1152, 4608], P(None, 'dp', 'tensor')
- w_fc2_grad: float32 [2, 4608, 1152], P(None, 'tensor', 'dp')
- w_ada_grad: float32 [2, 1152, 6, 1152], P(None, ('dp', 'tensor'))
- b_ada_grad: float32 [2, 6, 1152], P(None, None, ('dp', 'tensor'))
- b_proj_grad: float32 [2, 4, 1152], P(None, None, ('dp', 'tensor'))
- b_fc1_grad: float32 [2, 4608], P(None, ('dp', 'tensor'))
All inputs are finite; a program needn't handle non-finite values.
Results may differ from a plain program's by a relative error of at most 0.03.
Values may be sent and summed in bfloat16 or wider, within the bound.
No kernel may reach another device: no remote copies, remote signals or barrier semaphores. Data moves between devices by JAX's collectives and lax.ppermute only.
A program may use at most 256 MiB of HBM per device.

v0:
```python
import jax
import jax.numpy as jnp
from jax import lax
from jax.sharding import PartitionSpec as P

HEAD_DIM = 72
FRAMES = 16


epsilon = 1e-06
highest = lax.Precision.HIGHEST
spatial_forms = ("flhe,fmhe->fhlm", "fhlm,fmhe->flhe", "fhlm,flhe->fmhe")
temporal_forms = ("clphe,cmphe->cphlm", "cphlm,cmphe->clphe", "cphlm,clphe->cmphe")


def normalize(values):
    average = jnp.mean(values, axis=-1, keepdims=True)
    centred = values - average
    inverse = lax.rsqrt(jnp.mean(centred * centred, axis=-1, keepdims=True) + epsilon)
    return (centred * inverse, inverse)


def normalize_back(normed, inverse, upstream):
    first_moment = jnp.mean(upstream, axis=-1, keepdims=True)
    second_moment = jnp.mean(upstream * normed, axis=-1, keepdims=True)
    return inverse * (upstream - first_moment - normed * second_moment)


def product(left_side, right_side):
    return jnp.dot(left_side, right_side, preferred_element_type=jnp.float32)


def product_left(left_side, right_side):
    return lax.dot_general(
        left_side, right_side, (((0,), (0,)), ((), ())), preferred_element_type=jnp.float32
    )


def product_right(left_side, right_side):
    return lax.dot_general(
        left_side, right_side, (((1,), (1,)), ((), ())), preferred_element_type=jnp.float32
    )


def gelu_tanh(values):
    return jax.nn.gelu(values, approximate=True)


def row_gather(values):
    return lax.all_gather(values, "tensor", axis=1, tiled=True)


def row_scatter(values):
    return lax.psum_scatter(
        values.astype(jnp.bfloat16), "tensor", scatter_dimension=1, tiled=True
    ).astype(jnp.float32)


def grad_gather(values):
    return lax.all_gather(values, "tensor", axis=1, tiled=True)


def grad_scatter(values):
    return lax.psum_scatter(
        values.astype(jnp.bfloat16), "tensor", scatter_dimension=1, tiled=True
    ).astype(jnp.float32)


def gather_layer(w_qkv, w_out, w_fc1, w_fc2, layer_index):
    return (
        lax.all_gather(w_qkv[layer_index], "dp", axis=0, tiled=True),
        lax.all_gather(w_out[layer_index], "dp", axis=1, tiled=True),
        lax.all_gather(w_fc1[layer_index], "dp", axis=0, tiled=True),
        lax.all_gather(w_fc2[layer_index], "dp", axis=1, tiled=True),
    )


def gather_layer_again(w_qkv, w_out, w_fc1, w_fc2, layer_index):
    return (
        lax.all_gather(w_qkv[layer_index], "dp", axis=0, tiled=True),
        lax.all_gather(w_out[layer_index], "dp", axis=1, tiled=True),
        lax.all_gather(w_fc1[layer_index], "dp", axis=0, tiled=True),
        lax.all_gather(w_fc2[layer_index], "dp", axis=1, tiled=True),
    )


def reduce_layer(gradients):
    return (
        lax.psum_scatter(gradients[0], "dp", scatter_dimension=0, tiled=True),
        lax.psum_scatter(gradients[1], "dp", scatter_dimension=1, tiled=True),
        lax.psum_scatter(gradients[2], "dp", scatter_dimension=0, tiled=True),
        lax.psum_scatter(gradients[3], "dp", scatter_dimension=1, tiled=True),
    )


def layer_biases(proj_full, hidden_full, layer_index, head_width, hidden_width):
    tensor_index = lax.axis_index("tensor")
    bias_query = lax.dynamic_slice_in_dim(
        proj_full[layer_index, 0], tensor_index * head_width, head_width
    ).astype(jnp.float32)
    bias_value = lax.dynamic_slice_in_dim(
        proj_full[layer_index, 1], tensor_index * head_width, head_width
    ).astype(jnp.float32)
    bias_out = proj_full[layer_index, 2].astype(jnp.float32)
    bias_fc2 = proj_full[layer_index, 3].astype(jnp.float32)
    bias_fc1 = lax.dynamic_slice_in_dim(
        hidden_full[layer_index], tensor_index * hidden_width, hidden_width
    ).astype(jnp.float32)
    return (bias_query, bias_value, bias_out, bias_fc2, bias_fc1)


def widen(local_part, full_width):
    offset = lax.axis_index("tensor") * local_part.shape[0]
    return lax.dynamic_update_slice_in_dim(
        jnp.zeros((full_width,), jnp.float32), local_part, offset, 0
    )


def split_heads(flat_rows, full_shape, across):
    heads_dev = flat_rows.shape[1] // HEAD_DIM
    if across:
        return flat_rows.reshape(
            full_shape[0] // FRAMES, FRAMES, full_shape[1] * full_shape[2], heads_dev, HEAD_DIM
        )
    return flat_rows.reshape(full_shape[0], full_shape[1] * full_shape[2], heads_dev, HEAD_DIM)


def attend(query, keys_rows, value_rows, forms):
    score_scale = HEAD_DIM ** (-0.5)
    scores = (
        jnp.einsum(forms[0], query, keys_rows, preferred_element_type=jnp.float32) * score_scale
    )
    peak_score = jnp.max(scores, axis=-1, keepdims=True)
    exponent = jnp.exp(scores - peak_score)
    row_total = jnp.sum(exponent, axis=-1, keepdims=True)
    weights = (exponent / row_total).astype(jnp.bfloat16)
    attended = jnp.einsum(forms[1], weights, value_rows, preferred_element_type=jnp.float32)
    return (attended, peak_score + jnp.log(row_total))


def attend_back(query, keys_rows, value_rows, log_total, upstream, forms):
    score_scale = HEAD_DIM ** (-0.5)
    scores = (
        jnp.einsum(forms[0], query, keys_rows, preferred_element_type=jnp.float32) * score_scale
    )
    probs = jnp.exp(scores - log_total)
    value_grad = jnp.einsum(
        forms[2], probs.astype(jnp.bfloat16), upstream, preferred_element_type=jnp.float32
    )
    prob_grad = jnp.einsum(forms[0], upstream, value_rows, preferred_element_type=jnp.float32)
    centre = jnp.sum(probs * prob_grad, axis=-1, keepdims=True)
    score_grad = (probs * (prob_grad - centre)).astype(jnp.bfloat16)
    query_grad = (
        jnp.einsum(forms[1], score_grad, keys_rows, preferred_element_type=jnp.float32)
        * score_scale
    )
    keys_grad = (
        jnp.einsum(forms[2], score_grad, query, preferred_element_type=jnp.float32) * score_scale
    )
    return (query_grad, keys_grad, value_grad)


def block_forward(inputs, modulation, weights, biases, across):
    wqkv, wout, wfc1, wfc2 = weights
    bias_query, bias_value, bias_out, bias_fc2, bias_fc1 = biases
    mod_parts = [modulation[:, index][:, None, None, :] for index in range(6)]
    forms = temporal_forms if across else spatial_forms
    normed_attn, inverse_attn = normalize(inputs)
    hidden_attn = (normed_attn * (1.0 + mod_parts[1]) + mod_parts[0]).astype(jnp.bfloat16)
    full_attn = row_gather(hidden_attn)
    full_shape = full_attn.shape
    row_count = full_shape[0] * full_shape[1] * full_shape[2]
    flat_attn = full_attn.reshape(row_count, full_shape[3])
    head_width = wqkv.shape[2]
    projected = product(flat_attn, wqkv.reshape(wqkv.shape[0], 3 * head_width)).reshape(
        row_count, 3, head_width
    )
    query = split_heads((projected[:, 0] + bias_query).astype(jnp.bfloat16), full_shape, across)
    keys_rows = split_heads(projected[:, 1].astype(jnp.bfloat16), full_shape, across)
    value_rows = split_heads(
        (projected[:, 2] + bias_value).astype(jnp.bfloat16), full_shape, across
    )
    attended, log_total = attend(query, keys_rows, value_rows, forms)
    attended_low = attended.astype(jnp.bfloat16).reshape(row_count, head_width)
    branch_attn = row_scatter(product(attended_low, wout).reshape(full_shape)) + bias_out
    middle = inputs + mod_parts[2] * branch_attn
    normed_mlp, inverse_mlp = normalize(middle)
    hidden_mlp = (normed_mlp * (1.0 + mod_parts[4]) + mod_parts[3]).astype(jnp.bfloat16)
    full_mlp = row_gather(hidden_mlp).reshape(row_count, full_shape[3])
    inner_pre = product(full_mlp, wfc1) + bias_fc1
    activated = gelu_tanh(inner_pre).astype(jnp.bfloat16)
    branch_mlp = row_scatter(product(activated, wfc2).reshape(full_shape)) + bias_fc2
    result = middle + mod_parts[5] * branch_mlp
    saved = (
        normed_attn,
        inverse_attn,
        flat_attn,
        query,
        keys_rows,
        value_rows,
        log_total,
        attended_low,
        branch_attn,
        normed_mlp,
        inverse_mlp,
        full_mlp,
        inner_pre,
        activated,
        branch_mlp,
        full_shape,
    )
    return (result, saved)


def block_backward(upstream, saved, modulation, weights, across):
    (
        normed_attn,
        inverse_attn,
        flat_attn,
        query,
        keys_rows,
        value_rows,
        log_total,
        attended_low,
        branch_attn,
        normed_mlp,
        inverse_mlp,
        full_mlp,
        inner_pre,
        activated,
        branch_mlp,
        full_shape,
    ) = saved
    wqkv, wout, wfc1, wfc2 = weights
    forms = temporal_forms if across else spatial_forms
    mod_parts = [modulation[:, index][:, None, None, :] for index in range(6)]
    row_count, width = flat_attn.shape
    head_width = wqkv.shape[2]
    gate_mlp_grad = jnp.sum(upstream * branch_mlp, axis=(1, 2))
    mlp_out_grad = (upstream * mod_parts[5]).astype(jnp.bfloat16)
    fc2_bias_grad = jnp.sum(mlp_out_grad.astype(jnp.float32), axis=(0, 1, 2))
    mlp_full_grad = grad_gather(mlp_out_grad).reshape(row_count, width)
    fc2_weight_grad = product_left(activated, mlp_full_grad)
    activated_grad = product_right(mlp_full_grad, wfc2)
    inner_grad = jax.vjp(gelu_tanh, inner_pre)[1](activated_grad)[0].astype(jnp.bfloat16)
    fc1_bias_local = jnp.sum(inner_grad.astype(jnp.float32), axis=0)
    fc1_weight_grad = product_left(full_mlp, inner_grad)
    hidden_mlp_grad = grad_scatter(product_right(inner_grad, wfc1).reshape(full_shape))
    scale_mlp_grad = jnp.sum(hidden_mlp_grad * normed_mlp, axis=(1, 2))
    shift_mlp_grad = jnp.sum(hidden_mlp_grad, axis=(1, 2))
    middle_grad = upstream + normalize_back(
        normed_mlp, inverse_mlp, hidden_mlp_grad * (1.0 + mod_parts[4])
    )
    gate_attn_grad = jnp.sum(middle_grad * branch_attn, axis=(1, 2))
    attn_out_grad = (middle_grad * mod_parts[2]).astype(jnp.bfloat16)
    out_bias_grad = jnp.sum(attn_out_grad.astype(jnp.float32), axis=(0, 1, 2))
    attn_full_grad = grad_gather(attn_out_grad).reshape(row_count, width)
    out_weight_grad = product_left(attended_low, attn_full_grad)
    attended_grad = product_right(attn_full_grad, wout).astype(jnp.bfloat16)
    query_grad, keys_grad, value_grad = attend_back(
        query,
        keys_rows,
        value_rows,
        log_total,
        split_heads(attended_grad, full_shape, across),
        forms,
    )
    qkv_grad = jnp.stack(
        [
            part.reshape(row_count, head_width).astype(jnp.bfloat16)
            for part in (query_grad, keys_grad, value_grad)
        ],
        axis=1,
    )
    qkv_flat = qkv_grad.reshape(row_count, 3 * head_width)
    qkv_weight_grad = product_left(flat_attn, qkv_flat).reshape(width, 3, head_width)
    hidden_attn_grad = grad_scatter(
        product_right(qkv_flat, wqkv.reshape(width, 3 * head_width)).reshape(full_shape)
    )
    scale_attn_grad = jnp.sum(hidden_attn_grad * normed_attn, axis=(1, 2))
    shift_attn_grad = jnp.sum(hidden_attn_grad, axis=(1, 2))
    input_grad = middle_grad + normalize_back(
        normed_attn, inverse_attn, hidden_attn_grad * (1.0 + mod_parts[1])
    )
    mod_grad = jnp.stack(
        [
            shift_attn_grad,
            scale_attn_grad,
            gate_attn_grad,
            shift_mlp_grad,
            scale_mlp_grad,
            gate_mlp_grad,
        ],
        axis=1,
    )
    query_bias = jnp.sum(qkv_grad[:, 0].astype(jnp.float32), axis=0)
    value_bias = jnp.sum(qkv_grad[:, 2].astype(jnp.float32), axis=0)
    proj_grad = jnp.stack(
        [widen(query_bias, width), widen(value_bias, width), out_bias_grad, fc2_bias_grad]
    )
    hidden_grad = widen(fc1_bias_local, fc1_bias_local.shape[0] * lax.axis_size("tensor"))
    weight_grads = (qkv_weight_grad, out_weight_grad, fc1_weight_grad, fc2_weight_grad)
    return (input_grad, mod_grad, weight_grads, proj_grad, hidden_grad)


def per_device(tokens, cond, out_grad, w_qkv, w_out, w_fc1, w_fc2, w_ada, b_ada, b_proj, b_fc1):
    all_devices = lax.axis_size(("dp", "tensor"))
    flat_index = lax.axis_index(("dp", "tensor"))
    width = tokens.shape[3]
    clip_count = cond.shape[0]
    head_width = w_qkv.shape[3]
    hidden_width = w_fc1.shape[2]
    hidden_total = hidden_width * lax.axis_size("tensor")
    own_width = width // all_devices
    own_start = flat_index * own_width
    own_hidden = hidden_total // all_devices
    cond_float = cond.astype(jnp.float32)
    gated_low = jax.nn.silu(cond_float).astype(jnp.bfloat16)
    gated_own = lax.dynamic_slice_in_dim(gated_low, own_start, own_width, 1)
    ada_bias_full, proj_full, hidden_full = (
        lax.all_gather(b_ada, ("dp", "tensor"), axis=2, tiled=True),
        lax.all_gather(b_proj, ("dp", "tensor"), axis=2, tiled=True),
        lax.all_gather(b_fc1, ("dp", "tensor"), axis=1, tiled=True),
    )
    partial_mod = jnp.einsum("cd,ldkj->lckj", gated_own, w_ada, preferred_element_type=jnp.float32)
    modulation = lax.psum(partial_mod, ("dp", "tensor"))
    modulation = modulation + ada_bias_full.astype(jnp.float32)[:, None]
    frames_dev = tokens.shape[0]
    frame_ids = lax.axis_index("dp") * frames_dev + jnp.arange(frames_dev, dtype=jnp.int32)
    onehot = (
        frame_ids[:, None] // FRAMES == jnp.arange(clip_count, dtype=jnp.int32)[None, :]
    ).astype(jnp.float32)
    first_mod = jnp.einsum("gc,ckd->gkd", onehot, modulation[0], precision=highest)
    second_mod = jnp.repeat(modulation[1], FRAMES, axis=0)
    first_in = tokens.astype(jnp.float32)
    first_weights = gather_layer(w_qkv, w_out, w_fc1, w_fc2, 0)
    first_biases = layer_biases(proj_full, hidden_full, 0, head_width, hidden_width)
    first_out, first_saved = block_forward(first_in, first_mod, first_weights, first_biases, False)
    second_in = lax.all_to_all(
        first_out.astype(jnp.bfloat16), "dp", split_axis=2, concat_axis=0, tiled=True
    ).astype(jnp.float32)
    second_weights = gather_layer(w_qkv, w_out, w_fc1, w_fc2, 1)
    second_biases = layer_biases(proj_full, hidden_full, 1, head_width, hidden_width)
    second_out, second_saved = block_forward(
        second_in, second_mod, second_weights, second_biases, True
    )
    output = second_out.astype(jnp.bfloat16)
    second_back = gather_layer_again(w_qkv, w_out, w_fc1, w_fc2, 1)
    second_saved = block_forward(second_in, second_mod, second_back, second_biases, True)[1]
    second_grad, second_dmod, second_wgrads, second_proj, second_hidden = block_backward(
        out_grad.astype(jnp.float32), second_saved, second_mod, second_back, True
    )
    second_reduced = reduce_layer(second_wgrads)
    first_upstream = lax.all_to_all(
        second_grad.astype(jnp.bfloat16), "dp", split_axis=0, concat_axis=2, tiled=True
    ).astype(jnp.float32)
    first_back = gather_layer_again(w_qkv, w_out, w_fc1, w_fc2, 0)
    first_saved = block_forward(first_in, first_mod, first_back, first_biases, False)[1]
    first_grad, first_dmod, first_wgrads, first_proj, first_hidden = block_backward(
        first_upstream, first_saved, first_mod, first_back, False
    )
    first_reduced = reduce_layer(first_wgrads)
    dmod_clips = (
        jnp.einsum("gc,gkd->ckd", onehot, first_dmod, precision=highest),
        jnp.sum(second_dmod.reshape(clip_count, FRAMES, 6, width), axis=1),
    )
    proj_grads = (first_proj, second_proj)
    hidden_grads = (first_hidden, second_hidden)
    summed_mod, summed_proj, summed_hidden = lax.psum(
        (jnp.stack(dmod_clips), jnp.stack(proj_grads), jnp.stack(hidden_grads)), ("dp", "tensor")
    )
    w_ada_grad = jnp.einsum(
        "cd,lckj->ldkj", gated_own.astype(jnp.float32), summed_mod, precision=highest
    )
    b_ada_grad = lax.dynamic_slice_in_dim(jnp.sum(summed_mod, axis=1), own_start, own_width, 2)
    b_proj_grad = lax.dynamic_slice_in_dim(summed_proj, own_start, own_width, 2)
    b_fc1_grad = lax.dynamic_slice_in_dim(summed_hidden, flat_index * own_hidden, own_hidden, 1)
    silu_grad = jnp.einsum(
        "lckj,ldkj->cd", summed_mod, w_ada.astype(jnp.float32), precision=highest
    )
    cond_own = lax.dynamic_slice_in_dim(cond_float, own_start, own_width, 1)
    cond_grad = jax.vjp(jax.nn.silu, cond_own)[1](silu_grad)[0]
    w_qkv_grad = jnp.stack([first_reduced[0], second_reduced[0]])
    w_out_grad = jnp.stack([first_reduced[1], second_reduced[1]])
    w_fc1_grad = jnp.stack([first_reduced[2], second_reduced[2]])
    w_fc2_grad = jnp.stack([first_reduced[3], second_reduced[3]])
    return (
        output,
        first_grad,
        cond_grad,
        w_qkv_grad,
        w_out_grad,
        w_fc1_grad,
        w_fc2_grad,
        w_ada_grad,
        b_ada_grad,
        b_proj_grad,
        b_fc1_grad,
    )


def solution(mesh):
    return jax.shard_map(
        per_device,
        mesh=mesh,
        in_specs=(
            P("dp", "tensor", None, None),
            P(),
            P(None, "tensor", "dp", None),
            P(None, "dp", None, "tensor"),
            P(None, "tensor", "dp"),
            P(None, "dp", "tensor"),
            P(None, "tensor", "dp"),
            P(None, ("dp", "tensor"), None, None),
            P(None, None, ("dp", "tensor")),
            P(None, None, ("dp", "tensor")),
            P(None, ("dp", "tensor")),
        ),
        out_specs=(
            P(None, "tensor", "dp", None),
            P("dp", "tensor", None, None),
            P(None, ("dp", "tensor")),
            P(None, "dp", None, "tensor"),
            P(None, "tensor", "dp"),
            P(None, "dp", "tensor"),
            P(None, "tensor", "dp"),
            P(None, ("dp", "tensor"), None, None),
            P(None, None, ("dp", "tensor")),
            P(None, None, ("dp", "tensor")),
            P(None, ("dp", "tensor")),
        ),
        check_vma=False,
    )
```

profile of v0, /device:TPU:0, one launch (start us, length us, event | category | flops | bytes accessed | tf_op | source)
XLA Modules:
  0.0 2405.5 jit_solution(14349272981216917003)
XLA Ops:
  12.7 45.7 %all_gather.72 = bf16[2,4,1152]{1,0,2:T(2,128)(2,1)S(1)} all-gather(bf16[2,4,36]{1,0,2:T(2,128)(2,1)S(1)} %copy.213), channel_id=1, replica_groups=mesh['dp'=16,'tensor'=2] {'dp','tensor'}, dimensions={2}, use_global_device_ids=true | all-gather | bytes 19008 | tf_op jit(solution)/shard_map/all_gather | solution.py:322
  58.3 42.5 %all_gather.69 = bf16[2,6,1152]{1,0,2:T(2,128)(2,1)} all-gather(bf16[2,6,36]{1,0,2:T(2,128)(2,1)S(1)} %copy.210), channel_id=1, replica_groups=mesh['dp'=16,'tensor'=2] {'dp','tensor'}, dimensions={2}, use_global_device_ids=true | all-gather | bytes 28512 | tf_op jit(solution)/shard_map/all_gather | solution.py:321
  102.3 55.0 %psum.28 = f32[2,1,6,1152]{2,0,3,1:T(2,128)} all-reduce(f32[2,1,6,1152]{2,0,3,1:T(2,128)S(1)} %bitcast.327), channel_id=1, replica_groups=mesh['dp'=16,'tensor'=2] {'dp','tensor'}, use_global_device_ids=true, to_apply=%region_0.1 | all-reduce | flops 13824 | bytes 110592 | tf_op jit(solution)/shard_map/psum | solution.py:326
  193.3 39.8 %all-gather.8 = bf16[32,144,2]{1,2,0:T(2,128)(2,1)S(1)} all-gather(bf16[1,144,2]{1,2,0:T(2,128)(2,1)S(1)} %bitcast.375), channel_id=1, replica_groups=mesh['dp'=16,'tensor'=2] {'dp','tensor'}, dimensions={0}, use_global_device_ids=true | all-gather | bytes 19008 | tf_op jit(solution)/shard_map/all_gather | solution.py:323
  233.9 24.0 fusion.137
  264.4 22.0 all-gather.22.cloned.1.call-done
  292.2 81.4 %all-gather.24.cloned.1.call-done = bf16[1,2304,1152]{1,2,0:T(8,128)(2,1)} async-done(((bf16[1,2304,72]{1,2,0:T(8,128)(2,1)}), bf16[1,2304,1152]{1,2,0:T(8,128)(2,1)}) %all-gather.24.cloned.1.call-update) | async-done | bytes 5308432 | tf_op jit(solution)/shard_map/all_gather | solution.py:74
  402.3 25.8 %fusion.144 = (f32[1152]{0:T(1024)}, f32[1152]{0:T(1024)}, f32[1152]{0:T(1024)}, f32[1152]{0:T(1024)S(1)}, f32[1152]{0:T(1024)S(1)}, /*index=5*/f32[1152]{0:T(1024)}) fusion(f32[2,1,6,1152]{2,0,3,1:T(2,128)} %copy-done.5), kind=kLoop, calls=%fused_computation.231 | loop fusion | flops 2304 | bytes 55296 | tf_op jit(solution)/shard_map/add | solution.py:188
  428.1 43.1 %all-gather.26.cloned.1.call-done = bf16[1,1152,3,576]{3,1,2,0:T(8,128)(2,1)} async-done(((bf16[1,72,3,576]{3,1,2,0:T(8,128)(2,1)}), bf16[1,1152,3,576]{3,1,2,0:T(8,128)(2,1)}) %all-gather.26.cloned.1.call-update) | async-done | bytes 3981328 | tf_op jit(solution)/shard_map/all_gather | solution.py:71
  522.1 8.1 all-gather.28.cloned.1.call-done
  540.6 10.3 all-reduce.13.cloned.1.call-done
  557.4 83.4 %all-gather.30.cloned.1.call-done = bf16[1,1152,2304]{2,1,0:T(8,128)(2,1)} async-done(((bf16[1,72,2304]{2,1,0:T(8,128)(2,1)}), bf16[1,1152,2304]{2,1,0:T(8,128)(2,1)}) %all-gather.30.cloned.1.call-update) | async-done | bytes 5308432 | tf_op jit(solution)/shard_map/all_gather | solution.py:73
  646.5 82.3 %all-gather.32.cloned.1.call-done = bf16[1,2304,1152]{1,2,0:T(8,128)(2,1)} async-done(((bf16[1,2304,72]{1,2,0:T(8,128)(2,1)}), bf16[1,2304,1152]{1,2,0:T(8,128)(2,1)}) %all-gather.32.cloned.1.call-update) | async-done | bytes 5308432 | tf_op jit(solution)/shard_map/all_gather | solution.py:74
  744.3 11.3 all-reduce.15.cloned.1.call-done
  807.0 17.7 all-reduce.19.cloned.1.call-done
  952.5 75.2 %all-reduce.17.cloned.1.call-done = (f32[2,1,6,1152]{3,2,1,0:T(8,128)}, f32[2,4,1152]{2,1,0:T(4,128)}, f32[2,4608]{1,0:T(2,128)}) async-done(((f32[2,1,6,1152]{3,2,1,0:T(8,128)}, f32[2,4,1152]{2,1,0:T(4,128)}, f32[2,4608]{1,0:T(2,128)}), (f32[2,1,6,1152]{3,2,1,0:T(8,128)}, f32[2,4,1152]{2,1,0:T(4,128)}, f32[2,4608]{1,0:T(2,128)})) %all-reduce.17.cloned.1.call-update) | async-done | bytes 129040 | tf_op jit(solution)/shard_map/psum | solution.py:369
  1036.9 129.0 %reduce-scatter.43.cloned.1.call-done = f32[576,72]{0,1:T(8,128)} async-done(((f32[576,1152]{0,1:T(8,128)}), f32[576,72]{0,1:T(8,128)}) %reduce-scatter.43.cloned.1.call-update) | async-done | bytes 165904
  1165.9 134.7 %reduce-scatter.41.cloned.1.call-done = f32[576,72]{0,1:T(8,128)} async-done(((f32[576,1152]{0,1:T(8,128)}), f32[576,72]{0,1:T(8,128)}) %reduce-scatter.41.cloned.1.call-update) | async-done | bytes 165904
  1302.4 171.4 %reduce-scatter.31.cloned.1.call-done = f32[72,3,576]{2,0,1:T(8,128)} async-done(((f32[1152,3,576]{2,0,1:T(8,128)}), f32[72,3,576]{2,0,1:T(8,128)}) %reduce-scatter.31.cloned.1.call-update) | async-done | bytes 497680 | tf_op jit(solution)/shard_map/reduce_scatter | solution.py:89
  1473.7 172.6 %reduce-scatter.29.cloned.1.call-done = f32[72,3,576]{2,0,1:T(8,128)} async-done(((f32[1152,3,576]{2,0,1:T(8,128)}), f32[72,3,576]{2,0,1:T(8,128)}) %reduce-scatter.29.cloned.1.call-update) | async-done | bytes 497680 | tf_op jit(solution)/shard_map/reduce_scatter | solution.py:89
  1648.6 184.8 %reduce-scatter.39.cloned.1.call-done = f32[2304,72]{0,1:T(8,128)} async-done(((f32[2304,1152]{0,1:T(8,128)}), f32[2304,72]{0,1:T(8,128)}) %reduce-scatter.39.cloned.1.call-update) | async-done | bytes 663568 | tf_op jit(solution)/shard_map/reduce_scatter | solution.py:92
  1833.4 187.2 %reduce-scatter.37.cloned.1.call-done = f32[2304,72]{0,1:T(8,128)} async-done(((f32[2304,1152]{0,1:T(8,128)}), f32[2304,72]{0,1:T(8,128)}) %reduce-scatter.37.cloned.1.call-update) | async-done | bytes 663568 | tf_op jit(solution)/shard_map/reduce_scatter | solution.py:92
  2023.1 185.8 %reduce-scatter.35.cloned.1.call-done = f32[72,2304]{1,0:T(8,128)} async-done(((f32[1152,2304]{1,0:T(8,128)}), f32[72,2304]{1,0:T(8,128)}) %reduce-scatter.35.cloned.1.call-update) | async-done | bytes 663568 | tf_op jit(solution)/shard_map/reduce_scatter | solution.py:91
  2208.9 187.2 %reduce-scatter.33.cloned.1.call-done = f32[72,2304]{1,0:T(8,128)} async-done(((f32[1152,2304]{1,0:T(8,128)}), f32[72,2304]{1,0:T(8,128)}) %reduce-scatter.33.cloned.1.call-update) | async-done | bytes 663568 | tf_op jit(solution)/shard_map/reduce_scatter | solution.py:91
  (480 shorter events, 369.5 us)
Async XLA Ops:
  7.2 163.5 %all-gather.18.cloned.1.call-start = ((), (), s32[]{:S(2)}) async-start(), calls=%async_computation.24 | async-start | bytes 4700160 | tf_op jit(solution)/shard_map/all_gather | solution.py:71
  9.3 176.8 %all-gather.20.cloned.1.call-start = ((), (), s32[]{:S(2)}) async-start(), calls=%async_computation.25 | async-start | bytes 1566720 | tf_op jit(solution)/shard_map/all_gather | solution.py:72
  11.0 247.0 %reduce-scatter.21.cloned.1.call-start = ((), (), s32[]{:S(2)}) async-start(), calls=%async_computation.14 | async-start | bytes 884736 | tf_op jit(solution)/shard_map/reduce_scatter | solution.py:54
  189.1 97.2 %all-gather.22.cloned.1.call-start = ((), (), s32[]{:S(2)}) async-start(), calls=%async_computation.26 | async-start | bytes 5640192 | tf_op jit(solution)/shard_map/all_gather | solution.py:73
  191.2 182.4 %all-gather.24.cloned.1.call-start = ((), (), s32[]{:S(2)}) async-start(), calls=%async_computation.27 | async-start | bytes 5640192 | tf_op jit(solution)/shard_map/all_gather | solution.py:74
  193.2 193.2 %reduce-scatter.23.cloned.1.call-start = ((), (), s32[]{:S(2)}) async-start(), calls=%async_computation.15 | async-start | bytes 884736 | tf_op jit(solution)/shard_map/reduce_scatter | solution.py:54
  379.7 91.5 %all-gather.26.cloned.1.call-start = ((), (), s32[]{:S(2)}) async-start(), calls=%async_computation.28 | async-start | bytes 4700160 | tf_op jit(solution)/shard_map/all_gather | solution.py:71
  380.5 149.7 %all-gather.28.cloned.1.call-start = ((), (), s32[]{:S(2)}) async-start(), calls=%async_computation.29 | async-start | bytes 1566720 | tf_op jit(solution)/shard_map/all_gather | solution.py:72
  395.3 82.4 %all-to-all-start = ((bf16[16,2,4608]{2,1,0:T(2,128)(2,1)}), bf16[16,2,4608]{2,1,0:T(2,128)(2,1)}, u32[]{:S(2)}, u32[]{:S(2)}) async-start(bf16[16,2,4608]{2,1,0:T(2,128)(2,1)} %reshape.1070), calls=%async_computation.2 | async-start | bytes 589824 | tf_op jit(solution)/shard_map/all_to_all | solution.py:339
  402.1 148.8 %all-reduce.13.cloned.1.call-start = ((), (), s32[]{:S(2)}) async-start(), calls=%async_computation.32 | async-start | bytes 1179648
  533.2 107.7 %all-gather.30.cloned.1.call-start = ((), (), s32[]{:S(2)}) async-start(), calls=%async_computation.30 | async-start | bytes 5640192 | tf_op jit(solution)/shard_map/all_gather | solution.py:73
  533.7 195.0 %all-gather.32.cloned.1.call-start = ((), (), s32[]{:S(2)}) async-start(), calls=%async_computation.31 | async-start | bytes 5640192 | tf_op jit(solution)/shard_map/all_gather | solution.py:74
  534.5 221.2 %all-reduce.15.cloned.1.call-start = ((), (), s32[]{:S(2)}) async-start(), calls=%async_computation.33 | async-start | bytes 1179648
  738.2 86.5 %all-reduce.19.cloned.1.call-start = ((), (), s32[]{:S(2)}) async-start(), calls=%async_computation.37 | async-start | bytes 2359296
  837.7 33.6 %reduce-scatter.25.cloned.1.call-start = ((), (), s32[]{:S(2)}) async-start(), calls=%async_computation.16 | async-start | bytes 884736 | tf_op jit(solution)/shard_map/reduce_scatter | solution.py:64
  888.9 138.7 %all-reduce.17.cloned.1.call-start = ((), (), s32[]{:S(2)}) async-start(), calls=%async_computation.36 | async-start | bytes 294912 | tf_op jit(solution)/shard_map/psum | solution.py:369
  899.6 266.3 %reduce-scatter.43.cloned.1.call-start = ((), (), s32[]{:S(2)}) async-start(), calls=%async_computation.35 | async-start | bytes 3133440
  902.2 398.4 %reduce-scatter.41.cloned.1.call-start = ((), (), s32[]{:S(2)}) async-start(), calls=%async_computation.34 | async-start | bytes 3133440
  905.5 568.2 %reduce-scatter.31.cloned.1.call-start = ((), (), s32[]{:S(2)}) async-start(), calls=%async_computation.19 | async-start | bytes 9400320 | tf_op jit(solution)/shard_map/reduce_scatter | solution.py:89
  913.3 733.0 %reduce-scatter.29.cloned.1.call-start = ((), (), s32[]{:S(2)}) async-start(), calls=%async_computation.18 | async-start | bytes 9400320 | tf_op jit(solution)/shard_map/reduce_scatter | solution.py:89
  919.4 914.0 %reduce-scatter.39.cloned.1.call-start = ((), (), s32[]{:S(2)}) async-start(), calls=%async_computation.23 | async-start | bytes 11280384 | tf_op jit(solution)/shard_map/reduce_scatter | solution.py:92
  927.9 1092.8 %reduce-scatter.37.cloned.1.call-start = ((), (), s32[]{:S(2)}) async-start(), calls=%async_computation.22 | async-start | bytes 11280384 | tf_op jit(solution)/shard_map/reduce_scatter | solution.py:92
  936.2 1272.7 %reduce-scatter.35.cloned.1.call-start = ((), (), s32[]{:S(2)}) async-start(), calls=%async_computation.21 | async-start | bytes 11280384 | tf_op jit(solution)/shard_map/reduce_scatter | solution.py:91
  943.3 1452.8 %reduce-scatter.33.cloned.1.call-start = ((), (), s32[]{:S(2)}) async-start(), calls=%async_computation.20 | async-start | bytes 11280384 | tf_op jit(solution)/shard_map/reduce_scatter | solution.py:91
  (107 other events, 1627.3 us)
Sparse Core Ops, SparseCore 0:
  11.4 84.7 all-gather.17
  99.5 57.9 all-gather.19
  189.3 7.2 reduce-scatter.20
  199.6 86.6 all-gather.21
  289.4 84.1 all-gather.23
  379.8 6.5 reduce-scatter.22
  389.2 81.9 all-gather.25
  473.9 56.2 all-gather.27
  533.3 17.5 all-reduce.12
  553.9 86.8 all-gather.29
  644.6 84.1 all-gather.31
  738.3 17.3 all-reduce.14
  803.6 21.0 all-reduce.18
  864.7 5.8 reduce-scatter.24
  889.0 8.4 reduce-scatter.26
  904.9 122.7 all-reduce.16
  1033.3 132.5 reduce-scatter.42
  1171.6 128.9 reduce-scatter.40
  1307.3 166.4 reduce-scatter.30
  1480.3 166.0 reduce-scatter.28
  1653.1 180.1 reduce-scatter.38
  1839.2 181.3 reduce-scatter.36
  2027.5 181.3 reduce-scatter.34
  2214.6 181.4 reduce-scatter.32
where the time goes:
time: 2420 us; the launch traced here: 2410 us
  waiting for transfers between devices  1800 us (74%)
  blocking collectives  203 us (8%)
  other arithmetic  127 us (5%)
  matrix products  127 us (5%)
  local copies, waits for them, and re-layouts  114 us (5%)
    reduce_scatter x2, waiting for transfers between devices, reduce_layer(): lax.psum_scatter(gradients[2], 'dp', scatter_dimension=0, tiled=True)  373 us
    reduce_scatter x2, waiting for transfers between devices, reduce_layer(): lax.psum_scatter(gradients[3], 'dp', scatter_dimension=1, tiled=True)  372 us
    reduce_scatter x2, waiting for transfers between devices, reduce_layer(): lax.psum_scatter(gradients[0], 'dp', scatter_dimension=0, tiled=True)  344 us
    unnamed x29, waiting for transfers between devices  306 us
    all_gather x2, waiting for transfers between devices, gather_layer(): lax.all_gather(w_fc2[layer_index], 'dp', axis=1, tiled=True)  164 us
    all_gather x2, waiting for transfers between devices, gather_layer(): lax.all_gather(w_fc1[layer_index], 'dp', axis=0, tiled=True)  105 us
    psum x1, waiting for transfers between devices, per_device(): lax.psum((jnp.stack(dmod_clips), jnp.stack(proj_grads), jnp.stack(hidden_...  75.2 us
    psum x1, blocking collectives, per_device(): modulation = lax.psum(partial_mod, ('dp', 'tensor'))  55 us
  transfers between devices with their start and end apart: 26, of which 21 were waited for; matrix products, arithmetic and copies ran while one was open for 10% of the time, Pallas kernels for 0%

commit v1 on v0

v1 whole, which is shorter than its diff:
```python
import functools

import jax
import jax.numpy as jnp
from jax import lax
from jax.experimental import pallas as pl
from jax.experimental.pallas import tpu as pltpu
from jax.sharding import PartitionSpec as P

HEAD_DIM = 72
FRAMES = 16


epsilon = 1e-06
highest = lax.Precision.HIGHEST
low = jnp.bfloat16
wide = jnp.float32
everyone = ("dp", "tensor")


def normalize(values):
    average = jnp.mean(values, axis=-1, keepdims=True)
    centred = values - average
    inverse = lax.rsqrt(jnp.mean(centred * centred, axis=-1, keepdims=True) + epsilon)
    return (centred * inverse, inverse)


def normalize_back(normed, inverse, upstream):
    first_moment = jnp.mean(upstream, axis=-1, keepdims=True)
    second_moment = jnp.mean(upstream * normed, axis=-1, keepdims=True)
    return inverse * (upstream - first_moment - normed * second_moment)


def product(left_side, right_side):
    return jnp.dot(left_side, right_side, preferred_element_type=wide)


def product_left(left_side, right_side):
    return lax.dot_general(
        left_side, right_side, (((0,), (0,)), ((), ())), preferred_element_type=wide
    )


def product_right(left_side, right_side):
    return lax.dot_general(
        left_side, right_side, (((1,), (1,)), ((), ())), preferred_element_type=wide
    )


def gelu_tanh(values):
    return jax.nn.gelu(values, approximate=True)


def bit_orders(count):
    bits = list(range(count.bit_length() - 1))
    tail, head = bits[:2], bits[2:]
    return (head + tail, head + tail[::-1])


def swap_bit(values, bit, count):
    return lax.ppermute(values, "dp", [(i, i ^ (1 << bit)) for i in range(count)])


def my_bit(bit):
    return (lax.axis_index("dp") >> bit) & 1


def gather_rows(shard, order, count):
    rows, columns = shard.shape
    held = shard[None]
    done = []
    for bit in order:
        got = swap_bit(held, bit, count)
        below = 1 << len([other for other in done if other < bit])
        shape = (-1, below, rows, columns)
        mine, theirs = held.reshape(shape), got.reshape(shape)
        first = my_bit(bit) == 0
        held = jnp.stack(
            [jnp.where(first, mine, theirs), jnp.where(first, theirs, mine)], axis=1
        ).reshape(-1, rows, columns)
        done.append(bit)
    return held.reshape(-1, columns)


def scatter_rows(partial, order, count):
    rows, columns = partial.shape[0] // count, partial.shape[1]
    held = partial.reshape(count, rows, columns)
    left = list(order)
    for bit in order[::-1]:
        left.remove(bit)
        below = 1 << len([other for other in left if other < bit])
        split = held.reshape(-1, 2, below, rows, columns)
        side = my_bit(bit)
        keep = lax.dynamic_index_in_dim(split, side, 1, keepdims=False)
        send = lax.dynamic_index_in_dim(split, 1 - side, 1, keepdims=False)
        got = swap_bit(send.astype(low), bit, count)
        held = keep.astype(wide) + got.astype(wide)
        if left:
            held = held.astype(low)
    return held.reshape(rows, columns)


def swap_tensor(values):
    return lax.ppermute(values, "tensor", [(0, 1), (1, 0)])


def add_halves(partial):
    mine = partial.astype(low)
    return mine.astype(wide) + swap_tensor(mine).astype(wide)


def both_halves(values):
    return lax.all_gather(values, "tensor", axis=1, tiled=True)


def own_half(values):
    return lax.dynamic_slice_in_dim(
        values, lax.axis_index("tensor") * (values.shape[1] // 2), values.shape[1] // 2, 1
    )


def deal(values):
    return lax.all_to_all(values, everyone, split_axis=0, concat_axis=0, tiled=True)


def sum_to_owner(values, owners):
    lead = values.shape[:-1]
    dealt = jnp.moveaxis(values.reshape(lead + (owners, -1)), -2, 0)
    return dealt.reshape(owners, -1)


def from_owners(values, lead):
    owners = values.shape[0]
    return jnp.moveaxis(values.reshape((owners,) + lead + (-1,)), 0, -2).reshape(lead + (-1,))


def same_group(rows, place_count, across):
    first = lax.broadcasted_iota(jnp.int32, (rows, rows), 0)
    second = lax.broadcasted_iota(jnp.int32, (rows, rows), 1)
    if across:
        period = FRAMES * place_count
        alike = lax.rem(first, place_count) == lax.rem(second, place_count)
        if rows > period:
            alike = alike & (lax.div(first, period) == lax.div(second, period))
        return alike
    if rows == place_count:
        return None
    return lax.div(first, place_count) == lax.div(second, place_count)


def head_probs(query, keys, mask):
    scores = product_right(query, keys) * (HEAD_DIM ** (-0.5))
    if mask is not None:
        scores = jnp.where(mask, scores, -1e30)
    exponent = jnp.exp(scores - jnp.max(scores, axis=-1, keepdims=True))
    return exponent / jnp.sum(exponent, axis=-1, keepdims=True)


def attend_kernel(place_count, across, joined_ref, out_ref):
    rows, width = out_ref.shape
    mask = same_group(rows, place_count, across)
    for start in range(0, width, HEAD_DIM):
        query, keys, value = (
            joined_ref[:, part * width + start : part * width + start + HEAD_DIM]
            for part in range(3)
        )
        probs = head_probs(query, keys, mask).astype(low)
        out_ref[:, start : start + HEAD_DIM] = product(probs, value).astype(low)


def attend_back_kernel(place_count, across, joined_ref, upstream_ref, out_ref):
    rows, width = upstream_ref.shape
    mask = same_group(rows, place_count, across)
    score_scale = HEAD_DIM ** (-0.5)
    for start in range(0, width, HEAD_DIM):
        query, keys, value = (
            joined_ref[:, part * width + start : part * width + start + HEAD_DIM]
            for part in range(3)
        )
        upstream = upstream_ref[:, start : start + HEAD_DIM]
        probs = head_probs(query, keys, mask)
        value_grad = product_left(probs.astype(low), upstream)
        prob_grad = product_right(upstream, value)
        centre = jnp.sum(probs * prob_grad, axis=-1, keepdims=True)
        score_grad = (probs * (prob_grad - centre)).astype(low)
        query_grad = product(score_grad, keys) * score_scale
        keys_grad = product_left(score_grad, query) * score_scale
        for part, grad in enumerate((query_grad, keys_grad, value_grad)):
            out_ref[:, part * width + start : part * width + start + HEAD_DIM] = grad.astype(low)


def attend(joined, place_count, across):
    rows, width = joined.shape[0], joined.shape[1] // 3
    heads = width // HEAD_DIM
    return pl.pallas_call(
        functools.partial(attend_kernel, place_count, across),
        out_shape=jax.ShapeDtypeStruct((rows, width), low),
        name="attend",
        cost_estimate=pl.CostEstimate(
            flops=4 * heads * rows * rows * HEAD_DIM,
            bytes_accessed=8 * rows * width,
            transcendentals=heads * rows * rows,
        ),
    )(joined)


def attend_back(joined, upstream, place_count, across):
    rows, width = upstream.shape
    heads = width // HEAD_DIM
    return pl.pallas_call(
        functools.partial(attend_back_kernel, place_count, across),
        out_shape=jax.ShapeDtypeStruct((rows, 3 * width), low),
        name="attend_back",
        cost_estimate=pl.CostEstimate(
            flops=10 * heads * rows * rows * HEAD_DIM,
            bytes_accessed=14 * rows * width,
            transcendentals=heads * rows * rows,
        ),
    )(joined, upstream)


def block_forward(inputs, modulation, weights, biases, across):
    wattn, wfc1, wfc2 = weights
    bias_joined, bias_out, bias_fc2, bias_fc1 = biases
    mod_parts = [modulation[:, index][:, None, :] for index in range(6)]
    shape = inputs.shape
    rows, width = shape[0] * shape[1], shape[2]
    joined_width = bias_joined.shape[0]
    normed_attn, inverse_attn = normalize(inputs)
    hidden_attn = (normed_attn * (1.0 + mod_parts[1]) + mod_parts[0]).astype(low)
    flat_attn = hidden_attn.reshape(rows, width)
    joined = (product(flat_attn, wattn[:, :joined_width]) + bias_joined).astype(low)
    attended = attend(joined, shape[1], across)
    branch_attn = (
        add_halves(product_right(attended, wattn[:, joined_width:])) + bias_out
    ).reshape(shape)
    middle = inputs + mod_parts[2] * branch_attn
    normed_mlp, inverse_mlp = normalize(middle)
    hidden_mlp = (normed_mlp * (1.0 + mod_parts[4]) + mod_parts[3]).astype(low)
    flat_mlp = hidden_mlp.reshape(rows, width)
    inner_pre = product(flat_mlp, wfc1) + bias_fc1
    activated = gelu_tanh(inner_pre).astype(low)
    branch_mlp = (add_halves(product_right(activated, wfc2)) + bias_fc2).reshape(shape)
    result = middle + mod_parts[5] * branch_mlp
    saved = (
        normed_attn,
        inverse_attn,
        flat_attn,
        joined,
        attended,
        branch_attn,
        normed_mlp,
        inverse_mlp,
        flat_mlp,
        inner_pre,
        activated,
        branch_mlp,
    )
    return (result, saved)


def block_backward(upstream, saved, modulation, weights, across, scatter):
    (
        normed_attn,
        inverse_attn,
        flat_attn,
        joined,
        attended,
        branch_attn,
        normed_mlp,
        inverse_mlp,
        flat_mlp,
        inner_pre,
        activated,
        branch_mlp,
    ) = saved
    wattn, wfc1, wfc2 = weights
    mod_parts = [modulation[:, index][:, None, :] for index in range(6)]
    shape = upstream.shape
    rows, width = flat_attn.shape
    joined_width = joined.shape[1]
    part_width = joined_width // 3
    gate_mlp_grad = jnp.sum(upstream * branch_mlp, axis=1)
    mlp_out_grad = (upstream * mod_parts[5]).astype(low)
    fc2_bias_grad = jnp.sum(mlp_out_grad.astype(wide), axis=(0, 1))
    flat_out_grad = mlp_out_grad.reshape(rows, width)
    fc2_reduced = scatter(product_left(flat_out_grad, activated).astype(low), 1)
    activated_grad = product(flat_out_grad, wfc2)
    inner_grad = jax.vjp(gelu_tanh, inner_pre)[1](activated_grad)[0].astype(low)
    fc1_bias_local = jnp.sum(inner_grad.astype(wide), axis=0)
    fc1_reduced = scatter(product_left(flat_mlp, inner_grad).astype(low), 0)
    hidden_mlp_grad = add_halves(product_right(inner_grad, wfc1)).reshape(shape)
    scale_mlp_grad = jnp.sum(hidden_mlp_grad * normed_mlp, axis=1)
    shift_mlp_grad = jnp.sum(hidden_mlp_grad, axis=1)
    middle_grad = upstream + normalize_back(
        normed_mlp, inverse_mlp, hidden_mlp_grad * (1.0 + mod_parts[4])
    )
    gate_attn_grad = jnp.sum(middle_grad * branch_attn, axis=1)
    attn_out_grad = (middle_grad * mod_parts[2]).astype(low)
    out_bias_grad = jnp.sum(attn_out_grad.astype(wide), axis=(0, 1))
    flat_attn_grad = attn_out_grad.reshape(rows, width)
    out_weight_grad = product_left(flat_attn_grad, attended).astype(low)
    attended_grad = product(flat_attn_grad, wattn[:, joined_width:]).astype(low)
    joined_grad = attend_back(joined, attended_grad, shape[1], across)
    joined_weight_grad = product_left(flat_attn, joined_grad).astype(low)
    attn_reduced = scatter(jnp.concatenate([joined_weight_grad, out_weight_grad], axis=1), 0)
    hidden_attn_grad = add_halves(product_right(joined_grad, wattn[:, :joined_width])).reshape(
        shape
    )
    scale_attn_grad = jnp.sum(hidden_attn_grad * normed_attn, axis=1)
    shift_attn_grad = jnp.sum(hidden_attn_grad, axis=1)
    input_grad = middle_grad + normalize_back(
        normed_attn, inverse_attn, hidden_attn_grad * (1.0 + mod_parts[1])
    )
    mod_grad = jnp.stack(
        [
            shift_attn_grad,
            scale_attn_grad,
            gate_attn_grad,
            shift_mlp_grad,
            scale_mlp_grad,
            gate_mlp_grad,
        ],
        axis=1,
    )
    joined_bias = jnp.sum(joined_grad.astype(wide), axis=0)
    proj_grad = jnp.stack(
        [
            widen(joined_bias[:part_width]),
            widen(joined_bias[2 * part_width :]),
            0.5 * out_bias_grad,
            0.5 * fc2_bias_grad,
        ]
    )
    hidden_grad = widen(fc1_bias_local)
    return (input_grad, 0.5 * mod_grad, (attn_reduced, fc1_reduced, fc2_reduced), proj_grad, hidden_grad)


def widen(local_part):
    offset = lax.axis_index("tensor") * local_part.shape[0]
    return lax.dynamic_update_slice_in_dim(
        jnp.zeros((local_part.shape[0] * 2,), wide), local_part, offset, 0
    )


def tensor_part(values):
    part = values.shape[-1] // 2
    return lax.dynamic_slice_in_dim(
        values, lax.axis_index("tensor") * part, part, values.ndim - 1
    )


def per_device(tokens, cond, out_grad, w_qkv, w_out, w_fc1, w_fc2, w_ada, b_ada, b_proj, b_fc1):
    dp_count = lax.axis_size("dp")
    all_devices = lax.axis_size(everyone)
    flat_index = lax.axis_index(everyone)
    width = tokens.shape[3]
    clip_count = cond.shape[0]
    own_rows, head_width = w_qkv.shape[1], w_qkv.shape[3]
    own_width = width // all_devices
    own_start = flat_index * own_width
    orders = bit_orders(dp_count)

    gathered = []
    for layer in range(2):
        shards = (
            jnp.concatenate([w_qkv[layer].reshape(own_rows, 3 * head_width), w_out[layer].T], axis=1),
            w_fc1[layer],
            w_fc2[layer].T,
        )
        gathered.append(
            [
                gather_rows(shard, orders[(index + layer) % 2], dp_count)
                for index, shard in enumerate(shards)
            ]
        )

    cond_float = cond.astype(wide)
    gated_low = jax.nn.silu(cond_float).astype(low)
    gated_own = lax.dynamic_slice_in_dim(gated_low, own_start, own_width, 1)
    partial_mod = jnp.einsum("cd,ldkj->lckj", gated_own, w_ada, preferred_element_type=wide)
    own_mod = jnp.sum(deal(sum_to_owner(partial_mod, all_devices)), axis=0).reshape(
        2, clip_count, 6, own_width
    )
    own_mod = own_mod + b_ada.astype(wide)[:, None]
    pieces = (own_mod, b_proj.astype(wide), b_fc1.astype(wide))
    packed = jnp.concatenate([piece.reshape(-1) for piece in pieces])
    dealt = deal(jnp.broadcast_to(packed[None], (all_devices, packed.shape[0])))
    first_end, second_end = pieces[0].size, pieces[0].size + pieces[1].size
    modulation = from_owners(dealt[:, :first_end], (2, clip_count, 6))
    proj_full = from_owners(dealt[:, first_end:second_end], (2, 4))
    hidden_full = from_owners(dealt[:, second_end:], (2,))

    frames_dev = tokens.shape[0]
    frame_ids = lax.axis_index("dp") * frames_dev + jnp.arange(frames_dev, dtype=jnp.int32)
    onehot = (
        frame_ids[:, None] // FRAMES == jnp.arange(clip_count, dtype=jnp.int32)[None, :]
    ).astype(wide)
    first_mod = jnp.einsum("gc,ckd->gkd", onehot, modulation[0], precision=highest)
    second_mod = jnp.repeat(modulation[1], FRAMES, axis=0)

    def layer_biases(layer):
        bias_query = tensor_part(proj_full[layer, 0])
        bias_value = tensor_part(proj_full[layer, 1])
        return (
            jnp.concatenate([bias_query, jnp.zeros_like(bias_query), bias_value]),
            proj_full[layer, 2],
            proj_full[layer, 3],
            tensor_part(hidden_full[layer]),
        )

    def merge(values):
        return values.reshape(values.shape[0], -1, width)

    first_in = merge(both_halves(tokens)).astype(wide)
    first_biases, second_biases = layer_biases(0), layer_biases(1)
    first_out, first_saved = block_forward(first_in, first_mod, gathered[0], first_biases, False)
    sent = own_half(first_out.astype(low))[:, None]
    arrived = lax.all_to_all(sent, "dp", split_axis=2, concat_axis=0, tiled=True)
    second_in = merge(both_halves(arrived)).astype(wide)
    second_out, second_saved = block_forward(
        second_in, second_mod, gathered[1], second_biases, True
    )
    output = own_half(second_out.astype(low))[:, None]

    def scatter(layer):
        return lambda partial, which: scatter_rows(partial, orders[(which + layer) % 2], dp_count)

    second_upstream = merge(both_halves(out_grad)).astype(wide)
    second_grad, second_dmod, second_reduced, second_proj, second_hidden = block_backward(
        second_upstream, second_saved, second_mod, gathered[1], True, scatter(1)
    )
    sent_back = own_half(second_grad.astype(low))[:, None]
    arrived_back = lax.all_to_all(sent_back, "dp", split_axis=0, concat_axis=2, tiled=True)
    first_upstream = merge(both_halves(arrived_back)).astype(wide)
    first_grad, first_dmod, first_reduced, first_proj, first_hidden = block_backward(
        first_upstream, first_saved, first_mod, gathered[0], False, scatter(0)
    )
    tokens_grad = own_half(first_grad)[:, None]

    dmod_clips = jnp.stack(
        [
            jnp.einsum("gc,gkd->ckd", onehot, first_dmod, precision=highest),
            jnp.sum(second_dmod.reshape(clip_count, FRAMES, 6, width), axis=1),
        ]
    )
    small = (
        dmod_clips,
        jnp.stack([first_proj, second_proj]),
        jnp.stack([first_hidden, second_hidden]),
    )
    owned = jnp.sum(
        deal(jnp.concatenate([sum_to_owner(piece, all_devices) for piece in small], axis=1)), axis=0
    )
    own_dmod = owned[:first_end]
    b_proj_grad = owned[first_end:second_end].reshape(2, 4, own_width)
    b_fc1_grad = owned[second_end:].reshape(2, -1)
    summed_mod = from_owners(
        deal(jnp.broadcast_to(own_dmod[None], (all_devices, own_dmod.shape[0]))), (2, clip_count, 6)
    )
    w_ada_grad = jnp.einsum(
        "cd,lckj->ldkj", gated_own.astype(wide), summed_mod, precision=highest
    )
    b_ada_grad = jnp.sum(own_dmod.reshape(2, clip_count, 6, own_width), axis=1)
    silu_grad = jnp.einsum("lckj,ldkj->cd", summed_mod, w_ada.astype(wide), precision=highest)
    cond_own = lax.dynamic_slice_in_dim(cond_float, own_start, own_width, 1)
    cond_grad = jax.vjp(jax.nn.silu, cond_own)[1](silu_grad)[0]

    reduced = (first_reduced, second_reduced)
    joined_width = 3 * head_width
    w_qkv_grad = jnp.stack(
        [part[0][:, :joined_width].reshape(own_rows, 3, head_width) for part in reduced]
    )
    w_out_grad = jnp.stack([part[0][:, joined_width:].T for part in reduced])
    w_fc1_grad = jnp.stack([part[1] for part in reduced])
    w_fc2_grad = jnp.stack([part[2].T for part in reduced])
    return (
        output,
        tokens_grad,
        cond_grad,
        w_qkv_grad,
        w_out_grad,
        w_fc1_grad,
        w_fc2_grad,
        w_ada_grad,
        b_ada_grad,
        b_proj_grad,
        b_fc1_grad,
    )


def solution(mesh):
    return jax.shard_map(
        per_device,
        mesh=mesh,
        in_specs=(
            P("dp", "tensor", None, None),
            P(),
            P(None, "tensor", "dp", None),
            P(None, "dp", None, "tensor"),
            P(None, "tensor", "dp"),
            P(None, "dp", "tensor"),
            P(None, "tensor", "dp"),
            P(None, ("dp", "tensor"), None, None),
            P(None, None, ("dp", "tensor")),
            P(None, None, ("dp", "tensor")),
            P(None, ("dp", "tensor")),
        ),
        out_specs=(
            P(None, "tensor", "dp", None),
            P("dp", "tensor", None, None),
            P(None, ("dp", "tensor")),
            P(None, "dp", None, "tensor"),
            P(None, "tensor", "dp"),
            P(None, "dp", "tensor"),
            P(None, "tensor", "dp"),
            P(None, ("dp", "tensor"), None, None),
            P(None, None, ("dp", "tensor")),
            P(None, None, ("dp", "tensor")),
            P(None, ("dp", "tensor")),
        ),
        check_vma=False,
    )
```

time: 2420 us -> 1130 us (0.47)
  waiting for transfers between devices: 1800 us -> 600 us
  blocking collectives: 203 us -> 9.5 us
  starting transfers between devices: 15.5 us -> 85.7 us
  local copies, waits for them, and re-layouts: 114 us -> 160 us
  matrix products: 127 us -> 90.2 us
  Pallas kernels: 0 us -> 27.9 us
    reduce_scatter x10 -> x0, waiting for transfers between devices: 1100 us -> none  [the longest x2 373 us: reduce_layer(): lax.psum_scatter(gradients[2], 'dp', scatter_dimension=0, tiled=True)]
    ppermute x0 -> x56, waiting for transfers between devices: none -> 503 us  [the longest x48 503 us: swap_bit(): return lax.ppermute(values, 'dp', [(i, i ^ 1 << bit) for i in range(count)])]
    all_gather x8 -> x0, waiting for transfers between devices: 320 us -> none  [the longest x2 164 us: gather_layer(): lax.all_gather(w_fc2[layer_index], 'dp', axis=1, tiled=True)]
    unnamed x29 -> x0, waiting for transfers between devices: 306 us -> none
    all_gather x11 -> x4, blocking collectives: 148 us -> 9.5 us  [both_halves(): return lax.all_gather(values, 'tensor', axis=1, tiled=True)]
    all_to_all x2 -> x6, waiting for transfers between devices: 7.46 us -> 96.5 us  [the longest x4 53.5 us: deal(): lax.all_to_all(values, everyone, split_axis=0, concat_axis=0, tiled=True)]
    psum x1 -> x0, waiting for transfers between devices: 75.2 us -> none  [per_device(): lax.psum((jnp.stack(dmod_clips), jnp.stack(proj_grads), jnp.stack(hidden_...]
    ppermute x0 -> x56, starting transfers between devices: none -> 62.6 us  [the longest x48 61 us: swap_bit(): return lax.ppermute(values, 'dp', [(i, i ^ 1 << bit) for i in range(count)])]
  transfers between devices with their start and end apart: 26 -> 62, of which waited for: 21 -> 30; matrix products, arithmetic and copies ran while one was open for 10% -> 29% of each run, Pallas kernels for 0% -> 2%
where the time goes in v1:
time: 1130 us; the launch traced here: 1120 us
  waiting for transfers between devices  600 us (53%)
  local copies, waits for them, and re-layouts  160 us (14%)
  other arithmetic  145 us (13%)
  matrix products  90.2 us (8%)
  starting transfers between devices  85.7 us (8%)
  Pallas kernels  27.9 us (2%)
    ppermute x48, waiting for transfers between devices, swap_bit(): return lax.ppermute(values, 'dp', [(i, i ^ 1 << bit) for i in range(count)])  503 us
    ppermute x48, starting transfers between devices, swap_bit(): return lax.ppermute(values, 'dp', [(i, i ^ 1 << bit) for i in range(count)])  61 us
    all_to_all x4, waiting for transfers between devices, deal(): lax.all_to_all(values, everyone, split_axis=0, concat_axis=0, tiled=True)  53.5 us
    all_to_all x1, waiting for transfers between devices, per_device(): lax.all_to_all(sent_back, 'dp', split_axis=0, concat_axis=2, tiled=True)  36.4 us
    dot_general x8, matrix products, product(): return jnp.dot(left_side, right_side, preferred_element_type=wide)  33.5 us
    dot_general x8, matrix products, product_right(): lax.dot_general(left_side, right_side, (((1,), (1,)), ((), ())), preferre...  30.9 us
    another operation x32, other arithmetic, gather_rows(): jnp.stack([jnp.where(first, mine, theirs), jnp.where(first, theirs, mine)...  29.7 us
    unnamed x381, local copies, waits for them, and re-layouts  28.7 us
  transfers between devices with their start and end apart: 62, of which 30 were waited for; matrix products, arithmetic and copies ran while one was open for 29% of the time, Pallas kernels for 2%

profile of v1, /device:TPU:0, one launch (start us, length us, event | category | flops | bytes accessed | tf_op | source)
XLA Modules:
  0.0 1121.7 jit_solution(9780370004682755551)
XLA Ops:
  14.6 11.3 %reshape.1813 = bf16[2,6,32,36,36]{3,2,0,1,4:T(8,128)(2,1)S(1)} reshape(bf16[2,6,1152,36]{2,0,1,3:T(2,128)(2,1)} %bitcast.674) | data formatting | bytes 1990656 | tf_op jit(solution)/shard_map/reshape.687
  84.1 63.5 %collective-permute-done.24 = bf16[2,72,2304]{2,1,0:T(8,128)(2,1)} collective-permute-done((bf16[2,72,2304]{2,1,0:T(8,128)(2,1)}, bf16[2,72,2304]{2,1,0:T(8,128)(2,1)}, u32[]{:S(2)}, u32[]{:S(2)}) %collective-permute-start.24) | collective-permute-done | bytes 663584 | tf_op jit(solution)/shard_map/ppermute | solution.py:61
  147.5 28.4 %collective-permute-done.10 = bf16[2,72,2304]{2,1,0:T(8,128)(2,1)} collective-permute-done((bf16[2,72,2304]{2,1,0:T(8,128)(2,1)}, bf16[2,72,2304]{2,1,0:T(8,128)(2,1)}, u32[]{:S(2)}, u32[]{:S(2)}) %collective-permute-start.10) | collective-permute-done | bytes 663584 | tf_op jit(solution)/shard_map/ppermute | solution.py:61
  179.2 11.0 collective-permute-done.6
  190.2 14.2 %collective-permute-done.15 = bf16[2,72,2304]{2,1,0:T(8,128)(2,1)} collective-permute-done((bf16[2,72,2304]{2,1,0:T(8,128)(2,1)}, bf16[2,72,2304]{2,1,0:T(8,128)(2,1)}, u32[]{:S(2)}, u32[]{:S(2)}) %collective-permute-start.15) | collective-permute-done | bytes 663584 | tf_op jit(solution)/shard_map/ppermute | solution.py:61
  207.6 10.9 collective-permute-done.1
  222.1 9.6 collective-permute-done.20
  233.4 14.8 %collective-permute-done.2 = bf16[4,72,2304]{2,1,0:T(8,128)(2,1)S(1)} collective-permute-done((bf16[4,72,2304]{2,1,0:T(8,128)(2,1)S(1)}, bf16[4,72,2304]{2,1,0:T(8,128)(2,1)S(1)}, u32[]{:S(2)}, u32[]{:S(2)}) %collective-permute-start.2) | collective-permute-done | bytes 1327136 | tf_op jit(solution)/shard_map/ppermute | solution.py:61
  250.1 16.5 %collective-permute-done.16 = bf16[4,72,2304]{2,1,0:T(8,128)(2,1)S(1)} collective-permute-done((bf16[4,72,2304]{2,1,0:T(8,128)(2,1)S(1)}, bf16[4,72,2304]{2,1,0:T(8,128)(2,1)S(1)}, u32[]{:S(2)}, u32[]{:S(2)}) %collective-permute-start.16) | collective-permute-done | bytes 1327136 | tf_op jit(solution)/shard_map/ppermute | solution.py:61
  268.6 26.5 %collective-permute-done.25 = bf16[4,72,2304]{2,1,0:T(8,128)(2,1)S(1)} collective-permute-done((bf16[4,72,2304]{2,1,0:T(8,128)(2,1)S(1)}, bf16[4,72,2304]{2,1,0:T(8,128)(2,1)S(1)}, u32[]{:S(2)}, u32[]{:S(2)}) %collective-permute-start.25) | collective-permute-done | bytes 1327136 | tf_op jit(solution)/shard_map/ppermute | solution.py:61
  311.6 40.3 %collective-permute-done.3 = bf16[8,72,2304]{2,1,0:T(8,128)(2,1)S(1)} collective-permute-done((bf16[8,72,2304]{2,1,0:T(8,128)(2,1)S(1)}, bf16[8,72,2304]{2,1,0:T(8,128)(2,1)S(1)}, u32[]{:S(2)}, u32[]{:S(2)}) %collective-permute-start.3) | collective-permute-done | bytes 2654240 | tf_op jit(solution)/shard_map/ppermute | solution.py:61
  365.3 43.6 %collective-permute-done.12 = bf16[8,72,2304]{2,1,0:T(8,128)(2,1)} collective-permute-done((bf16[8,72,2304]{2,1,0:T(8,128)(2,1)}, bf16[8,72,2304]{2,1,0:T(8,128)(2,1)}, u32[]{:S(2)}, u32[]{:S(2)}) %collective-permute-start.12) | collective-permute-done | bytes 2654240 | tf_op jit(solution)/shard_map/ppermute | solution.py:61
  424.6 46.7 %collective-permute-done.8 = bf16[8,72,2304]{2,1,0:T(8,128)(2,1)} collective-permute-done((bf16[8,72,2304]{2,1,0:T(8,128)(2,1)}, bf16[8,72,2304]{2,1,0:T(8,128)(2,1)}, u32[]{:S(2)}, u32[]{:S(2)}) %collective-permute-start.8) | collective-permute-done | bytes 2654240 | tf_op jit(solution)/shard_map/ppermute | solution.py:61
  682.0 36.4 %all-to-all-done.3 = bf16[16,1,8,1152]{3,2,1,0:T(8,128)(2,1)S(1)} async-done(((bf16[16,1,8,1152]{3,2,1,0:T(8,128)(2,1)}), bf16[16,1,8,1152]{3,2,1,0:T(8,128)(2,1)S(1)}, u32[]{:S(2)}, u32[]{:S(2)}) %all-to-all-start.3) | async-done | bytes 294944 | tf_op jit(solution)/shard_map/all_to_all | solution.py:434
  814.7 51.0 %all-to-all-done.4 = f32[32,1,1008]{2,1,0:T(1,128)} async-done(((f32[32,1,1008]{2,1,0:T(1,128)}), f32[32,1,1008]{2,1,0:T(1,128)}, u32[]{:S(2)}, u32[]{:S(2)}) %all-to-all-start.4) | async-done | bytes 129056 | tf_op jit(solution)/shard_map/all_to_all | solution.py:123
  890.1 14.9 %collective-permute-done.45 = bf16[4,1,72,2304]{3,2,0,1:T(8,128)(2,1)S(1)} collective-permute-done((bf16[4,1,72,2304]{3,2,0,1:T(8,128)(2,1)}, bf16[4,1,72,2304]{3,2,0,1:T(8,128)(2,1)S(1)}, u32[]{:S(2)}, u32[]{:S(2)}) %collective-permute-start.45) | collective-permute-done | bytes 1327136 | tf_op jit(solution)/shard_map/ppermute | solution.py:61
  913.6 19.4 %collective-permute-done.37 = bf16[4,1,72,2304]{3,2,0,1:T(8,128)(2,1)} collective-permute-done((bf16[4,1,72,2304]{3,2,0,1:T(8,128)(2,1)}, bf16[4,1,72,2304]{3,2,0,1:T(8,128)(2,1)}, u32[]{:S(2)}, u32[]{:S(2)}) %collective-permute-start.37) | collective-permute-done | bytes 1327136 | tf_op jit(solution)/shard_map/ppermute | solution.py:61
  940.8 18.7 %collective-permute-done.47 = bf16[1,1,72,2304]{3,2,1,0:T(8,128)(2,1)S(1)} collective-permute-done((bf16[1,1,72,2304]{3,2,1,0:T(8,128)(2,1)S(1)}, bf16[1,1,72,2304]{3,2,1,0:T(8,128)(2,1)S(1)}, u32[]{:S(2)}, u32[]{:S(2)}) %collective-permute-start.47) | collective-permute-done | bytes 331808 | tf_op jit(solution)/shard_map/ppermute | solution.py:61
  974.0 8.8 collective-permute-done.38
  983.1 13.1 %collective-permute-done.54 = bf16[1,2,72,2304]{3,2,1,0:T(8,128)(2,1)S(1)} collective-permute-done((bf16[1,2,72,2304]{3,2,1,0:T(8,128)(2,1)S(1)}, bf16[1,2,72,2304]{3,2,1,0:T(8,128)(2,1)S(1)}, u32[]{:S(2)}, u32[]{:S(2)}) %collective-permute-start.54) | collective-permute-done | bytes 663584 | tf_op jit(solution)/shard_map/ppermute | solution.py:61
  1022.5 40.3 %collective-permute-done.42 = bf16[1,2,72,2304]{3,2,1,0:T(8,128)(2,1)S(1)} collective-permute-done((bf16[1,2,72,2304]{3,2,1,0:T(8,128)(2,1)S(1)}, bf16[1,2,72,2304]{3,2,1,0:T(8,128)(2,1)S(1)}, u32[]{:S(2)}, u32[]{:S(2)}) %collective-permute-start.42) | collective-permute-done | bytes 663584 | tf_op jit(solution)/shard_map/ppermute | solution.py:61
  1065.3 14.4 %collective-permute-done.43 = bf16[1,1,72,2304]{3,2,1,0:T(8,128)(2,1)S(1)} collective-permute-done((bf16[1,1,72,2304]{3,2,1,0:T(8,128)(2,1)S(1)}, bf16[1,1,72,2304]{3,2,1,0:T(8,128)(2,1)S(1)}, u32[]{:S(2)}, u32[]{:S(2)}) %collective-permute-start.43) | collective-permute-done | bytes 331808 | tf_op jit(solution)/shard_map/ppermute | solution.py:61
  1081.0 10.2 collective-permute-done.34
  1091.5 13.4 %collective-permute-done.50 = bf16[1,2,72,2304]{3,2,1,0:T(8,128)(2,1)S(1)} collective-permute-done((bf16[1,2,72,2304]{3,2,1,0:T(8,128)(2,1)S(1)}, bf16[1,2,72,2304]{3,2,1,0:T(8,128)(2,1)S(1)}, u32[]{:S(2)}, u32[]{:S(2)}) %collective-permute-start.50) | collective-permute-done | bytes 663584 | tf_op jit(solution)/shard_map/ppermute | solution.py:61
  (837 shorter events, 540.1 us)
Async XLA Ops:
  57.4 90.1 %collective-permute-start.24 = (bf16[2,72,2304]{2,1,0:T(8,128)(2,1)}, bf16[2,72,2304]{2,1,0:T(8,128)(2,1)}, u32[]{:S(2)}, u32[]{:S(2)}) collective-permute-start(bf16[2,72,2304]{2,1,0:T(8,128)(2,1)} %maximum_bitcast_fusion.5), channel_id=1, source_target_pairs={{0,16},{2,18},{4,20},{6,22},{8,24},{10,26},{12,28},{14,30},{16,0},... | collective-permute-start | bytes 1990664 | tf_op jit(solution)/shard_map/ppermute | solution.py:61
  60.8 115.2 %collective-permute-start.10 = (bf16[2,72,2304]{2,1,0:T(8,128)(2,1)}, bf16[2,72,2304]{2,1,0:T(8,128)(2,1)}, u32[]{:S(2)}, u32[]{:S(2)}) collective-permute-start(bf16[2,72,2304]{2,1,0:T(8,128)(2,1)} %maximum_bitcast_fusion.2), channel_id=1, source_target_pairs={{0,16},{2,18},{4,20},{6,22},{8,24},{10,26},{12,28},{14,30},{16,0},... | collective-permute-start | bytes 1990664 | tf_op jit(solution)/shard_map/ppermute | solution.py:61
  62.2 128.0 %collective-permute-start.6 = (bf16[2,72,2304]{2,1,0:T(8,128)(2,1)}, bf16[2,72,2304]{2,1,0:T(8,128)(2,1)}, u32[]{:S(2)}, u32[]{:S(2)}) collective-permute-start(bf16[2,72,2304]{2,1,0:T(8,128)(2,1)} %maximum_bitcast_fusion.1), channel_id=1, source_target_pairs={{0,16},{2,18},{4,20},{6,22},{8,24},{10,26},{12,28},{14,30},{16,0},... | collective-permute-start | bytes 1990664 | tf_op jit(solution)/shard_map/ppermute | solution.py:61
  66.7 137.7 %collective-permute-start.15 = (bf16[2,72,2304]{2,1,0:T(8,128)(2,1)}, bf16[2,72,2304]{2,1,0:T(8,128)(2,1)}, u32[]{:S(2)}, u32[]{:S(2)}) collective-permute-start(bf16[2,72,2304]{2,1,0:T(8,128)(2,1)} %maximum_bitcast_fusion.3), channel_id=1, source_target_pairs={{0,16},{2,18},{4,20},{6,22},{8,24},{10,26},{12,28},{14,30},{16,0},... | collective-permute-start | bytes 1990664 | tf_op jit(solution)/shard_map/ppermute | solution.py:61
  80.4 138.1 %collective-permute-start.1 = (bf16[2,72,2304]{2,1,0:T(8,128)(2,1)}, bf16[2,72,2304]{2,1,0:T(8,128)(2,1)S(1)}, u32[]{:S(2)}, u32[]{:S(2)}) collective-permute-start(bf16[2,72,2304]{2,1,0:T(8,128)(2,1)} %maximum_bitcast_fusion), channel_id=1, source_target_pairs={{0,16},{2,18},{4,20},{6,22},{8,24},{10,26},{12,28},{14,30},{16,0},... | collective-permute-start | bytes 1990664 | tf_op jit(solution)/shard_map/ppermute | solution.py:61
  147.5 84.1 %collective-permute-start.20 = (bf16[2,72,2304]{2,1,0:T(8,128)(2,1)S(1)}, bf16[2,72,2304]{2,1,0:T(8,128)(2,1)S(1)}, u32[]{:S(2)}, u32[]{:S(2)}) collective-permute-start(bf16[2,72,2304]{2,1,0:T(8,128)(2,1)S(1)} %maximum_bitcast_fusion.4), channel_id=1, source_target_pairs={{0,16},{2,18},{4,20},{6,22},{8,24},{10,26},{12,28},{14,30},{16,0},... | collective-permute-start | bytes 1990664 | tf_op jit(solution)/shard_map/ppermute | solution.py:61
  177.6 117.9 %collective-permute-start.11 = (bf16[4,72,2304]{2,1,0:T(8,128)(2,1)S(1)}, bf16[4,72,2304]{2,1,0:T(8,128)(2,1)S(1)}, u32[]{:S(2)}, u32[]{:S(2)}) collective-permute-start(bf16[4,72,2304]{2,1,0:T(8,128)(2,1)S(1)} %bitcast.646), channel_id=1, source_target_pairs={{0,2},{2,0},{4,6},{6,4},{8,10},{10,8},{12,14},{14,12},{16,18},{18,... | collective-permute-start | bytes 3981320 | tf_op jit(solution)/shard_map/ppermute | solution.py:61
  206.1 99.4 %collective-permute-start.7 = (bf16[4,72,2304]{2,1,0:T(8,128)(2,1)S(1)}, bf16[4,72,2304]{2,1,0:T(8,128)(2,1)S(1)}, u32[]{:S(2)}, u32[]{:S(2)}) collective-permute-start(bf16[4,72,2304]{2,1,0:T(8,128)(2,1)S(1)} %bitcast.645), channel_id=1, source_target_pairs={{0,4},{2,6},{4,0},{6,2},{8,12},{10,14},{12,8},{14,10},{16,20},{18,... | collective-permute-start | bytes 3981320 | tf_op jit(solution)/shard_map/ppermute | solution.py:61
  266.6 85.3 %collective-permute-start.3 = (bf16[8,72,2304]{2,1,0:T(8,128)(2,1)S(1)}, bf16[8,72,2304]{2,1,0:T(8,128)(2,1)S(1)}, u32[]{:S(2)}, u32[]{:S(2)}) collective-permute-start(bf16[8,72,2304]{2,1,0:T(8,128)(2,1)S(1)} %bitcast.664), channel_id=1, source_target_pairs={{0,4},{2,6},{4,0},{6,2},{8,12},{10,14},{12,8},{14,10},{16,20},{18,... | collective-permute-start | bytes 7962632 | tf_op jit(solution)/shard_map/ppermute | solution.py:61
  302.5 106.4 %collective-permute-start.12 = (bf16[8,72,2304]{2,1,0:T(8,128)(2,1)}, bf16[8,72,2304]{2,1,0:T(8,128)(2,1)}, u32[]{:S(2)}, u32[]{:S(2)}) collective-permute-start(bf16[8,72,2304]{2,1,0:T(8,128)(2,1)} %bitcast.65), channel_id=1, source_target_pairs={{0,4},{2,6},{4,0},{6,2},{8,12},{10,14},{12,8},{14,10},{16,20},{18,... | collective-permute-start | bytes 7962632 | tf_op jit(solution)/shard_map/ppermute | solution.py:61
  304.0 111.2 %collective-permute-start.26 = (bf16[8,72,2304]{2,1,0:T(8,128)(2,1)}, bf16[8,72,2304]{2,1,0:T(8,128)(2,1)}, u32[]{:S(2)}, u32[]{:S(2)}) collective-permute-start(bf16[8,72,2304]{2,1,0:T(8,128)(2,1)} %bitcast.119), channel_id=1, source_target_pairs={{0,2},{2,0},{4,6},{6,4},{8,10},{10,8},{12,14},{14,12},{16,18},{18,... | collective-permute-start | bytes 7962632 | tf_op jit(solution)/shard_map/ppermute | solution.py:61
  305.4 116.2 %collective-permute-start.17 = (bf16[8,72,2304]{2,1,0:T(8,128)(2,1)}, bf16[8,72,2304]{2,1,0:T(8,128)(2,1)}, u32[]{:S(2)}, u32[]{:S(2)}) collective-permute-start(bf16[8,72,2304]{2,1,0:T(8,128)(2,1)} %bitcast.85), channel_id=1, source_target_pairs={{0,2},{2,0},{4,6},{6,4},{8,10},{10,8},{12,14},{14,12},{16,18},{18,... | collective-permute-start | bytes 7962632 | tf_op jit(solution)/shard_map/ppermute | solution.py:61
  308.0 163.3 %collective-permute-start.8 = (bf16[8,72,2304]{2,1,0:T(8,128)(2,1)}, bf16[8,72,2304]{2,1,0:T(8,128)(2,1)}, u32[]{:S(2)}, u32[]{:S(2)}) collective-permute-start(bf16[8,72,2304]{2,1,0:T(8,128)(2,1)} %bitcast.46), channel_id=1, source_target_pairs={{0,2},{2,0},{4,6},{6,4},{8,10},{10,8},{12,14},{14,12},{16,18},{18,... | collective-permute-start | bytes 7962632 | tf_op jit(solution)/shard_map/ppermute | solution.py:61
  352.0 161.4 %collective-permute-start.22 = (bf16[8,72,2304]{2,1,0:T(8,128)(2,1)}, bf16[8,72,2304]{2,1,0:T(8,128)(2,1)}, u32[]{:S(2)}, u32[]{:S(2)}) collective-permute-start(bf16[8,72,2304]{2,1,0:T(8,128)(2,1)} %bitcast.102), channel_id=1, source_target_pairs={{0,4},{2,6},{4,0},{6,2},{8,12},{10,14},{12,8},{14,10},{16,20},{18,... | collective-permute-start | bytes 7962632 | tf_op jit(solution)/shard_map/ppermute | solution.py:61
  414.7 70.6 %collective-permute-start.4 = (bf16[256,1152]{1,0:T(8,128)(2,1)}, bf16[256,1152]{1,0:T(8,128)(2,1)}, u32[]{:S(2)}, u32[]{:S(2)}) collective-permute-start(bf16[256,1152]{1,0:T(8,128)(2,1)} %convolution_convert_fusion.9), channel_id=1, source_target_pairs={{0,1},{1,0},{2,3},{3,2},{4,5},{5,4},{6,7},{7,6},{8,9},{9,8},{10,11... | collective-permute-start | bytes 1769480 | tf_op jit(solution)/shard_map/ppermute | solution.py:104
  585.1 83.1 %collective-permute-start.27 = (bf16[256,1152]{1,0:T(8,128)(2,1)}, bf16[256,1152]{1,0:T(8,128)(2,1)}, u32[]{:S(2)}, u32[]{:S(2)}) collective-permute-start(bf16[256,1152]{1,0:T(8,128)(2,1)} %convolution_convert_fusion.12), channel_id=1, source_target_pairs={{0,1},{1,0},{2,3},{3,2},{4,5},{5,4},{6,7},{7,6},{8,9},{9,8},{10,11... | collective-permute-start | bytes 1769480 | tf_op jit(solution)/shard_map/ppermute | solution.py:104
  587.0 211.8 %collective-permute-start.44 = (bf16[8,1,72,2304]{3,2,0,1:T(8,128)(2,1)}, bf16[8,1,72,2304]{3,2,0,1:T(8,128)(2,1)}, u32[]{:S(2)}, u32[]{:S(2)}) collective-permute-start(bf16[8,1,72,2304]{3,2,0,1:T(8,128)(2,1)} %dynamic-slice_bitcast_fusion.2), channel_id=1, source_target_pairs={{0,2},{2,0},{4,6},{6,4},{8,10},{10,8},{12,14},{14,12},{16,18},{18,... | collective-permute-start | bytes 7962632 | tf_op jit(solution)/shard_map/ppermute | solution.py:61
  649.4 222.8 %collective-permute-start.36 = (bf16[8,1,72,2304]{3,2,0,1:T(8,128)(2,1)}, bf16[8,1,72,2304]{3,2,0,1:T(8,128)(2,1)}, u32[]{:S(2)}, u32[]{:S(2)}) collective-permute-start(bf16[8,1,72,2304]{3,2,0,1:T(8,128)(2,1)} %dynamic-slice_bitcast_fusion.4), channel_id=1, source_target_pairs={{0,2},{2,0},{4,6},{6,4},{8,10},{10,8},{12,14},{14,12},{16,18},{18,... | collective-permute-start | bytes 7962632 | tf_op jit(solution)/shard_map/ppermute | solution.py:61
  655.7 223.5 %collective-permute-start.52 = (bf16[4,2,72,2304]{3,2,1,0:T(8,128)(2,1)}, bf16[4,2,72,2304]{3,2,1,0:T(8,128)(2,1)}, u32[]{:S(2)}, u32[]{:S(2)}) collective-permute-start(bf16[4,2,72,2304]{3,2,1,0:T(8,128)(2,1)} %dynamic-slice_bitcast_fusion), channel_id=1, source_target_pairs={{0,4},{2,6},{4,0},{6,2},{8,12},{10,14},{12,8},{14,10},{16,20},{18,... | collective-permute-start | bytes 7962632 | tf_op jit(solution)/shard_map/ppermute | solution.py:61
  742.5 164.6 %collective-permute-start.40 = (bf16[4,2,72,2304]{3,2,1,0:T(8,128)(2,1)}, bf16[4,2,72,2304]{3,2,1,0:T(8,128)(2,1)}, u32[]{:S(2)}, u32[]{:S(2)}) collective-permute-start(bf16[4,2,72,2304]{3,2,1,0:T(8,128)(2,1)} %dynamic-slice_bitcast_fusion.3), channel_id=1, source_target_pairs={{0,4},{2,6},{4,0},{6,2},{8,12},{10,14},{12,8},{14,10},{16,20},{18,... | collective-permute-start | bytes 7962632 | tf_op jit(solution)/shard_map/ppermute | solution.py:61
  798.8 164.1 %collective-permute-start.32 = (bf16[4,2,72,2304]{3,2,1,0:T(8,128)(2,1)}, bf16[4,2,72,2304]{3,2,1,0:T(8,128)(2,1)}, u32[]{:S(2)}, u32[]{:S(2)}) collective-permute-start(bf16[4,2,72,2304]{3,2,1,0:T(8,128)(2,1)} %dynamic-slice_bitcast_fusion.5), channel_id=1, source_target_pairs={{0,4},{2,6},{4,0},{6,2},{8,12},{10,14},{12,8},{14,10},{16,20},{18,... | collective-permute-start | bytes 7962632 | tf_op jit(solution)/shard_map/ppermute | solution.py:61
  804.4 164.2 %collective-permute-start.48 = (bf16[8,1,72,2304]{3,2,0,1:T(8,128)(2,1)}, bf16[8,1,72,2304]{3,2,0,1:T(8,128)(2,1)}, u32[]{:S(2)}, u32[]{:S(2)}) collective-permute-start(bf16[8,1,72,2304]{3,2,0,1:T(8,128)(2,1)} %dynamic-slice_bitcast_fusion.1), channel_id=1, source_target_pairs={{0,2},{2,0},{4,6},{6,4},{8,10},{10,8},{12,14},{14,12},{16,18},{18,... | collective-permute-start | bytes 7962632 | tf_op jit(solution)/shard_map/ppermute | solution.py:61
  933.0 81.0 %collective-permute-start.41 = (bf16[4,1,72,2304]{3,2,1,0:T(8,128)(2,1)}, bf16[4,1,72,2304]{3,2,1,0:T(8,128)(2,1)}, u32[]{:S(2)}, u32[]{:S(2)}) collective-permute-start(bf16[4,1,72,2304]{3,2,1,0:T(8,128)(2,1)} %constant_dynamic-slice_fusion.7), channel_id=1, source_target_pairs={{0,2},{2,0},{4,6},{6,4},{8,10},{10,8},{12,14},{14,12},{16,18},{18,... | collective-permute-start | bytes 3981320 | tf_op jit(solution)/shard_map/ppermute | solution.py:61
  1019.1 72.1 %collective-permute-start.34 = (bf16[1,2,72,2304]{3,2,1,0:T(8,128)(2,1)S(1)}, bf16[1,2,72,2304]{3,2,1,0:T(8,128)(2,1)S(1)}, u32[]{:S(2)}, u32[]{:S(2)}) collective-permute-start(bf16[1,2,72,2304]{3,2,1,0:T(8,128)(2,1)S(1)} %dynamic-slice_bitcast_fusion.14), channel_id=1, source_target_pairs={{0,16},{2,18},{4,20},{6,22},{8,24},{10,26},{12,28},{14,30},{16,0},... | collective-permute-start | bytes 1990664 | tf_op jit(solution)/shard_map/ppermute | solution.py:61
  (220 other events, 4914.4 us)

commit v2 on v1

v2 whole, which is shorter than its diff:
```python
import functools

import jax
import jax.numpy as jnp
from jax import lax
from jax.experimental import pallas as pl
from jax.experimental.pallas import tpu as pltpu
from jax.sharding import PartitionSpec as P

HEAD_DIM = 72
FRAMES = 16


epsilon = 1e-06
highest = lax.Precision.HIGHEST
low = jnp.bfloat16
wide = jnp.float32
everyone = ("dp", "tensor")


def layer_norm(values):
    centred = values - jnp.mean(values, axis=-1, keepdims=True)
    inverse = lax.rsqrt(jnp.mean(centred * centred, axis=-1, keepdims=True) + epsilon)
    return (centred * inverse, inverse)


def layer_norm_back(normed, inverse, upstream):
    first_moment = jnp.mean(upstream, axis=-1, keepdims=True)
    second_moment = jnp.mean(upstream * normed, axis=-1, keepdims=True)
    return inverse * (upstream - first_moment - normed * second_moment)


def product(left_side, right_side):
    return jnp.dot(left_side, right_side, preferred_element_type=wide)


def product_left(left_side, right_side):
    return lax.dot_general(
        left_side, right_side, (((0,), (0,)), ((), ())), preferred_element_type=wide
    )


def product_right(left_side, right_side):
    return lax.dot_general(
        left_side, right_side, (((1,), (1,)), ((), ())), preferred_element_type=wide
    )


PLANE = 2
PAIR = 2


def swap_bit(values, bit, count):
    return lax.ppermute(values, "dp", [(i, i ^ (1 << bit)) for i in range(count)])


def my_bit(bit):
    return (lax.axis_index("dp") >> bit) & 1


def after(value, *others):
    return lax.optimization_barrier((value,) + others)[0]


def outer_bits(count):
    return range(PLANE, count.bit_length() - 1)


def pick(first, mine, theirs, axis):
    return jnp.stack(
        [jnp.where(first, mine, theirs), jnp.where(first, theirs, mine)], axis=axis
    )


def gather_outer(shard, count):
    paired = isinstance(shard, tuple)
    rows, columns = shard[0].shape if paired else shard.shape
    held = shard[0][None] if paired else shard[None]
    for bit in outer_bits(count):
        sent = shard[1][None] if bit == PAIR and paired else held
        got = swap_bit(sent, bit, count)
        held = pick(my_bit(bit) == 0, held, got, 0).reshape(-1, rows, columns)
    return held


def arrange_kernel(me_ref, own_ref, across_ref, along_ref, low_ref, high_ref, out_ref):
    me = me_ref[0]
    out_ref[me] = own_ref[0]
    out_ref[me ^ 1] = across_ref[0]
    out_ref[me ^ 2] = along_ref[0]
    in_low = pl.program_id(0) < pl.num_programs(0) // 2

    @pl.when(in_low)
    def _():
        out_ref[me ^ 3] = low_ref[0]

    @pl.when(jnp.logical_not(in_low))
    def _():
        out_ref[me ^ 3] = high_ref[0]


def arrange(own, across, along, low_part, high_part):
    groups, rows, columns = own.shape
    half = groups // 2
    block = (1, rows, columns)
    whole = pl.BlockSpec(block, lambda i, me: (i, 0, 0))
    me = jnp.reshape(lax.axis_index("dp") & 3, (1,)).astype(jnp.int32)
    out = pl.pallas_call(
        arrange_kernel,
        out_shape=jax.ShapeDtypeStruct((groups * 4, rows, columns), own.dtype),
        grid_spec=pltpu.PrefetchScalarGridSpec(
            num_scalar_prefetch=1,
            grid=(groups,),
            in_specs=[
                whole,
                whole,
                whole,
                pl.BlockSpec(block, lambda i, me: (jnp.minimum(i, half - 1), 0, 0)),
                pl.BlockSpec(block, lambda i, me: (jnp.maximum(i - half, 0), 0, 0)),
            ],
            out_specs=pl.BlockSpec((4, rows, columns), lambda i, me: (i, 0, 0)),
        ),
        name="arrange",
        cost_estimate=pl.CostEstimate(
            flops=0, bytes_accessed=16 * groups * rows * columns, transcendentals=0
        ),
    )(me, own, across, along, low_part, high_part)
    return out.reshape(groups * 4 * rows, columns)


def gather_all(shards, count):
    full = []
    last_outer = last_plane = None
    for shard in shards:
        if last_outer is not None:
            shard = lax.optimization_barrier((shard, last_outer))[0]
        own = gather_outer(shard, count)
        last_outer = own
        if last_plane is not None:
            own = after(own, *last_plane)
        across, along = swap_bit(own, 0, count), swap_bit(own, 1, count)
        last_plane = (across, along)
        half = own.shape[0] // 2
        low_part = swap_bit(across[:half], 1, count)
        high_part = swap_bit(along[half:], 0, count)
        full.append(arrange(own, across, along, low_part, high_part))
    return full


def place_scalars():
    return jnp.stack([lax.axis_index("tensor"), lax.axis_index("dp") & 3]).astype(jnp.int32)


def weight_grad_kernel(count, starts, place_ref, *refs):
    pairs = len(starts)
    operands, outs, total = refs[: 2 * pairs], refs[2 * pairs : -1], refs[-1]
    me = place_ref[1]
    rows = total.shape[0] // count
    for index, start in enumerate(starts):
        left, right = operands[2 * index], operands[2 * index + 1]
        total[:, start : start + right.shape[1]] = product_left(left[...], right[...])
        spare = -right.shape[1] % 128
        if spare:
            end = start + right.shape[1]
            total[:, end : end + spare] = jnp.zeros((total.shape[0], spare), wide)
    for relative, out in enumerate(outs):
        mate = me ^ relative
        if rows % 8 == 0:

            @pl.loop(0, count // 4)
            def _(group, mate=mate, out=out):
                first = pl.multiple_of((group * 4 + mate) * rows, 8)
                out[group] = total[pl.ds(first, rows), :].astype(low)
        else:
            for place in range(4):

                @pl.when(mate == place)
                def _(place=place, out=out):
                    for group in range(count // 4):
                        first = (group * 4 + place) * rows
                        out[group] = total[first : first + rows, :].astype(low)


def scatter_product(pairs, paired):
    count = lax.axis_size("dp")
    groups = count // 4
    half = groups // 2
    width = pairs[0][0].shape[1]
    rows = width // count
    starts, columns = [], 0
    for _, right in pairs:
        starts.append(columns)
        columns += padded(right.shape[1])
    tokens = pairs[0][0].shape[0]
    own, across, along, far = pl.pallas_call(
        functools.partial(weight_grad_kernel, count, tuple(starts)),
        out_shape=[jax.ShapeDtypeStruct((groups, rows, columns), low)] * 4,
        in_specs=[pl.BlockSpec(memory_space=pltpu.SMEM)]
        + [pl.BlockSpec(memory_space=pltpu.VMEM)] * (2 * len(pairs)),
        scratch_shapes=[pltpu.VMEM((width, columns), wide)],
        name="weight_grad",
        cost_estimate=pl.CostEstimate(
            flops=2 * tokens * width * columns,
            bytes_accessed=2 * width * columns + 4 * tokens * (width + columns),
            transcendentals=0,
        ),
    )(place_scalars(), *[operand for pair in pairs for operand in pair])
    low_part = swap_bit(far[:half], 1, count)
    high_part = swap_bit(far[half:], 0, count)
    across = jnp.concatenate(
        [(across[:half].astype(wide) + low_part.astype(wide)).astype(low), across[half:]]
    )
    along = jnp.concatenate(
        [along[:half], (along[half:].astype(wide) + high_part.astype(wide)).astype(low)]
    )
    got_across, got_along = swap_bit(across, 0, count), swap_bit(along, 1, count)
    held = own.astype(wide) + got_across.astype(wide) + got_along.astype(wide)
    for bit in reversed(outer_bits(count)):
        split = held.reshape(2, -1, rows, columns)
        side = my_bit(bit)
        keep = lax.dynamic_index_in_dim(split, side, 0, keepdims=False)
        send = lax.dynamic_index_in_dim(split, 1 - side, 0, keepdims=False)
        got = swap_bit(send.astype(low), bit, count).astype(wide)
        if bit == PAIR and paired:
            return pick(side == 0, keep[0], got[0], 0)
        held = keep + got
    return held[0]


def swap_tensor(values):
    return lax.ppermute(values, "tensor", [(0, 1), (1, 0)])


def both_halves(values):
    return lax.all_gather(values, "tensor", axis=1, tiled=True)


def own_half(values):
    return lax.dynamic_slice_in_dim(
        values, lax.axis_index("tensor") * (values.shape[1] // 2), values.shape[1] // 2, 1
    )


def rows_half(values, axis):
    half = values.shape[axis] // 2
    return values.reshape(values.shape[:axis] + (2, half) + values.shape[axis + 1 :])


def pair_rows(values):
    tensor = lax.axis_index("tensor")
    half = lax.dynamic_index_in_dim(rows_half(values, 0), tensor, 0, keepdims=False)
    got = swap_bit(half, PAIR, lax.axis_size("dp"))
    return jnp.concatenate([values, lax.all_gather(got, "tensor", axis=0, tiled=True)])


def pair_sum(keep, send):
    chip = keep.astype(wide) + swap_tensor(send).astype(wide)
    got = swap_bit(chip[1].astype(low), PAIR, lax.axis_size("dp"))
    total = (chip[0] + got.astype(wide)).astype(low)
    return lax.all_gather(total, "tensor", axis=0, tiled=True)


def unit_start(units):
    return (lax.axis_index("tensor") * 2 + my_bit(PAIR)) * units


def deal(values):
    return lax.all_to_all(values, everyone, split_axis=0, concat_axis=0, tiled=True)


def sum_to_owner(values, owners):
    lead = values.shape[:-1]
    dealt = jnp.moveaxis(values.reshape(lead + (owners, -1)), -2, 0)
    return dealt.reshape(owners, -1)


def from_owners(values, lead):
    owners = values.shape[0]
    return jnp.moveaxis(values.reshape((owners,) + lead + (-1,)), 0, -2).reshape(lead + (-1,))


def padded(width):
    return width + -width % 128


def fixed(*shape):
    return pl.BlockSpec(shape, lambda i, *_: (0,) * len(shape))


def by_rows(rows, *rest):
    return pl.BlockSpec((rows,) + rest, lambda i, *_: (i,) + (0,) * len(rest))


def cost(flops, bytes_accessed, transcendentals=0):
    return pl.CostEstimate(
        flops=flops, bytes_accessed=bytes_accessed, transcendentals=transcendentals
    )


def column_sum(values):
    return jnp.sum(values, axis=0, keepdims=True)


def same_place(rows, place_count):
    if rows == place_count:
        return None
    first = lax.broadcasted_iota(jnp.int32, (rows, rows), 0)
    second = lax.broadcasted_iota(jnp.int32, (rows, rows), 1)
    return lax.rem(first, place_count) == lax.rem(second, place_count)


def head_probs(query, keys, mask):
    scores = product_right(query, keys) * (HEAD_DIM ** (-0.5))
    if mask is not None:
        scores = jnp.where(mask, scores, -1e30)
    exponent = jnp.exp(scores - jnp.max(scores, axis=-1, keepdims=True))
    return exponent * (1.0 / jnp.sum(exponent, axis=-1, keepdims=True))


def attention_kernel(
    place_count, x_ref, mod_ref, weight_ref, bias_ref, hidden_ref, joined_ref, attended_ref, out_ref
):
    rows, width = attended_ref.shape
    joined_width = joined_ref.shape[1]
    normed, _ = layer_norm(x_ref[...].astype(wide))
    hidden = (normed * (1.0 + mod_ref[0, 1:2]) + mod_ref[0, 0:1]).astype(low)
    hidden_ref[...] = hidden
    joined_ref[...] = (product(hidden, weight_ref[:, :joined_width]) + bias_ref[...]).astype(low)
    mask = None if place_count is None else same_place(rows, place_count)
    for start in range(0, width, HEAD_DIM):
        query, keys, value = (
            joined_ref[:, part * width + start : part * width + start + HEAD_DIM]
            for part in range(3)
        )
        probs = head_probs(query, keys, mask).astype(low)
        attended_ref[:, start : start + HEAD_DIM] = product(probs, value).astype(low)
    out_ref[...] = product_right(
        attended_ref[...], weight_ref[:, joined_width : joined_width + width]
    ).astype(low)


def attention_back_kernel(
    place_count, upstream_ref, weight_ref, joined_ref, grad_ref, out_ref, bias_ref
):
    rows, joined_width = joined_ref.shape
    width = upstream_ref.shape[1] // 2
    score_scale = HEAD_DIM ** (-0.5)
    attended_grad = product(
        upstream_ref[...], weight_ref[:, joined_width : joined_width + width]
    ).astype(low)
    mask = None if place_count is None else same_place(rows, place_count)
    for start in range(0, width, HEAD_DIM):
        query, keys, value = (
            joined_ref[:, part * width + start : part * width + start + HEAD_DIM]
            for part in range(3)
        )
        upstream = attended_grad[:, start : start + HEAD_DIM]
        probs = head_probs(query, keys, mask)
        value_grad = product_left(probs.astype(low), upstream)
        prob_grad = product_right(upstream, value)
        centre = jnp.sum(probs * prob_grad, axis=-1, keepdims=True)
        score_grad = (probs * (prob_grad - centre)).astype(low)
        query_grad = product(score_grad, keys) * score_scale
        keys_grad = product_left(score_grad, query) * score_scale
        for part, grad in enumerate((query_grad, keys_grad, value_grad)):
            grad_ref[:, part * width + start : part * width + start + HEAD_DIM] = grad.astype(low)
    spare = joined_width - 3 * width
    if spare:
        grad_ref[:, 3 * width :] = jnp.zeros((rows, spare), low)
    joined_grad = grad_ref[...]
    bias_ref[0] = column_sum(joined_grad.astype(wide))
    out_ref[...] = product_right(joined_grad, weight_ref[:, :joined_width]).astype(low)


def middle_kernel(x_ref, mine_ref, theirs_ref, bias_ref, mod_ref, middle_ref, hidden_ref):
    branch = mine_ref[...].astype(wide) + theirs_ref[...].astype(wide) + bias_ref[...]
    middle = x_ref[...].astype(wide) + mod_ref[0, 2:3] * branch
    middle_ref[...] = middle
    normed, _ = layer_norm(middle)
    hidden_ref[...] = (normed * (1.0 + mod_ref[0, 4:5]) + mod_ref[0, 3:4]).astype(low)


def split_halves(place_ref, partial_ref, keep_ref, send_ref):
    tensor = place_ref[0]
    half = keep_ref.shape[1]
    keep_ref[0] = partial_ref[pl.ds(pl.multiple_of(tensor * half, 8), half), :].astype(low)
    send_ref[0] = partial_ref[pl.ds(pl.multiple_of((1 - tensor) * half, 8), half), :].astype(low)


def gelu_parts(values):
    root = 0.7978845608028654
    square = values * values
    bend = jnp.tanh(root * (values + 0.044715 * values * square))
    return (bend, root * (1.0 + 3.0 * 0.044715 * square))


def units_kernel(
    place_ref,
    hidden_ref,
    up_ref,
    down_ref,
    bias_ref,
    inner_ref,
    active_ref,
    keep_ref,
    send_ref,
    partial_ref,
):
    inner = product(hidden_ref[...], up_ref[...]) + bias_ref[...]
    inner_ref[...] = inner
    bend, _ = gelu_parts(inner)
    active = (0.5 * inner * (1.0 + bend)).astype(low)
    active_ref[...] = active
    partial_ref[...] = product_right(active, down_ref[...])
    split_halves(place_ref, partial_ref, keep_ref, send_ref)


def units_back_kernel(
    place_ref,
    upstream_ref,
    up_ref,
    down_ref,
    inner_ref,
    grad_ref,
    keep_ref,
    send_ref,
    bias_ref,
    partial_ref,
):
    inner = inner_ref[...]
    bend, slope = gelu_parts(inner)
    derivative = 0.5 * (1.0 + bend) + 0.5 * inner * (1.0 - bend * bend) * slope
    grad = (product(upstream_ref[...], down_ref[...]) * derivative).astype(low)
    grad_ref[...] = grad

    @pl.when(pl.program_id(0) == 0)
    def _():
        bias_ref[...] = jnp.zeros_like(bias_ref)

    bias_ref[...] += column_sum(grad.astype(wide))
    partial_ref[...] = product_right(grad, up_ref[...])
    split_halves(place_ref, partial_ref, keep_ref, send_ref)


def result_kernel(middle_ref, branch_ref, bias_ref, mod_ref, out_ref):
    branch = branch_ref[...].astype(wide) + bias_ref[...]
    out_ref[...] = (middle_ref[...] + mod_ref[0, 5:6] * branch).astype(low)


def turn_kernel(upstream_ref, branch_ref, bias_ref, mod_ref, grad_ref, sums_ref):
    upstream = upstream_ref[...].astype(wide)
    branch = branch_ref[...].astype(wide) + bias_ref[...]
    grad = (upstream * mod_ref[0, 5:6]).astype(low)
    grad_ref[...] = grad
    sums_ref[0, 0:1] = column_sum(upstream * branch)
    sums_ref[0, 1:2] = column_sum(grad.astype(wide))


def middle_back_kernel(
    upstream_ref,
    hidden_ref,
    middle_ref,
    mine_ref,
    theirs_ref,
    bias_ref,
    mod_ref,
    out_ref,
    grad_ref,
    sums_ref,
):
    normed, inverse = layer_norm(middle_ref[...])
    hidden_grad = hidden_ref[...].astype(wide)
    middle_grad = upstream_ref[...].astype(wide) + layer_norm_back(
        normed, inverse, hidden_grad * (1.0 + mod_ref[0, 4:5])
    )
    out_ref[...] = middle_grad
    grad = (middle_grad * mod_ref[0, 2:3]).astype(low)
    grad_ref[...] = grad
    branch = mine_ref[...].astype(wide) + theirs_ref[...].astype(wide) + bias_ref[...]
    sums_ref[0, 0:1] = column_sum(hidden_grad)
    sums_ref[0, 1:2] = column_sum(hidden_grad * normed)
    sums_ref[0, 2:3] = column_sum(middle_grad * branch)
    sums_ref[0, 3:4] = column_sum(grad.astype(wide))


def input_back_kernel(middle_ref, mine_ref, theirs_ref, x_ref, mod_ref, out_ref, sums_ref):
    normed, inverse = layer_norm(x_ref[...].astype(wide))
    hidden_grad = mine_ref[...].astype(wide) + theirs_ref[...].astype(wide)
    out_ref[...] = (
        middle_ref[...] + layer_norm_back(normed, inverse, hidden_grad * (1.0 + mod_ref[0, 1:2]))
    ).astype(out_ref.dtype)
    sums_ref[0, 0:1] = column_sum(hidden_grad)
    sums_ref[0, 1:2] = column_sum(hidden_grad * normed)


def array(dtype, *shape):
    return jax.ShapeDtypeStruct(shape, dtype)


def attention_forward(x, mods, weight, bias, place_count):
    rows, width = x.shape
    groups = mods.shape[0]
    block = rows // groups
    part, joined = width // 2, bias.shape[1]
    return pl.pallas_call(
        functools.partial(attention_kernel, place_count),
        grid=(groups,),
        in_specs=[
            by_rows(block, width),
            by_rows(1, 6, width),
            fixed(*weight.shape),
            fixed(*bias.shape),
        ],
        out_specs=[by_rows(block, n) for n in (width, joined, part, width)],
        out_shape=[array(low, rows, n) for n in (width, joined, part, width)],
        name="attention",
        cost_estimate=cost(
            2 * rows * width * (joined + part) + 4 * rows * block * part,
            2 * weight.size + 2 * rows * (3 * width + joined + part),
            rows * block * part // HEAD_DIM,
        ),
    )(x, mods, weight, bias)


def attention_backward(upstream, weight, joined, groups, place_count):
    rows, width = upstream.shape
    block = rows // groups
    columns = joined.shape[1]
    return pl.pallas_call(
        functools.partial(attention_back_kernel, place_count),
        grid=(groups,),
        in_specs=[by_rows(block, width), fixed(*weight.shape), by_rows(block, columns)],
        out_specs=[by_rows(block, columns), by_rows(block, width), by_rows(1, 1, columns)],
        out_shape=[
            array(low, rows, columns),
            array(low, rows, width),
            array(wide, groups, 1, columns),
        ],
        name="attention_back",
        cost_estimate=cost(
            2 * rows * width * weight.shape[1] + 5 * rows * block * width,
            2 * weight.size + 2 * rows * (2 * width + 2 * columns),
            rows * block * width // (2 * HEAD_DIM),
        ),
    )(upstream, weight, joined)


def row_kernel(body, groups, row_inputs, fixed_inputs, mods, outs, sums, name):
    rows, width = row_inputs[0].shape
    block = rows // groups
    sum_shape = [array(wide, groups, 8, width)] * sums
    moved = sum(item.size * item.dtype.itemsize for item in row_inputs)
    return pl.pallas_call(
        body,
        grid=(groups,),
        in_specs=[by_rows(block, width) for _ in row_inputs]
        + [fixed(*item.shape) for item in fixed_inputs]
        + [by_rows(1, 6, width)],
        out_specs=[by_rows(block, width) for _ in outs] + [by_rows(1, 8, width)] * sums,
        out_shape=[array(dtype, rows, width) for dtype in outs] + sum_shape,
        name=name,
        cost_estimate=cost(20 * rows * width, moved + 4 * rows * width * len(outs)),
    )(*row_inputs, *fixed_inputs, mods)


def units_call(body, rows_in, up, down, extra, extra_spec, outs, out_specs, name):
    rows, width = rows_in.shape
    units = up.shape[1]
    half = rows // 2
    halves = array(low, 2, half // 2, width)
    at = pl.BlockSpec((1, half // 2, width), lambda i, *_: (i, 0, 0))
    return pl.pallas_call(
        body,
        grid_spec=pltpu.PrefetchScalarGridSpec(
            num_scalar_prefetch=1,
            grid=(2,),
            in_specs=[
                by_rows(half, width),
                fixed(width, units),
                fixed(width, units),
                extra_spec,
            ],
            out_specs=out_specs[: len(outs) - 1] + [at, at] + out_specs[len(outs) - 1 :]
            if name == "units_back"
            else out_specs + [at, at],
            scratch_shapes=[pltpu.VMEM((half, width), wide)],
        ),
        out_shape=outs[:-1] + [halves, halves] + outs[-1:]
        if name == "units_back"
        else outs + [halves, halves],
        name=name,
        cost_estimate=cost(
            4 * rows * width * units,
            4 * width * units + 4 * rows * width + 6 * rows * units,
            rows * units,
        ),
    )(place_scalars(), rows_in, up, down, extra)


def units_forward(hidden, up, down, bias):
    rows, units = hidden.shape[0], up.shape[1]
    block = by_rows(rows // 2, units)
    return units_call(
        units_kernel,
        hidden,
        up,
        down,
        bias,
        fixed(1, units),
        [array(wide, rows, units), array(low, rows, units)],
        [block, block],
        "units",
    )


def units_backward(upstream, up, down, inner):
    rows, units = inner.shape
    block = by_rows(rows // 2, units)
    return units_call(
        units_back_kernel,
        upstream,
        up,
        down,
        inner,
        block,
        [array(low, rows, units), array(wide, 1, units)],
        [block, fixed(1, units)],
        "units_back",
    )


def block_forward(x, mods, weights, biases, place_count):
    wattn, up, down = weights
    bias_joined, bias_out, bias_fc2, bias_fc1 = biases
    groups = mods.shape[0]
    hidden_attn, joined, attended, mine = attention_forward(
        x, mods, wattn, bias_joined, place_count
    )
    theirs = swap_tensor(mine)
    middle, hidden_mlp = row_kernel(
        middle_kernel, groups, (x, mine, theirs), (bias_out,), mods, (wide, low), 0, "middle"
    )
    flat_mlp = pair_rows(hidden_mlp)
    inner, active, keep, send = units_forward(flat_mlp, up, down, bias_fc1)
    branch_mlp = pair_sum(keep, send)
    (result,) = row_kernel(
        result_kernel, groups, (middle, branch_mlp), (bias_fc2,), mods, (low,), 0, "result"
    )
    saved = (
        x,
        hidden_attn,
        joined,
        attended,
        mine,
        theirs,
        middle,
        flat_mlp,
        inner,
        active,
        branch_mlp,
    )
    return (result, saved)


def block_backward(upstream, saved, mods, weights, biases, place_count, grad_dtype):
    x, hidden_attn, joined, attended, mine, theirs, middle, flat_mlp, inner, active, branch = saved
    wattn, up, down = weights
    _, bias_out, bias_fc2, _ = biases
    groups, width = mods.shape[0], x.shape[1]
    part_width = width // 2
    mlp_grad, turn_sums = row_kernel(
        turn_kernel, groups, (upstream, branch), (bias_fc2,), mods, (low,), 1, "turn"
    )
    flat_grad = pair_rows(mlp_grad)
    inner_grad, keep, send, fc1_bias = units_backward(flat_grad, up, down, inner)
    units_reduced = scatter_product([(flat_mlp, inner_grad), (flat_grad, active)], True)
    hidden_grad = pair_sum(keep, send)
    middle_grad, attn_grad, middle_sums = row_kernel(
        middle_back_kernel,
        groups,
        (upstream, hidden_grad, middle, mine, theirs),
        (bias_out,),
        mods,
        (wide, low),
        1,
        "middle_back",
    )
    joined_grad, mine_grad, joined_bias = attention_backward(
        attn_grad, wattn, joined, groups, place_count
    )
    attn_reduced = scatter_product([(hidden_attn, joined_grad), (attn_grad, attended)], False)
    theirs_grad = swap_tensor(mine_grad)
    input_grad, input_sums = row_kernel(
        input_back_kernel,
        groups,
        (middle_grad, mine_grad, theirs_grad, x),
        (),
        mods,
        (grad_dtype,),
        1,
        "input_back",
    )
    mod_grad = 0.5 * jnp.concatenate(
        [input_sums[:, :2], middle_sums[:, 2:3], middle_sums[:, :2], turn_sums[:, :1]], axis=1
    )
    joined_bias = jnp.sum(joined_bias, axis=(0, 1))
    at = lax.axis_index("tensor") * part_width
    proj_grad = jnp.stack(
        [
            widen(joined_bias[:part_width], at, width),
            widen(joined_bias[2 * part_width : 3 * part_width], at, width),
            0.5 * jnp.sum(middle_sums[:, 3], axis=0),
            0.5 * jnp.sum(turn_sums[:, 1], axis=0),
        ]
    )
    units = fc1_bias.shape[1]
    hidden_bias = widen(fc1_bias[0], unit_start(units), units * 4)
    return (input_grad, mod_grad, (attn_reduced, units_reduced), proj_grad, hidden_bias)


def widen(local_part, offset, total):
    return lax.dynamic_update_slice_in_dim(jnp.zeros((total,), wide), local_part, offset, 0)


def tensor_part(values):
    part = values.shape[-1] // 2
    return lax.dynamic_slice_in_dim(
        values, lax.axis_index("tensor") * part, part, values.ndim - 1
    )


def per_device(tokens, cond, out_grad, w_qkv, w_out, w_fc1, w_fc2, w_ada, b_ada, b_proj, b_fc1):
    dp_count = lax.axis_size("dp")
    all_devices = lax.axis_size(everyone)
    flat_index = lax.axis_index(everyone)
    tensor = lax.axis_index("tensor")
    width = tokens.shape[3]
    clip_count = cond.shape[0]
    own_rows, head_width = w_qkv.shape[1], w_qkv.shape[3]
    units = w_fc1.shape[2] // 2
    own_width = width // all_devices
    own_start = flat_index * own_width
    joined_width = 3 * head_width

    def pad_columns(values):
        return jnp.pad(values, ((0, 0), (0, padded(values.shape[1]) - values.shape[1])))

    def units_part(layer, side):
        first = side * units
        return jnp.concatenate(
            [
                lax.dynamic_slice_in_dim(w_fc1[layer], first, units, 1),
                lax.dynamic_slice_in_dim(w_fc2[layer], first, units, 0).T,
            ],
            axis=1,
        )

    shards = []
    for layer in range(2):
        shards.append(
            jnp.concatenate(
                [
                    pad_columns(w_qkv[layer].reshape(own_rows, joined_width)),
                    pad_columns(w_out[layer].T),
                ],
                axis=1,
            )
        )
        shards.append((units_part(layer, my_bit(PAIR)), units_part(layer, 1 - my_bit(PAIR))))
    full = gather_all(shards, dp_count)
    gathered = [
        (full[2 * layer], full[2 * layer + 1][:, :units], full[2 * layer + 1][:, units:])
        for layer in range(2)
    ]

    cond_float = cond.astype(wide)
    gated_low = jax.nn.silu(cond_float).astype(low)
    gated_own = lax.dynamic_slice_in_dim(gated_low, own_start, own_width, 1).astype(wide)
    w_ada_wide = w_ada.astype(wide)
    partial_mod = jnp.stack(
        [
            jnp.sum(gated_own[clip][None, :, None, None] * w_ada_wide, axis=1)
            for clip in range(clip_count)
        ],
        axis=1,
    )
    own_mod = jnp.sum(deal(sum_to_owner(partial_mod, all_devices)), axis=0).reshape(
        2, clip_count, 6, own_width
    )
    own_mod = own_mod + b_ada.astype(wide)[:, None]
    pieces = (own_mod, b_proj.astype(wide), b_fc1.astype(wide))
    packed = jnp.concatenate([piece.reshape(-1) for piece in pieces])
    dealt = deal(jnp.broadcast_to(packed[None], (all_devices, packed.shape[0])))
    first_end, second_end = pieces[0].size, pieces[0].size + pieces[1].size
    modulation = from_owners(dealt[:, :first_end], (2, clip_count, 6))
    proj_full = from_owners(dealt[:, first_end:second_end], (2, 4))
    hidden_full = from_owners(dealt[:, second_end:], (2,))

    frames_dev, place_half = tokens.shape[0], tokens.shape[2]
    frame_ids = lax.axis_index("dp") * frames_dev + jnp.arange(frames_dev, dtype=jnp.int32)
    onehot = (
        frame_ids[:, None] // FRAMES == jnp.arange(clip_count, dtype=jnp.int32)[None, :]
    ).astype(wide)
    first_mod = jnp.sum(onehot[:, :, None, None] * modulation[0][None], axis=1)
    second_mod = modulation[1]

    def layer_biases(layer):
        bias_query = tensor_part(proj_full[layer, 0])
        bias_value = tensor_part(proj_full[layer, 1])
        joined = jnp.concatenate([bias_query, jnp.zeros_like(bias_query), bias_value])
        return (
            jnp.pad(joined, (0, padded(joined_width) - joined_width))[None],
            proj_full[layer, 2:3],
            proj_full[layer, 3:4],
            lax.dynamic_slice_in_dim(hidden_full[layer], unit_start(units), units)[None],
        )

    def flat(values):
        return both_halves(values).reshape(-1, width)

    def own_places(values, frames):
        split = values.reshape(frames, 2, -1, width)
        return lax.dynamic_slice_in_dim(split, tensor, 1, 1)

    all_frames, own_place_count = frames_dev * dp_count, 2 * (place_half // dp_count)
    first_x = flat(tokens)
    first_biases, second_biases = layer_biases(0), layer_biases(1)
    first_out, first_saved = block_forward(first_x, first_mod, gathered[0], first_biases, None)
    arrived = lax.all_to_all(
        own_places(first_out, frames_dev), "dp", split_axis=2, concat_axis=0, tiled=True
    )
    second_out, second_saved = block_forward(
        flat(arrived), second_mod, gathered[1], second_biases, own_place_count
    )
    output = own_places(second_out, all_frames)

    second_grad, second_dmod, second_reduced, second_proj, second_hidden = block_backward(
        flat(out_grad), second_saved, second_mod, gathered[1], second_biases, own_place_count, low
    )
    arrived_back = lax.all_to_all(
        own_places(second_grad, all_frames), "dp", split_axis=0, concat_axis=2, tiled=True
    )
    first_grad, first_dmod, first_reduced, first_proj, first_hidden = block_backward(
        flat(arrived_back), first_saved, first_mod, gathered[0], first_biases, None, wide
    )
    tokens_grad = own_places(first_grad, frames_dev)

    dmod_clips = jnp.stack(
        [jnp.sum(onehot[:, :, None, None] * first_dmod[:, None], axis=0), second_dmod]
    )
    small = (
        dmod_clips,
        jnp.stack([first_proj, second_proj]),
        jnp.stack([first_hidden, second_hidden]),
    )
    owned = jnp.sum(
        deal(jnp.concatenate([sum_to_owner(piece, all_devices) for piece in small], axis=1)), axis=0
    )
    own_dmod = owned[:first_end]
    b_proj_grad = owned[first_end:second_end].reshape(2, 4, own_width)
    b_fc1_grad = owned[second_end:].reshape(2, -1)
    summed_mod = from_owners(
        deal(jnp.broadcast_to(own_dmod[None], (all_devices, own_dmod.shape[0]))), (2, clip_count, 6)
    )
    w_ada_grad = sum(
        gated_own[clip][None, :, None, None] * summed_mod[:, clip][:, None]
        for clip in range(clip_count)
    )
    b_ada_grad = jnp.sum(own_dmod.reshape(2, clip_count, 6, own_width), axis=1)
    silu_grad = jnp.stack(
        [
            jnp.sum(summed_mod[:, clip][:, None] * w_ada_wide, axis=(0, 2, 3))
            for clip in range(clip_count)
        ]
    )
    cond_own = lax.dynamic_slice_in_dim(cond_float, own_start, own_width, 1)
    cond_grad = jax.vjp(jax.nn.silu, cond_own)[1](silu_grad)[0]

    reduced = (first_reduced, second_reduced)
    out_start = padded(joined_width)
    w_qkv_grad = jnp.stack(
        [part[0][:, :joined_width].reshape(own_rows, 3, head_width) for part in reduced]
    )
    w_out_grad = jnp.stack(
        [part[0][:, out_start : out_start + head_width].T for part in reduced]
    )
    w_fc1_grad = jnp.stack(
        [jnp.concatenate([part[1][0, :, :units], part[1][1, :, :units]], axis=1) for part in reduced]
    )
    w_fc2_grad = jnp.stack(
        [part[1][:, :, units:].transpose(0, 2, 1).reshape(2 * units, own_rows) for part in reduced]
    )
    return (
        output,
        tokens_grad,
        cond_grad,
        w_qkv_grad,
        w_out_grad,
        w_fc1_grad,
        w_fc2_grad,
        w_ada_grad,
        b_ada_grad,
        b_proj_grad,
        b_fc1_grad,
    )


def solution(mesh):
    return jax.shard_map(
        per_device,
        mesh=mesh,
        in_specs=(
            P("dp", "tensor", None, None),
            P(),
            P(None, "tensor", "dp", None),
            P(None, "dp", None, "tensor"),
            P(None, "tensor", "dp"),
            P(None, "dp", "tensor"),
            P(None, "tensor", "dp"),
            P(None, ("dp", "tensor"), None, None),
            P(None, None, ("dp", "tensor")),
            P(None, None, ("dp", "tensor")),
            P(None, ("dp", "tensor")),
        ),
        out_specs=(
            P(None, "tensor", "dp", None),
            P("dp", "tensor", None, None),
            P(None, ("dp", "tensor")),
            P(None, "dp", None, "tensor"),
            P(None, "tensor", "dp"),
            P(None, "dp", "tensor"),
            P(None, "tensor", "dp"),
            P(None, ("dp", "tensor"), None, None),
            P(None, None, ("dp", "tensor")),
            P(None, None, ("dp", "tensor")),
            P(None, ("dp", "tensor")),
        ),
        check_vma=False,
    )
```

time: 1130 us -> 762 us (0.67)
  waiting for transfers between devices: 600 us -> 293 us
  Pallas kernels: 27.9 us -> 158 us
  matrix products: 90.2 us -> 0 us
  other arithmetic: 145 us -> 70.5 us
  local copies, waits for them, and re-layouts: 160 us -> 105 us
  blocking collectives: 9.5 us -> 29.1 us
    ppermute x48 -> x56, waiting for transfers between devices: 503 us -> 263 us  [swap_bit(): return lax.ppermute(values, 'dp', [(i, i ^ 1 << bit) for i in range(count)])]
    pallas_call x4 -> x26, Pallas kernels: 27.9 us -> 158 us  [the longest x4 35.6 us: units_call(): pl.pallas_call(body, grid_spec=pltpu.PrefetchScalarGridSpec(num_scalar_pr...]
    dot_general x26 -> x0, matrix products: 90.2 us -> none  [the longest x8 33.5 us: product(): return jnp.dot(left_side, right_side, preferred_element_type=wide)]
    all_to_all x2, waiting for transfers between devices: 43 us -> 6.2 us  [the longest x1 6.2 us: per_device(): lax.all_to_all(own_places(first_out, frames_dev), 'dp', split_axis=2, con...]
    all_to_all x4, waiting for transfers between devices: 53.5 us -> 18.8 us  [deal(): lax.all_to_all(values, everyone, split_axis=0, concat_axis=0, tiled=True)]
    another operation x41 -> x18, local copies, waits for them, and re-layouts: 39 us -> 6.63 us  [the longest x10 2.37 us: block_backward(): jnp.stack([widen(joined_bias[:part_width], at, width), widen(joined_bias[...]
    another operation x46 -> x18, other arithmetic: 42.3 us -> 11.3 us  [the longest x12 6.62 us: pick(): jnp.stack([jnp.where(first, mine, theirs), jnp.where(first, theirs, mine)...]
    slice x11 -> x31, local copies, waits for them, and re-layouts: 5.07 us -> 35 us  [the longest x2 10.5 us: per_device(): full[2 * layer + 1][:, units:]]
  transfers between devices with their start and end apart: 62 -> 70, of which waited for: 30 -> 30; matrix products, arithmetic and copies ran while one was open for 29% -> 19% of each run, Pallas kernels for 2% -> 17%
where the time goes in v2:
time: 762 us; the launch traced here: 754 us
  waiting for transfers between devices  293 us (38%)
  Pallas kernels  158 us (21%)
  local copies, waits for them, and re-layouts  105 us (14%)
  starting transfers between devices  96.3 us (13%)
  other arithmetic  70.5 us (9%)
  blocking collectives  29.1 us (4%)
    ppermute x56, waiting for transfers between devices, swap_bit(): return lax.ppermute(values, 'dp', [(i, i ^ 1 << bit) for i in range(count)])  263 us
    ppermute x56, starting transfers between devices, swap_bit(): return lax.ppermute(values, 'dp', [(i, i ^ 1 << bit) for i in range(count)])  70.8 us
    pallas_call x4, Pallas kernels, units_call(): pl.pallas_call(body, grid_spec=pltpu.PrefetchScalarGridSpec(num_scalar_pr...  35.6 us
    pallas_call x10, Pallas kernels, row_kernel(): pl.pallas_call(body, grid=(groups,), in_specs=[by_rows(block, width) for...  32.1 us
    pallas_call x4, Pallas kernels, scatter_product(): pl.pallas_call(functools.partial(weight_grad_kernel, count, tuple(starts)...  30.1 us
    pallas_call x2, Pallas kernels, attention_backward(): pl.pallas_call(functools.partial(attention_back_kernel, place_count), gri...  22.1 us
    pallas_call x4, Pallas kernels, arrange(): pl.pallas_call(arrange_kernel, out_shape=jax.ShapeDtypeStruct((groups * 4...  21.5 us
    all_to_all x4, waiting for transfers between devices, deal(): lax.all_to_all(values, everyone, split_axis=0, concat_axis=0, tiled=True)  18.8 us
  transfers between devices with their start and end apart: 70, of which 30 were waited for; matrix products, arithmetic and copies ran while one was open for 19% of the time, Pallas kernels for 17%

profile of v2, /device:TPU:0, one launch (start us, length us, event | category | flops | bytes accessed | tf_op | source)
XLA Modules:
  0.0 754.0 jit_solution(1793102098072067623)
XLA Ops:
  5.7 7.4 all-to-all-start
  17.8 7.7 %collective-permute-done = bf16[1,72,2432]{2,1,0:T(8,128)(2,1)} collective-permute-done((bf16[1,72,2432]{2,1,0:T(8,128)(2,1)}, bf16[1,72,2432]{2,1,0:T(8,128)(2,1)}, u32[]{:S(2)}, u32[]{:S(2)}) %collective-permute-start) | collective-permute-done | bytes 350240 | tf_op jit(solution)/shard_map/ppermute | solution.py:54
  30.1 30.8 %collective-permute-done.1 = bf16[2,72,2432]{2,1,0:T(8,128)(2,1)S(1)} collective-permute-done((bf16[2,72,2432]{2,1,0:T(8,128)(2,1)}, bf16[2,72,2432]{2,1,0:T(8,128)(2,1)S(1)}, u32[]{:S(2)}, u32[]{:S(2)}) %collective-permute-start.1) | collective-permute-done | bytes 700448 | tf_op jit(solution)/shard_map/ppermute | solution.py:54
  62.8 7.9 %collective-permute-done.8 = bf16[1,72,2304]{2,1,0:T(8,128)(2,1)S(1)} collective-permute-done((bf16[1,72,2304]{2,1,0:T(8,128)(2,1)S(1)}, bf16[1,72,2304]{2,1,0:T(8,128)(2,1)S(1)}, u32[]{:S(2)}, u32[]{:S(2)}) %collective-permute-start.8) | collective-permute-done | bytes 331808 | tf_op jit(solution)/shard_map/ppermute | solution.py:54
  80.3 24.7 %collective-permute-done.9 = bf16[2,72,2304]{2,1,0:T(8,128)(2,1)} collective-permute-done((bf16[2,72,2304]{2,1,0:T(8,128)(2,1)}, bf16[2,72,2304]{2,1,0:T(8,128)(2,1)}, u32[]{:S(2)}, u32[]{:S(2)}) %collective-permute-start.9) | collective-permute-done | bytes 663584 | tf_op jit(solution)/shard_map/ppermute | solution.py:54
  119.9 22.6 %collective-permute-done.2.across_ref = bf16[4,72,2432]{2,1,0:T(8,128)(2,1)} collective-permute-done((bf16[4,72,2432]{2,1,0:T(8,128)(2,1)S(1)}, bf16[4,72,2432]{2,1,0:T(8,128)(2,1)}, u32[]{:S(2)}, u32[]{:S(2)}) %collective-permute-start.2) | collective-permute-done | bytes 1400864 | tf_op jit(solution)/shard_map/ppermute | solution.py:54
  172.2 8.4 %attention.2 = (bf16[256,1152]{1,0:T(8,128)(2,1)}, bf16[256,1792]{1,0:T(8,128)(2,1)}, bf16[256,576]{1,0:T(8,128)(2,1)}, bf16[256,1152]{1,0:T(8,128)(2,1)}) custom-call(bf16[256,1152]{1,0:T(8,128)(2,1)} %bitcast.316, f32[1,6,1152]{2,1,0:T(8,128)} %mul.246.mod_ref, bf16[1152,2432]{1,0:T(8,128)(2,1)} %bitcast.310, f32[1,1792]{1,0:T(1,128)} %broadcast_in_dim.48.bias_ref), custom_call_target="tpu_custom_call" | custom-call | flops 1547698176 | bytes 8585216 | tf_op jit(solution)/shard_map/attention/pallas_call | solution.py:505
  220.5 8.3 %units.2 = (f32[512,1152]{1,0:T(8,128)}, bf16[512,1152]{1,0:T(8,128)(2,1)}, bf16[2,128,1152]{2,1,0:T(8,128)(2,1)}, bf16[2,128,1152]{2,1,0:T(8,128)(2,1)}) custom-call(s32[2]{0:T(128)} %pad_add_fusion.place_ref, bf16[512,1152]{1,0:T(8,128)(2,1)} %copy-done.60, bf16[1152,1152]{1,0:T(8,128)(2,1)} %get-tuple-element.236.up_ref, ...), custom_call_target="tpu_custom_call" | custom-call | flops 2717908992 | bytes 11206656 | tf_op jit(solution)/shard_map/units/pallas_call | solution.py:572
  235.5 26.0 %collective-permute-done.25 = bf16[2,72,2304]{2,1,0:T(8,128)(2,1)S(1)} collective-permute-done((bf16[2,72,2304]{2,1,0:T(8,128)(2,1)S(1)}, bf16[2,72,2304]{2,1,0:T(8,128)(2,1)S(1)}, u32[]{:S(2)}, u32[]{:S(2)}) %collective-permute-start.25) | collective-permute-done | bytes 663584 | tf_op jit(solution)/shard_map/ppermute | solution.py:54
  303.3 8.4 %attention.3 = (bf16[256,1152]{1,0:T(8,128)(2,1)}, bf16[256,1792]{1,0:T(8,128)(2,1)}, bf16[256,576]{1,0:T(8,128)(2,1)}, bf16[256,1152]{1,0:T(8,128)(2,1)}) custom-call(bf16[256,1152]{1,0:T(8,128)(2,1)} %bitcast.319, f32[1,6,1152]{2,1,0:T(8,128)} %squeeze.157.mod_ref, bf16[1152,2432]{1,0:T(8,128)(2,1)} %bitcast.312, f32[1,1792]{1,0:T(1,128)} %broadcast_in_dim.53.bias_ref), custom_call_target="tpu_custom_call" | custom-call | flops 1547698176 | bytes 8585216 | tf_op jit(solution)/shard_map/attention/pallas_call | solution.py:505
  331.0 7.4 collective-permute-done.28.low_ref
  351.2 8.2 %units.3 = (f32[512,1152]{1,0:T(8,128)}, bf16[512,1152]{1,0:T(8,128)(2,1)}, bf16[2,128,1152]{2,1,0:T(8,128)(2,1)}, bf16[2,128,1152]{2,1,0:T(8,128)(2,1)}) custom-call(s32[2]{0:T(128)} %pad_add_fusion.place_ref, bf16[512,1152]{1,0:T(8,128)(2,1)} %copy-done.61, bf16[1152,1152]{1,0:T(8,128)(2,1)} %get-tuple-element.234.up_ref, ...), custom_call_target="tpu_custom_call" | custom-call | flops 2717908992 | bytes 11206656 | tf_op jit(solution)/shard_map/units/pallas_call | solution.py:572
  394.4 9.5 %units_back.2 = (bf16[512,1152]{1,0:T(8,128)(2,1)}, bf16[2,128,1152]{2,1,0:T(8,128)(2,1)}, bf16[2,128,1152]{2,1,0:T(8,128)(2,1)}, f32[1,1152]{1,0:T(1,128)}) custom-call(s32[2]{0:T(128)} %pad_add_fusion.place_ref, bf16[512,1152]{1,0:T(8,128)(2,1)} %copy-done.62, bf16[1152,1152]{1,0:T(8,128)(2,1)} %get-tuple-element.234.up_ref, ...), custom_call_target="tpu_custom_call" | custom-call | flops 2717908992 | bytes 11206656 | tf_op jit(solution)/shard_map/units_back/pallas_call | solution.py:572
  404.1 8.6 %weight_grad.7 = (bf16[4,72,2304]{2,1,0:T(8,128)(2,1)}, bf16[4,72,2304]{2,1,0:T(8,128)(2,1)}, bf16[4,72,2304]{2,1,0:T(8,128)(2,1)}, bf16[4,72,2304]{2,1,0:T(8,128)(2,1)}) custom-call(s32[2]{0:T(128)} %pad_add_fusion.place_ref, bf16[512,1152]{1,0:T(8,128)(2,1)} %copy-done.61, bf16[512,1152]{1,0:T(8,128)(2,1)} %get-tuple-element.149.refs_1_, ...), custom_call_target="tpu_custom_call" | custom-call | flops 2717908992 | bytes 12386304 | tf_op jit(solution)/shard_map/weight_grad/pallas_call | solution.py:195
  418.2 13.2 %collective-permute-done.60 = bf16[2,72,2304]{2,1,0:T(8,128)(2,1)S(1)} collective-permute-done((bf16[2,72,2304]{2,1,0:T(8,128)(2,1)S(1)}, bf16[2,72,2304]{2,1,0:T(8,128)(2,1)S(1)}, u32[]{:S(2)}, u32[]{:S(2)}) %collective-permute-start.60) | collective-permute-done | bytes 663584 | tf_op jit(solution)/shard_map/ppermute | solution.py:54
  441.3 11.1 %attention_back.2 = (bf16[256,1792]{1,0:T(8,128)(2,1)}, bf16[256,1152]{1,0:T(8,128)(2,1)}, f32[1,1,1792]{2,1,0:T(1,128)}) custom-call(bf16[256,1152]{1,0:T(8,128)(2,1)} %get-tuple-element.106.upstream_ref.refs_2_, bf16[1152,2432]{1,0:T(8,128)(2,1)} %bitcast.313, bf16[256,1792]{1,0:T(8,128)(2,1)} %get-tuple-element.107.joined_ref), custom_call_target="tpu_custom_call" | custom-call | flops 1811939328 | bytes 8617984 | tf_op jit(solution)/shard_map/attention_back/pallas_call | solution.py:529
  492.8 18.4 %collective-permute-done.59 = bf16[4,72,2304]{2,1,0:T(8,128)(2,1)} collective-permute-done((bf16[4,72,2304]{2,1,0:T(8,128)(2,1)}, bf16[4,72,2304]{2,1,0:T(8,128)(2,1)}, u32[]{:S(2)}, u32[]{:S(2)}) %collective-permute-start.59) | collective-permute-done | bytes 1327136 | tf_op jit(solution)/shard_map/ppermute | solution.py:54
  524.8 10.4 %collective-permute-done.36 = bf16[128,1152]{1,0:T(8,128)(2,1)S(1)} collective-permute-done((bf16[128,1152]{1,0:T(8,128)(2,1)S(1)}, bf16[128,1152]{1,0:T(8,128)(2,1)S(1)}, u32[]{:S(2)}, u32[]{:S(2)}) %collective-permute-start.36) | collective-permute-done | bytes 294944 | tf_op jit(solution)/shard_map/ppermute | solution.py:54
  538.6 9.5 %units_back.3 = (bf16[512,1152]{1,0:T(8,128)(2,1)}, bf16[2,128,1152]{2,1,0:T(8,128)(2,1)}, bf16[2,128,1152]{2,1,0:T(8,128)(2,1)}, f32[1,1152]{1,0:T(1,128)}) custom-call(s32[2]{0:T(128)} %pad_add_fusion.place_ref, bf16[512,1152]{1,0:T(8,128)(2,1)} %copy-done.63, bf16[1152,1152]{1,0:T(8,128)(2,1)} %get-tuple-element.236.up_ref, ...), custom_call_target="tpu_custom_call" | custom-call | flops 2717908992 | bytes 11206656 | tf_op jit(solution)/shard_map/units_back/pallas_call | solution.py:572
  549.3 8.6 %weight_grad.6 = (bf16[4,72,2304]{2,1,0:T(8,128)(2,1)}, bf16[4,72,2304]{2,1,0:T(8,128)(2,1)}, bf16[4,72,2304]{2,1,0:T(8,128)(2,1)}, bf16[4,72,2304]{2,1,0:T(8,128)(2,1)}) custom-call(s32[2]{0:T(128)} %pad_add_fusion.place_ref, bf16[512,1152]{1,0:T(8,128)(2,1)} %copy-done.60, bf16[512,1152]{1,0:T(8,128)(2,1)} %get-tuple-element.143.refs_1_, ...), custom_call_target="tpu_custom_call" | custom-call | flops 2717908992 | bytes 12386304 | tf_op jit(solution)/shard_map/weight_grad/pallas_call | solution.py:195
  601.7 11.1 %attention_back.3 = (bf16[256,1792]{1,0:T(8,128)(2,1)}, bf16[256,1152]{1,0:T(8,128)(2,1)}, f32[1,1,1792]{2,1,0:T(1,128)}) custom-call(bf16[256,1152]{1,0:T(8,128)(2,1)} %get-tuple-element.115.upstream_ref.refs_2_, bf16[1152,2432]{1,0:T(8,128)(2,1)} %bitcast.311, bf16[256,1792]{1,0:T(8,128)(2,1)} %get-tuple-element.116.joined_ref), custom_call_target="tpu_custom_call" | custom-call | flops 1811939328 | bytes 8617984 | tf_op jit(solution)/shard_map/attention_back/pallas_call | solution.py:529
  671.2 18.8 %all-to-all-done.5 = f32[32,1,432]{2,1,0:T(1,128)S(1)} async-done(((f32[32,1,432]{2,1,0:T(1,128)}), f32[32,1,432]{2,1,0:T(1,128)S(1)}, u32[]{:S(2)}, u32[]{:S(2)}) %all-to-all-start.5) | async-done | bytes 55328 | tf_op jit(solution)/shard_map/all_to_all | solution.py:268
  712.8 28.9 %collective-permute-done.44 = bf16[2,72,2432]{2,1,0:T(8,128)(2,1)S(1)} collective-permute-done((bf16[2,72,2432]{2,1,0:T(8,128)(2,1)S(1)}, bf16[2,72,2432]{2,1,0:T(8,128)(2,1)S(1)}, u32[]{:S(2)}, u32[]{:S(2)}) %collective-permute-start.44) | collective-permute-done | bytes 700448 | tf_op jit(solution)/shard_map/ppermute | solution.py:54
  743.6 7.6 %collective-permute-done.45 = bf16[1,72,2432]{2,1,0:T(8,128)(2,1)S(1)} collective-permute-done((bf16[1,72,2432]{2,1,0:T(8,128)(2,1)S(1)}, bf16[1,72,2432]{2,1,0:T(8,128)(2,1)S(1)}, u32[]{:S(2)}, u32[]{:S(2)}) %collective-permute-start.45) | collective-permute-done | bytes 350240 | tf_op jit(solution)/shard_map/ppermute | solution.py:54
  (582 shorter events, 428.1 us)
Async XLA Ops:
  5.7 68.8 %all-to-all-start = ((f32[32,1,432]{2,1,0:T(1,128)}), f32[32,1,432]{2,1,0:T(1,128)}, u32[]{:S(2)}, u32[]{:S(2)}) async-start(f32[32,1,432]{2,1,0:T(1,128)} %all_to_all.51), calls=%async_computation | async-start | bytes 131072 | tf_op jit(solution)/shard_map/all_to_all | solution.py:268
  27.5 33.4 %collective-permute-start.1 = (bf16[2,72,2432]{2,1,0:T(8,128)(2,1)}, bf16[2,72,2432]{2,1,0:T(8,128)(2,1)S(1)}, u32[]{:S(2)}, u32[]{:S(2)}) collective-permute-start(bf16[2,72,2432]{2,1,0:T(8,128)(2,1)} %maximum_bitcast_fusion), channel_id=1, source_target_pairs={{0,16},{2,18},{4,20},{6,22},{8,24},{10,26},{12,28},{14,30},{16,0},... | collective-permute-start | bytes 2101256 | tf_op jit(solution)/shard_map/ppermute | solution.py:54
  71.7 33.2 %collective-permute-start.9 = (bf16[2,72,2304]{2,1,0:T(8,128)(2,1)}, bf16[2,72,2304]{2,1,0:T(8,128)(2,1)}, u32[]{:S(2)}, u32[]{:S(2)}) collective-permute-start(bf16[2,72,2304]{2,1,0:T(8,128)(2,1)} %maximum_bitcast_fusion.2), channel_id=1, source_target_pairs={{0,16},{2,18},{4,20},{6,22},{8,24},{10,26},{12,28},{14,30},{16,0},... | collective-permute-start | bytes 1990664 | tf_op jit(solution)/shard_map/ppermute | solution.py:54
  76.3 36.9 %all-to-all-start.1 = ((f32[32,1,1008]{2,1,0:T(1,128)}), f32[32,1,1008]{2,1,0:T(1,128)S(1)}, u32[]{:S(2)}, u32[]{:S(2)}) async-start(f32[32,1,1008]{2,1,0:T(1,128)} %broadcast_in_dim.46), calls=%async_computation.1 | async-start | bytes 262144 | tf_op jit(solution)/shard_map/all_to_all | solution.py:268
  111.2 34.7 %collective-permute-start.3 = (bf16[4,72,2432]{2,1,0:T(8,128)(2,1)S(1)}, bf16[4,72,2432]{2,1,0:T(8,128)(2,1)}, u32[]{:S(2)}, u32[]{:S(2)}) collective-permute-start(bf16[4,72,2432]{2,1,0:T(8,128)(2,1)S(1)} %bitcast.331), channel_id=1, source_target_pairs={{0,4},{2,6},{4,0},{6,2},{8,12},{10,14},{12,8},{14,10},{16,20},{18,... | collective-permute-start | bytes 4202504 | tf_op jit(solution)/shard_map/ppermute | solution.py:54
  117.2 63.3 %collective-permute-start.17 = (bf16[2,72,2432]{2,1,0:T(8,128)(2,1)}, bf16[2,72,2432]{2,1,0:T(8,128)(2,1)}, u32[]{:S(2)}, u32[]{:S(2)}) collective-permute-start(bf16[2,72,2432]{2,1,0:T(8,128)(2,1)} %maximum_bitcast_fusion.1), channel_id=1, source_target_pairs={{0,16},{2,18},{4,20},{6,22},{8,24},{10,26},{12,28},{14,30},{16,0},... | collective-permute-start | bytes 2101256 | tf_op jit(solution)/shard_map/ppermute | solution.py:54
  150.4 42.7 %collective-permute-start.10 = (bf16[4,72,2304]{2,1,0:T(8,128)(2,1)S(1)}, bf16[4,72,2304]{2,1,0:T(8,128)(2,1)S(1)}, u32[]{:S(2)}, u32[]{:S(2)}) collective-permute-start(bf16[4,72,2304]{2,1,0:T(8,128)(2,1)S(1)} %bitcast.340), channel_id=1, source_target_pairs={{0,2},{2,0},{4,6},{6,4},{8,10},{10,8},{12,14},{14,12},{16,18},{18,... | collective-permute-start | bytes 3981320 | tf_op jit(solution)/shard_map/ppermute | solution.py:54
  150.8 43.1 %collective-permute-start.11 = (bf16[4,72,2304]{2,1,0:T(8,128)(2,1)S(1)}, bf16[4,72,2304]{2,1,0:T(8,128)(2,1)}, u32[]{:S(2)}, u32[]{:S(2)}) collective-permute-start(bf16[4,72,2304]{2,1,0:T(8,128)(2,1)S(1)} %bitcast.341), channel_id=1, source_target_pairs={{0,4},{2,6},{4,0},{6,2},{8,12},{10,14},{12,8},{14,10},{16,20},{18,... | collective-permute-start | bytes 3981320 | tf_op jit(solution)/shard_map/ppermute | solution.py:54
  233.1 33.7 %collective-permute-start.19 = (bf16[4,72,2432]{2,1,0:T(8,128)(2,1)S(1)}, bf16[4,72,2432]{2,1,0:T(8,128)(2,1)S(1)}, u32[]{:S(2)}, u32[]{:S(2)}) collective-permute-start(bf16[4,72,2432]{2,1,0:T(8,128)(2,1)S(1)} %bitcast.334), channel_id=1, source_target_pairs={{0,4},{2,6},{4,0},{6,2},{8,12},{10,14},{12,8},{14,10},{16,20},{18,... | collective-permute-start | bytes 4202504 | tf_op jit(solution)/shard_map/ppermute | solution.py:54
  234.7 34.6 %collective-permute-start.15 = (bf16[128,1152]{1,0:T(8,128)(2,1)S(1)}, bf16[128,1152]{1,0:T(8,128)(2,1)S(1)}, u32[]{:S(2)}, u32[]{:S(2)}) collective-permute-start(bf16[128,1152]{1,0:T(8,128)(2,1)S(1)} %fusion.27), channel_id=1, source_target_pairs={{0,8},{2,10},{4,12},{6,14},{8,0},{10,2},{12,4},{14,6},{16,24},{18,... | collective-permute-start | bytes 884744 | tf_op jit(solution)/shard_map/ppermute | solution.py:54
  283.4 37.1 %collective-permute-start.26 = (bf16[4,72,2304]{2,1,0:T(8,128)(2,1)S(1)}, bf16[4,72,2304]{2,1,0:T(8,128)(2,1)S(1)}, u32[]{:S(2)}, u32[]{:S(2)}) collective-permute-start(bf16[4,72,2304]{2,1,0:T(8,128)(2,1)S(1)} %bitcast.343), channel_id=1, source_target_pairs={{0,2},{2,0},{4,6},{6,4},{8,10},{10,8},{12,14},{14,12},{16,18},{18,... | collective-permute-start | bytes 3981320 | tf_op jit(solution)/shard_map/ppermute | solution.py:54
  285.2 36.9 %collective-permute-start.27 = (bf16[4,72,2304]{2,1,0:T(8,128)(2,1)S(1)}, bf16[4,72,2304]{2,1,0:T(8,128)(2,1)}, u32[]{:S(2)}, u32[]{:S(2)}) collective-permute-start(bf16[4,72,2304]{2,1,0:T(8,128)(2,1)S(1)} %bitcast.344), channel_id=1, source_target_pairs={{0,4},{2,6},{4,0},{6,2},{8,12},{10,14},{12,8},{14,10},{16,20},{18,... | collective-permute-start | bytes 3981320 | tf_op jit(solution)/shard_map/ppermute | solution.py:54
  432.8 60.0 %collective-permute-start.61 = (bf16[4,72,2304]{2,1,0:T(8,128)(2,1)}, bf16[4,72,2304]{2,1,0:T(8,128)(2,1)}, u32[]{:S(2)}, u32[]{:S(2)}) collective-permute-start(bf16[4,72,2304]{2,1,0:T(8,128)(2,1)} %pad_maximum_fusion.12), channel_id=1, source_target_pairs={{0,4},{2,6},{4,0},{6,2},{8,12},{10,14},{12,8},{14,10},{16,20},{18,... | collective-permute-start | bytes 3981320 | tf_op jit(solution)/shard_map/ppermute | solution.py:54
  463.3 47.9 %collective-permute-start.59 = (bf16[4,72,2304]{2,1,0:T(8,128)(2,1)}, bf16[4,72,2304]{2,1,0:T(8,128)(2,1)}, u32[]{:S(2)}, u32[]{:S(2)}) collective-permute-start(bf16[4,72,2304]{2,1,0:T(8,128)(2,1)} %pad_maximum_fusion.11), channel_id=1, source_target_pairs={{0,2},{2,0},{4,6},{6,4},{8,10},{10,8},{12,14},{14,12},{16,18},{18,... | collective-permute-start | bytes 3981320 | tf_op jit(solution)/shard_map/ppermute | solution.py:54
  475.7 39.6 %all-to-all-start.3 = ((bf16[16,1,8,1152]{3,2,1,0:T(8,128)(2,1)}), bf16[16,1,8,1152]{3,2,1,0:T(8,128)(2,1)S(1)}, u32[]{:S(2)}, u32[]{:S(2)}) async-start(bf16[16,1,8,1152]{3,2,1,0:T(8,128)(2,1)} %constant_dynamic-slice_fusion.1), calls=%async_computation.3 | async-start | bytes 589824 | tf_op jit(solution)/shard_map/all_to_all | solution.py:840
  483.9 96.0 %collective-permute-start.49 = (bf16[4,72,2432]{2,1,0:T(8,128)(2,1)}, bf16[4,72,2432]{2,1,0:T(8,128)(2,1)}, u32[]{:S(2)}, u32[]{:S(2)}) collective-permute-start(bf16[4,72,2432]{2,1,0:T(8,128)(2,1)} %pad_maximum_fusion.6), channel_id=1, source_target_pairs={{0,4},{2,6},{4,0},{6,2},{8,12},{10,14},{12,8},{14,10},{16,20},{18,... | collective-permute-start | bytes 4202504 | tf_op jit(solution)/shard_map/ppermute | solution.py:54
  492.4 87.4 %collective-permute-start.47 = (bf16[4,72,2432]{2,1,0:T(8,128)(2,1)}, bf16[4,72,2432]{2,1,0:T(8,128)(2,1)}, u32[]{:S(2)}, u32[]{:S(2)}) collective-permute-start(bf16[4,72,2432]{2,1,0:T(8,128)(2,1)} %pad_maximum_fusion.5), channel_id=1, source_target_pairs={{0,2},{2,0},{4,6},{6,4},{8,10},{10,8},{12,14},{14,12},{16,18},{18,... | collective-permute-start | bytes 4202504 | tf_op jit(solution)/shard_map/ppermute | solution.py:54
  514.3 47.7 %collective-permute-start.62 = (bf16[2,72,2304]{2,1,0:T(8,128)(2,1)}, bf16[2,72,2304]{2,1,0:T(8,128)(2,1)}, u32[]{:S(2)}, u32[]{:S(2)}) collective-permute-start(bf16[2,72,2304]{2,1,0:T(8,128)(2,1)} %fusion.9), channel_id=1, source_target_pairs={{0,16},{2,18},{4,20},{6,22},{8,24},{10,26},{12,28},{14,30},{16,0},... | collective-permute-start | bytes 1990664 | tf_op jit(solution)/shard_map/ppermute | solution.py:54
  583.8 43.9 %collective-permute-start.50 = (bf16[2,72,2432]{2,1,0:T(8,128)(2,1)}, bf16[2,72,2432]{2,1,0:T(8,128)(2,1)}, u32[]{:S(2)}, u32[]{:S(2)}) collective-permute-start(bf16[2,72,2432]{2,1,0:T(8,128)(2,1)} %fusion.3), channel_id=1, source_target_pairs={{0,16},{2,18},{4,20},{6,22},{8,24},{10,26},{12,28},{14,30},{16,0},... | collective-permute-start | bytes 2101256 | tf_op jit(solution)/shard_map/ppermute | solution.py:54
  587.1 66.2 %collective-permute-start.55 = (bf16[4,72,2304]{2,1,0:T(8,128)(2,1)}, bf16[4,72,2304]{2,1,0:T(8,128)(2,1)}, u32[]{:S(2)}, u32[]{:S(2)}) collective-permute-start(bf16[4,72,2304]{2,1,0:T(8,128)(2,1)} %pad_maximum_fusion.10), channel_id=1, source_target_pairs={{0,4},{2,6},{4,0},{6,2},{8,12},{10,14},{12,8},{14,10},{16,20},{18,... | collective-permute-start | bytes 3981320 | tf_op jit(solution)/shard_map/ppermute | solution.py:54
  590.4 62.8 %collective-permute-start.53 = (bf16[4,72,2304]{2,1,0:T(8,128)(2,1)}, bf16[4,72,2304]{2,1,0:T(8,128)(2,1)}, u32[]{:S(2)}, u32[]{:S(2)}) collective-permute-start(bf16[4,72,2304]{2,1,0:T(8,128)(2,1)} %pad_maximum_fusion.9), channel_id=1, source_target_pairs={{0,2},{2,0},{4,6},{6,4},{8,10},{10,8},{12,14},{14,12},{16,18},{18,... | collective-permute-start | bytes 3981320 | tf_op jit(solution)/shard_map/ppermute | solution.py:54
  647.6 58.5 %collective-permute-start.43 = (bf16[4,72,2432]{2,1,0:T(8,128)(2,1)}, bf16[4,72,2432]{2,1,0:T(8,128)(2,1)}, u32[]{:S(2)}, u32[]{:S(2)}) collective-permute-start(bf16[4,72,2432]{2,1,0:T(8,128)(2,1)} %pad_maximum_fusion.4), channel_id=1, source_target_pairs={{0,4},{2,6},{4,0},{6,2},{8,12},{10,14},{12,8},{14,10},{16,20},{18,... | collective-permute-start | bytes 4202504 | tf_op jit(solution)/shard_map/ppermute | solution.py:54
  651.7 54.4 %collective-permute-start.41 = (bf16[4,72,2432]{2,1,0:T(8,128)(2,1)}, bf16[4,72,2432]{2,1,0:T(8,128)(2,1)}, u32[]{:S(2)}, u32[]{:S(2)}) collective-permute-start(bf16[4,72,2432]{2,1,0:T(8,128)(2,1)} %pad_maximum_fusion.3), channel_id=1, source_target_pairs={{0,2},{2,0},{4,6},{6,4},{8,10},{10,8},{12,14},{14,12},{16,18},{18,... | collective-permute-start | bytes 4202504 | tf_op jit(solution)/shard_map/ppermute | solution.py:54
  656.5 37.4 %collective-permute-start.56 = (bf16[2,72,2304]{2,1,0:T(8,128)(2,1)}, bf16[2,72,2304]{2,1,0:T(8,128)(2,1)}, u32[]{:S(2)}, u32[]{:S(2)}) collective-permute-start(bf16[2,72,2304]{2,1,0:T(8,128)(2,1)} %fusion.8), channel_id=1, source_target_pairs={{0,16},{2,18},{4,20},{6,22},{8,24},{10,26},{12,28},{14,30},{16,0},... | collective-permute-start | bytes 1990664 | tf_op jit(solution)/shard_map/ppermute | solution.py:54
  (128 other events, 1433.3 us)

commit v3 on v2

--- a/solution.py
+++ b/solution.py
@@ -46,24 +46,20 @@
     )
 
 
-PLANE = 2
 PAIR = 2
 
 
-def swap_bit(values, bit, count):
-    return lax.ppermute(values, "dp", [(i, i ^ (1 << bit)) for i in range(count)])
+def swap_by(values, offset):
+    count = lax.axis_size("dp")
+    return lax.ppermute(values, "dp", [(i, i ^ offset) for i in range(count)])
 
 
 def my_bit(bit):
     return (lax.axis_index("dp") >> bit) & 1
 
 
-def after(value, *others):
-    return lax.optimization_barrier((value,) + others)[0]
-
-
-def outer_bits(count):
-    return range(PLANE, count.bit_length() - 1)
+def after(values, *others):
+    return lax.optimization_barrier((values,) + others)[0]
 
 
 def pick(first, mine, theirs, axis):
@@ -72,19 +68,35 @@
     )
 
 
-def gather_outer(shard, count):
+def place_scalars():
+    return jnp.stack(
+        [lax.axis_index("tensor"), lax.axis_index("dp") & 3, lax.axis_index("dp") >> 2]
+    ).astype(jnp.int32)
+
+
+def gather_pair(shard):
     paired = isinstance(shard, tuple)
-    rows, columns = shard[0].shape if paired else shard.shape
-    held = shard[0][None] if paired else shard[None]
-    for bit in outer_bits(count):
-        sent = shard[1][None] if bit == PAIR and paired else held
-        got = swap_bit(sent, bit, count)
-        held = pick(my_bit(bit) == 0, held, got, 0).reshape(-1, rows, columns)
+    own, sent = shard if paired else (shard, shard)
+    return jnp.stack([own, swap_by(sent, 1 << PAIR)])
+
+
+def gather_planes(held):
+    while held.shape[0] * 4 < lax.axis_size("dp"):
+        held = jnp.concatenate([held, swap_by(held, held.shape[0] * 4)])
     return held
 
 
-def arrange_kernel(me_ref, own_ref, across_ref, along_ref, low_ref, high_ref, out_ref):
-    me = me_ref[0]
+def gather_straight(shard):
+    paired = isinstance(shard, tuple)
+    parts = [shard[0] if paired else shard]
+    for relative in range(1, lax.axis_size("dp") // 4):
+        sent = shard[relative & 1] if paired else shard
+        parts.append(swap_by(sent, relative << 2))
+    return jnp.stack(parts)
+
+
+def arrange_kernel(place_ref, own_ref, across_ref, along_ref, low_ref, high_ref, out_ref):
+    me = place_ref[1]
     out_ref[me] = own_ref[0]
     out_ref[me ^ 1] = across_ref[0]
     out_ref[me ^ 2] = along_ref[0]
@@ -103,8 +115,7 @@
     groups, rows, columns = own.shape
     half = groups // 2
     block = (1, rows, columns)
-    whole = pl.BlockSpec(block, lambda i, me: (i, 0, 0))
-    me = jnp.reshape(lax.axis_index("dp") & 3, (1,)).astype(jnp.int32)
+    whole = pl.BlockSpec(block, lambda i, place: (i, 0, 0))
     out = pl.pallas_call(
         arrange_kernel,
         out_shape=jax.ShapeDtypeStruct((groups * 4, rows, columns), own.dtype),
@@ -115,47 +126,41 @@
                 whole,
                 whole,
                 whole,
-                pl.BlockSpec(block, lambda i, me: (jnp.minimum(i, half - 1), 0, 0)),
-                pl.BlockSpec(block, lambda i, me: (jnp.maximum(i - half, 0), 0, 0)),
+                pl.BlockSpec(block, lambda i, place: (jnp.minimum(i, half - 1), 0, 0)),
+                pl.BlockSpec(block, lambda i, place: (jnp.maximum(i - half, 0), 0, 0)),
             ],
-            out_specs=pl.BlockSpec((4, rows, columns), lambda i, me: (i, 0, 0)),
+            out_specs=pl.BlockSpec((4, rows, columns), lambda i, place: (i ^ place[2], 0, 0)),
         ),
         name="arrange",
-        cost_estimate=pl.CostEstimate(
-            flops=0, bytes_accessed=16 * groups * rows * columns, transcendentals=0
-        ),
-    )(me, own, across, along, low_part, high_part)
+        cost_estimate=cost(0, 16 * groups * rows * columns),
+    )(place_scalars(), own, across, along, low_part, high_part)
     return out.reshape(groups * 4 * rows, columns)
 
 
-def gather_all(shards, count):
-    full = []
-    last_outer = last_plane = None
-    for shard in shards:
-        if last_outer is not None:
-            shard = lax.optimization_barrier((shard, last_outer))[0]
-        own = gather_outer(shard, count)
-        last_outer = own
-        if last_plane is not None:
-            own = after(own, *last_plane)
-        across, along = swap_bit(own, 0, count), swap_bit(own, 1, count)
-        last_plane = (across, along)
-        half = own.shape[0] // 2
-        low_part = swap_bit(across[:half], 1, count)
-        high_part = swap_bit(along[half:], 0, count)
-        full.append(arrange(own, across, along, low_part, high_part))
-    return full
-
-
-def place_scalars():
-    return jnp.stack([lax.axis_index("tensor"), lax.axis_index("dp") & 3]).astype(jnp.int32)
+def gather_near(own):
+    return (own, swap_by(own, 1), swap_by(own, 2))
+
+
+def gather_halves(near):
+    half = near[0].shape[0] // 2
+    return (near[1][:half], near[2][half:])
+
+
+def gather_far(halves):
+    return (swap_by(halves[0], 2), swap_by(halves[1], 1))
+
+
+def together(*values):
+    return lax.optimization_barrier(values)
 
 
 def weight_grad_kernel(count, starts, place_ref, *refs):
     pairs = len(starts)
     operands, outs, total = refs[: 2 * pairs], refs[2 * pairs : -1], refs[-1]
-    me = place_ref[1]
-    rows = total.shape[0] // count
+    own, to_across, to_along, rest_across, rest_along = outs
+    me, plane = place_ref[1], place_ref[2]
+    rows, groups = total.shape[0] // count, count // 4
+    half = groups // 2
     for index, start in enumerate(starts):
         left, right = operands[2 * index], operands[2 * index + 1]
         total[:, start : start + right.shape[1]] = product_left(left[...], right[...])
@@ -163,25 +168,38 @@
         if spare:
             end = start + right.shape[1]
             total[:, end : end + spare] = jnp.zeros((total.shape[0], spare), wide)
-    for relative, out in enumerate(outs):
-        mate = me ^ relative
+
+    def copy(out, at, mate, first, length):
+        place = me ^ mate
         if rows % 8 == 0:
 
-            @pl.loop(0, count // 4)
-            def _(group, mate=mate, out=out):
-                first = pl.multiple_of((group * 4 + mate) * rows, 8)
-                out[group] = total[pl.ds(first, rows), :].astype(low)
+            @pl.loop(0, length)
+            def _(step):
+                chip = (plane ^ (first + step)) * 4 + place
+                out[at + step] = total[pl.ds(pl.multiple_of(chip * rows, 8), rows), :].astype(low)
+
         else:
-            for place in range(4):
-
-                @pl.when(mate == place)
-                def _(place=place, out=out):
-                    for group in range(count // 4):
-                        first = (group * 4 + place) * rows
-                        out[group] = total[first : first + rows, :].astype(low)
-
-
-def scatter_product(pairs, paired):
+
+            for chip in range(count):
+
+                @pl.when((chip & 3) == place)
+                def _(chip=chip):
+                    step = (plane ^ (chip >> 2)) - first
+
+                    @pl.when((step >= 0) & (step < length))
+                    def _():
+                        out[at + step] = total[chip * rows : (chip + 1) * rows, :].astype(low)
+
+    copy(to_along, 0, 3, 0, half)
+    copy(to_along, half, 2, 0, half)
+    copy(to_across, 0, 3, half, half)
+    copy(to_across, half, 1, half, half)
+    copy(rest_across, 0, 1, 0, half)
+    copy(rest_along, 0, 2, half, half)
+    copy(own, 0, 0, 0, groups)
+
+
+def weight_grad(pairs):
     count = lax.axis_size("dp")
     groups = count // 4
     half = groups // 2
@@ -192,39 +210,80 @@
         starts.append(columns)
         columns += padded(right.shape[1])
     tokens = pairs[0][0].shape[0]
-    own, across, along, far = pl.pallas_call(
+    own, to_across, to_along, rest_across, rest_along = pl.pallas_call(
         functools.partial(weight_grad_kernel, count, tuple(starts)),
-        out_shape=[jax.ShapeDtypeStruct((groups, rows, columns), low)] * 4,
+        out_shape=[
+            jax.ShapeDtypeStruct((blocks, rows, columns), low)
+            for blocks in (groups, groups, groups, half, half)
+        ],
         in_specs=[pl.BlockSpec(memory_space=pltpu.SMEM)]
         + [pl.BlockSpec(memory_space=pltpu.VMEM)] * (2 * len(pairs)),
         scratch_shapes=[pltpu.VMEM((width, columns), wide)],
         name="weight_grad",
-        cost_estimate=pl.CostEstimate(
-            flops=2 * tokens * width * columns,
-            bytes_accessed=2 * width * columns + 4 * tokens * (width + columns),
-            transcendentals=0,
+        cost_estimate=cost(
+            2 * tokens * width * columns, 2 * width * columns + 4 * tokens * (width + columns)
         ),
     )(place_scalars(), *[operand for pair in pairs for operand in pair])
-    low_part = swap_bit(far[:half], 1, count)
-    high_part = swap_bit(far[half:], 0, count)
-    across = jnp.concatenate(
-        [(across[:half].astype(wide) + low_part.astype(wide)).astype(low), across[half:]]
-    )
-    along = jnp.concatenate(
-        [along[:half], (along[half:].astype(wide) + high_part.astype(wide)).astype(low)]
-    )
-    got_across, got_along = swap_bit(across, 0, count), swap_bit(along, 1, count)
-    held = own.astype(wide) + got_across.astype(wide) + got_along.astype(wide)
-    for bit in reversed(outer_bits(count)):
-        split = held.reshape(2, -1, rows, columns)
-        side = my_bit(bit)
-        keep = lax.dynamic_index_in_dim(split, side, 0, keepdims=False)
-        send = lax.dynamic_index_in_dim(split, 1 - side, 0, keepdims=False)
-        got = swap_bit(send.astype(low), bit, count).astype(wide)
-        if bit == PAIR and paired:
-            return pick(side == 0, keep[0], got[0], 0)
-        held = keep + got
-    return held[0]
+    return (own, rest_across, rest_along, to_across, to_along)
+
+
+def scatter_start(parts):
+    own, rest_across, rest_along, to_across, to_along = parts
+    return (own, rest_across, rest_along, swap_by(to_across, 1), swap_by(to_along, 2))
+
+
+def scatter_near(state):
+    own, rest_across, rest_along, got_across, got_along = state
+    half = rest_across.shape[0]
+    rest_across = (rest_across.astype(wide) + got_along[:half].astype(wide)).astype(low)
+    rest_along = (rest_along.astype(wide) + got_across[:half].astype(wide)).astype(low)
+    return (own, got_across, got_along, swap_by(rest_across, 1), swap_by(rest_along, 2))
+
+
+def scatter_plane_blocks(state):
+    own, got_across, got_along, last_across, last_along = state
+    half = own.shape[0] // 2
+
+    def total(relative):
+        block = own[relative].astype(wide)
+        if relative < half:
+            return block + got_along[half + relative].astype(wide) + last_across[relative].astype(wide)
+        return block + got_across[relative].astype(wide) + last_along[relative - half].astype(wide)
+
+    return [total(relative) for relative in range(own.shape[0])]
+
+
+def scatter_planes(state):
+    blocks = scatter_plane_blocks(state)
+    got = [
+        swap_by(block.astype(low), relative << 2) for relative, block in enumerate(blocks) if relative
+    ]
+    return (blocks[0], got)
+
+
+def scatter_finish(state):
+    own, got = state
+    return own + sum(part.astype(wide) for part in got)
+
+
+def scatter_halve(blocks):
+    half = len(blocks) // 2
+    sent = jnp.stack([block.astype(low) for block in blocks[half:]])
+    return (blocks[:half], swap_by(sent, half * 4))
+
+
+def scatter_join(state, paired=False):
+    kept, got = state
+    if paired:
+        return pick(my_bit(PAIR) == 0, kept[0], got[0].astype(wide), 0)
+    return [block + got[index].astype(wide) for index, block in enumerate(kept)]
+
+
+def scatter_last(state):
+    blocks = scatter_join(state)
+    while len(blocks) > 2:
+        blocks = scatter_join(scatter_halve(blocks))
+    return scatter_halve(blocks)
 
 
 def swap_tensor(values):
@@ -241,21 +300,19 @@
     )
 
 
-def rows_half(values, axis):
-    half = values.shape[axis] // 2
-    return values.reshape(values.shape[:axis] + (2, half) + values.shape[axis + 1 :])
-
-
 def pair_rows(values):
-    tensor = lax.axis_index("tensor")
-    half = lax.dynamic_index_in_dim(rows_half(values, 0), tensor, 0, keepdims=False)
-    got = swap_bit(half, PAIR, lax.axis_size("dp"))
+    half = values.shape[0] // 2
+    sent = lax.dynamic_slice_in_dim(values, lax.axis_index("tensor") * half, half, 0)
+    got = swap_by(sent, 1 << PAIR)
     return jnp.concatenate([values, lax.all_gather(got, "tensor", axis=0, tiled=True)])
 
 
-def pair_sum(keep, send):
-    chip = keep.astype(wide) + swap_tensor(send).astype(wide)
-    got = swap_bit(chip[1].astype(low), PAIR, lax.axis_size("dp"))
+def chip_sum(keep, send):
+    return keep.astype(wide) + swap_tensor(send).astype(wide)
+
+
+def pair_sum(chip):
+    got = swap_by(chip[1].astype(low), 1 << PAIR)
     total = (chip[0] + got.astype(wide)).astype(low)
     return lax.all_gather(total, "tensor", axis=0, tiled=True)
 
@@ -291,9 +348,14 @@
     return pl.BlockSpec((rows,) + rest, lambda i, *_: (i,) + (0,) * len(rest))
 
 
+COST_SHARE = 16
+
+
 def cost(flops, bytes_accessed, transcendentals=0):
     return pl.CostEstimate(
-        flops=flops, bytes_accessed=bytes_accessed, transcendentals=transcendentals
+        flops=flops // COST_SHARE,
+        bytes_accessed=bytes_accessed // COST_SHARE,
+        transcendentals=transcendentals // COST_SHARE,
     )
 
 
@@ -391,7 +453,9 @@
     root = 0.7978845608028654
     square = values * values
     bend = jnp.tanh(root * (values + 0.044715 * values * square))
-    return (bend, root * (1.0 + 3.0 * 0.044715 * square))
+    share = 0.5 * (1.0 + bend)
+    steep = 0.5 * root * (1.0 - bend * bend) * (1.0 + 3.0 * 0.044715 * square)
+    return (values * share, share + values * steep)
 
 
 def units_kernel(
@@ -400,16 +464,16 @@
     up_ref,
     down_ref,
     bias_ref,
-    inner_ref,
+    slope_ref,
     active_ref,
     keep_ref,
     send_ref,
     partial_ref,
 ):
     inner = product(hidden_ref[...], up_ref[...]) + bias_ref[...]
-    inner_ref[...] = inner
-    bend, _ = gelu_parts(inner)
-    active = (0.5 * inner * (1.0 + bend)).astype(low)
+    active, slope = gelu_parts(inner)
+    slope_ref[...] = slope.astype(low)
+    active = active.astype(low)
     active_ref[...] = active
     partial_ref[...] = product_right(active, down_ref[...])
     split_halves(place_ref, partial_ref, keep_ref, send_ref)
@@ -420,17 +484,14 @@
     upstream_ref,
     up_ref,
     down_ref,
-    inner_ref,
+    slope_ref,
     grad_ref,
     keep_ref,
     send_ref,
     bias_ref,
     partial_ref,
 ):
-    inner = inner_ref[...]
-    bend, slope = gelu_parts(inner)
-    derivative = 0.5 * (1.0 + bend) + 0.5 * inner * (1.0 - bend * bend) * slope
-    grad = (product(upstream_ref[...], down_ref[...]) * derivative).astype(low)
+    grad = (product(upstream_ref[...], down_ref[...]) * slope_ref[...].astype(wide)).astype(low)
     grad_ref[...] = grad
 
     @pl.when(pl.program_id(0) == 0)
@@ -447,13 +508,15 @@
     out_ref[...] = (middle_ref[...] + mod_ref[0, 5:6] * branch).astype(low)
 
 
-def turn_kernel(upstream_ref, branch_ref, bias_ref, mod_ref, grad_ref, sums_ref):
-    upstream = upstream_ref[...].astype(wide)
+def turn_kernel(upstream_ref, mod_ref, grad_ref, sums_ref):
+    grad = (upstream_ref[...].astype(wide) * mod_ref[0, 5:6]).astype(low)
+    grad_ref[...] = grad
+    sums_ref[0, 0:1] = column_sum(grad.astype(wide))
+
+
+def gate_kernel(upstream_ref, branch_ref, bias_ref, mod_ref, sums_ref):
     branch = branch_ref[...].astype(wide) + bias_ref[...]
-    grad = (upstream * mod_ref[0, 5:6]).astype(low)
-    grad_ref[...] = grad
-    sums_ref[0, 0:1] = column_sum(upstream * branch)
-    sums_ref[0, 1:2] = column_sum(grad.astype(wide))
+    sums_ref[0, 0:1] = column_sum(upstream_ref[...].astype(wide) * branch)
 
 
 def middle_back_kernel(
@@ -563,9 +626,9 @@
     )(*row_inputs, *fixed_inputs, mods)
 
 
-def units_call(body, rows_in, up, down, extra, extra_spec, outs, out_specs, name):
+def units_call(body, rows_in, updown, extra, extra_spec, outs, out_specs, name):
     rows, width = rows_in.shape
-    units = up.shape[1]
+    units = updown.shape[1] // 2
     half = rows // 2
     halves = array(low, 2, half // 2, width)
     at = pl.BlockSpec((1, half // 2, width), lambda i, *_: (i, 0, 0))
@@ -576,8 +639,8 @@
             grid=(2,),
             in_specs=[
                 by_rows(half, width),
-                fixed(width, units),
-                fixed(width, units),
+                pl.BlockSpec((width, units), lambda i, *_: (0, 0)),
+                pl.BlockSpec((width, units), lambda i, *_: (0, 1)),
                 extra_spec,
             ],
             out_specs=out_specs[: len(outs) - 1] + [at, at] + out_specs[len(outs) - 1 :]
@@ -594,34 +657,32 @@
             4 * width * units + 4 * rows * width + 6 * rows * units,
             rows * units,
         ),
-    )(place_scalars(), rows_in, up, down, extra)
-
-
-def units_forward(hidden, up, down, bias):
-    rows, units = hidden.shape[0], up.shape[1]
+    )(place_scalars(), rows_in, updown, updown, extra)
+
+
+def units_forward(hidden, updown, bias):
+    rows, units = hidden.shape[0], updown.shape[1] // 2
     block = by_rows(rows // 2, units)
     return units_call(
         units_kernel,
         hidden,
-        up,
-        down,
+        updown,
         bias,
         fixed(1, units),
-        [array(wide, rows, units), array(low, rows, units)],
+        [array(low, rows, units), array(low, rows, units)],
         [block, block],
         "units",
     )
 
 
-def units_backward(upstream, up, down, inner):
-    rows, units = inner.shape
+def units_backward(upstream, updown, slope):
+    rows, units = slope.shape
     block = by_rows(rows // 2, units)
     return units_call(
         units_back_kernel,
         upstream,
-        up,
-        down,
-        inner,
+        updown,
+        slope,
         block,
         [array(low, rows, units), array(wide, 1, units)],
         [block, fixed(1, units)],
@@ -629,79 +690,62 @@
     )
 
 
-def block_forward(x, mods, weights, biases, place_count):
-    wattn, up, down = weights
-    bias_joined, bias_out, bias_fc2, bias_fc1 = biases
-    groups = mods.shape[0]
-    hidden_attn, joined, attended, mine = attention_forward(
-        x, mods, wattn, bias_joined, place_count
-    )
-    theirs = swap_tensor(mine)
+def first_half(x, mods, wattn, biases, place_count):
+    hidden, joined, attended, mine = attention_forward(x, mods, wattn, biases[0], place_count)
+    both = (mine, swap_tensor(mine))
     middle, hidden_mlp = row_kernel(
-        middle_kernel, groups, (x, mine, theirs), (bias_out,), mods, (wide, low), 0, "middle"
-    )
-    flat_mlp = pair_rows(hidden_mlp)
-    inner, active, keep, send = units_forward(flat_mlp, up, down, bias_fc1)
-    branch_mlp = pair_sum(keep, send)
-    (result,) = row_kernel(
-        result_kernel, groups, (middle, branch_mlp), (bias_fc2,), mods, (low,), 0, "result"
-    )
-    saved = (
-        x,
-        hidden_attn,
-        joined,
-        attended,
-        mine,
-        theirs,
-        middle,
-        flat_mlp,
-        inner,
-        active,
-        branch_mlp,
-    )
-    return (result, saved)
-
-
-def block_backward(upstream, saved, mods, weights, biases, place_count, grad_dtype):
-    x, hidden_attn, joined, attended, mine, theirs, middle, flat_mlp, inner, active, branch = saved
-    wattn, up, down = weights
-    _, bias_out, bias_fc2, _ = biases
-    groups, width = mods.shape[0], x.shape[1]
-    part_width = width // 2
-    mlp_grad, turn_sums = row_kernel(
-        turn_kernel, groups, (upstream, branch), (bias_fc2,), mods, (low,), 1, "turn"
-    )
-    flat_grad = pair_rows(mlp_grad)
-    inner_grad, keep, send, fc1_bias = units_backward(flat_grad, up, down, inner)
-    units_reduced = scatter_product([(flat_mlp, inner_grad), (flat_grad, active)], True)
-    hidden_grad = pair_sum(keep, send)
-    middle_grad, attn_grad, middle_sums = row_kernel(
+        middle_kernel, mods.shape[0], (x, *both), (biases[1],), mods, (wide, low), 0, "middle"
+    )
+    return (hidden, joined, attended, both, middle, hidden_mlp)
+
+
+def block_result(middle, branch, biases, mods):
+    return row_kernel(
+        result_kernel, mods.shape[0], (middle, branch), (biases[2],), mods, (low,), 0, "result"
+    )[0]
+
+
+def turn(upstream, mods):
+    return row_kernel(turn_kernel, mods.shape[0], (upstream,), (), mods, (low,), 1, "turn")
+
+
+def gate_sums(upstream, branch, biases, mods):
+    return row_kernel(
+        gate_kernel, mods.shape[0], (upstream, branch), (biases[2],), mods, (), 1, "gate"
+    )[0]
+
+
+def middle_back(upstream, hidden_grad, middle, both, biases, mods):
+    return row_kernel(
         middle_back_kernel,
-        groups,
-        (upstream, hidden_grad, middle, mine, theirs),
-        (bias_out,),
+        mods.shape[0],
+        (upstream, hidden_grad, middle, *both),
+        (biases[1],),
         mods,
         (wide, low),
         1,
         "middle_back",
     )
-    joined_grad, mine_grad, joined_bias = attention_backward(
-        attn_grad, wattn, joined, groups, place_count
-    )
-    attn_reduced = scatter_product([(hidden_attn, joined_grad), (attn_grad, attended)], False)
-    theirs_grad = swap_tensor(mine_grad)
-    input_grad, input_sums = row_kernel(
+
+
+def input_back(middle_grad, mine_grad, x, mods, grad_dtype):
+    return row_kernel(
         input_back_kernel,
-        groups,
-        (middle_grad, mine_grad, theirs_grad, x),
+        mods.shape[0],
+        (middle_grad, mine_grad, swap_tensor(mine_grad), x),
         (),
         mods,
         (grad_dtype,),
         1,
         "input_back",
     )
+
+
+def small_grads(input_sums, middle_sums, gate, turn_sums, joined_bias, fc1_bias):
+    width = gate.shape[2]
+    part_width, units = width // 2, fc1_bias.shape[1]
     mod_grad = 0.5 * jnp.concatenate(
-        [input_sums[:, :2], middle_sums[:, 2:3], middle_sums[:, :2], turn_sums[:, :1]], axis=1
+        [input_sums[:, :2], middle_sums[:, 2:3], middle_sums[:, :2], gate[:, :1]], axis=1
     )
     joined_bias = jnp.sum(joined_bias, axis=(0, 1))
     at = lax.axis_index("tensor") * part_width
@@ -710,12 +754,10 @@
             widen(joined_bias[:part_width], at, width),
             widen(joined_bias[2 * part_width : 3 * part_width], at, width),
             0.5 * jnp.sum(middle_sums[:, 3], axis=0),
-            0.5 * jnp.sum(turn_sums[:, 1], axis=0),
+            0.5 * jnp.sum(turn_sums[:, 0], axis=0),
         ]
     )
-    units = fc1_bias.shape[1]
-    hidden_bias = widen(fc1_bias[0], unit_start(units), units * 4)
-    return (input_grad, mod_grad, (attn_reduced, units_reduced), proj_grad, hidden_bias)
+    return (mod_grad, proj_grad, widen(fc1_bias[0], unit_start(units), units * 4))
 
 
 def widen(local_part, offset, total):
@@ -767,11 +809,18 @@
             )
         )
         shards.append((units_part(layer, my_bit(PAIR)), units_part(layer, 1 - my_bit(PAIR))))
-    full = gather_all(shards, dp_count)
-    gathered = [
-        (full[2 * layer], full[2 * layer + 1][:, :units], full[2 * layer + 1][:, units:])
-        for layer in range(2)
-    ]
+    own_attn_0 = gather_straight(shards[0])
+    near_attn_0 = gather_near(own_attn_0)
+    own_units_0 = gather_straight(after(shards[1], own_attn_0))
+    near_units_0 = gather_near(own_units_0)
+    far_attn_0 = gather_far(gather_halves(near_attn_0))
+    own_attn_1 = gather_planes(gather_pair(after(shards[2], own_units_0)))
+    near_attn_1 = gather_near(after(own_attn_1, near_attn_0))
+    own_units_1 = gather_planes(gather_pair(after(shards[3], own_attn_1)))
+    near_units_1 = gather_near(after(own_units_1, near_units_0))
+    far_units_0 = gather_far(gather_halves(near_units_0))
+    far_attn_1 = gather_far(gather_halves(near_attn_1))
+    far_units_1 = gather_far(gather_halves(near_units_1))
 
     cond_float = cond.astype(wide)
     gated_low = jax.nn.silu(cond_float).astype(low)
@@ -823,45 +872,124 @@
         return lax.dynamic_slice_in_dim(split, tensor, 1, 1)
 
     all_frames, own_place_count = frames_dev * dp_count, 2 * (place_half // dp_count)
-    first_x = flat(tokens)
-    first_biases, second_biases = layer_biases(0), layer_biases(1)
-    first_out, first_saved = block_forward(first_x, first_mod, gathered[0], first_biases, None)
-    arrived = lax.all_to_all(
-        own_places(first_out, frames_dev), "dp", split_axis=2, concat_axis=0, tiled=True
-    )
-    second_out, second_saved = block_forward(
-        flat(arrived), second_mod, gathered[1], second_biases, own_place_count
-    )
-    output = own_places(second_out, all_frames)
-
-    second_grad, second_dmod, second_reduced, second_proj, second_hidden = block_backward(
-        flat(out_grad), second_saved, second_mod, gathered[1], second_biases, own_place_count, low
-    )
-    arrived_back = lax.all_to_all(
-        own_places(second_grad, all_frames), "dp", split_axis=0, concat_axis=2, tiled=True
-    )
-    first_grad, first_dmod, first_reduced, first_proj, first_hidden = block_backward(
-        flat(arrived_back), first_saved, first_mod, gathered[0], first_biases, None, wide
-    )
-    tokens_grad = own_places(first_grad, frames_dev)
-
-    dmod_clips = jnp.stack(
-        [jnp.sum(onehot[:, :, None, None] * first_dmod[:, None], axis=0), second_dmod]
-    )
+    mods_0, mods_1 = first_mod, second_mod
+    biases_0, biases_1 = layer_biases(0), layer_biases(1)
+
+    upstream_1 = flat(out_grad)
+    mlp_grad_1, turn_sums_1 = turn(upstream_1, mods_1)
+    flat_grad_1 = pair_rows(mlp_grad_1)
+
+    wattn_0 = arrange(*after((*near_attn_0, *far_attn_0), own_attn_1))
+    x_0 = flat(tokens)
+    hidden_0, joined_0, attended_0, both_0, middle_0, hidden_mlp = first_half(
+        x_0, mods_0, wattn_0, biases_0, None
+    )
+    flat_0 = pair_rows(hidden_mlp)
+    units_0 = arrange(*near_units_0, *far_units_0)
+    slope_0, active_0, keep, send = units_forward(
+        after(flat_0, near_attn_1, flat_grad_1), units_0, biases_0[3]
+    )
+    branch_0 = pair_sum(chip_sum(keep, send))
+    result_0 = own_places(
+        block_result(after(middle_0, near_units_1), branch_0, biases_0, mods_0), frames_dev
+    )
+    x_1 = flat(lax.all_to_all(result_0, "dp", split_axis=2, concat_axis=0, tiled=True))
+
+    wattn_1 = arrange(*near_attn_1, *far_attn_1)
+    hidden_1, joined_1, attended_1, both_1, middle_1, hidden_mlp = first_half(
+        x_1, mods_1, wattn_1, biases_1, own_place_count
+    )
+    flat_1 = pair_rows(hidden_mlp)
+    units_1 = arrange(*near_units_1, *far_units_1)
+    slope_1, active_1, keep_1, send_1 = units_forward(flat_1, units_1, biases_1[3])
+
+    inner_grad_1, keep, send, fc1_bias_1 = units_backward(flat_grad_1, units_1, slope_1)
+    chip = chip_sum(keep, send)
+    hidden_grad = pair_sum(chip)
+    sums_units_1 = scatter_start(
+        weight_grad(after(((flat_1, inner_grad_1), (flat_grad_1, active_1)), chip))
+    )
+    middle_grad, attn_grad, middle_sums_1 = middle_back(
+        upstream_1, hidden_grad, middle_1, both_1, biases_1, mods_1
+    )
+    joined_grad, mine_grad, joined_bias_1 = attention_backward(
+        attn_grad, wattn_1, joined_1, mods_1.shape[0], own_place_count
+    )
+    x_grad_1, input_sums_1 = input_back(middle_grad, mine_grad, x_1, mods_1, low)
+    sent_back = own_places(x_grad_1, all_frames)
+    arrived_back = lax.all_to_all(sent_back, "dp", split_axis=0, concat_axis=2, tiled=True)
+    sums_attn_1 = scatter_start(
+        weight_grad(after(((hidden_1, joined_grad), (attn_grad, attended_1)), sent_back))
+    )
+    sums_units_1 = scatter_near(after(sums_units_1, sums_attn_1[0]))
+
+    branch_1 = pair_sum(chip_sum(*after((keep_1, send_1), attn_grad)))
+    output = own_places(block_result(middle_1, branch_1, biases_1, mods_1), all_frames)
+    gate_1 = gate_sums(upstream_1, branch_1, biases_1, mods_1)
+
+    upstream_0 = flat(arrived_back)
+    mlp_grad_0, turn_sums_0 = turn(upstream_0, mods_0)
+    flat_grad_0 = pair_rows(mlp_grad_0)
+    inner_grad_0, keep, send, fc1_bias_0 = units_backward(flat_grad_0, units_0, slope_0)
+    chip = chip_sum(keep, send)
+    hidden_grad = pair_sum(chip)
+    sums_units_1, sums_attn_1, chip = together(sums_units_1, sums_attn_1, chip)
+    sums_attn_1 = scatter_near(sums_attn_1)
+    units_blocks = scatter_plane_blocks(sums_units_1)
+    inner_grad_0 = after(inner_grad_0, chip, units_blocks)
+    sums_units_1 = scatter_halve(units_blocks)
+    sums_units_0 = scatter_start(weight_grad(((flat_0, inner_grad_0), (flat_grad_0, active_0))))
+    middle_grad, attn_grad, middle_sums_0 = middle_back(
+        upstream_0, hidden_grad, middle_0, both_0, biases_0, mods_0
+    )
+    sums_attn_1, sums_units_1, attn_grad = together(sums_attn_1, sums_units_1, attn_grad)
+    sums_attn_1 = scatter_halve(scatter_plane_blocks(sums_attn_1))
+    sums_units_1 = scatter_last(sums_units_1)
+    joined_grad, mine_grad, joined_bias_0 = attention_backward(
+        attn_grad, wattn_0, joined_0, mods_0.shape[0], None
+    )
+    sums_units_0, joined_grad = together(sums_units_0, joined_grad)
+    sums_units_0 = scatter_near(sums_units_0)
+    sums_attn_0 = scatter_start(weight_grad(((hidden_0, joined_grad), (attn_grad, attended_0))))
+    x_grad_0, input_sums_0 = input_back(middle_grad, mine_grad, x_0, mods_0, wide)
+    tokens_grad = own_places(x_grad_0, frames_dev)
+    gate_0 = gate_sums(upstream_0, branch_0, biases_0, mods_0)
+    sums_units_0, sums_attn_1, sums_units_1, input_sums_0, gate_0 = together(
+        sums_units_0, sums_attn_1, sums_units_1, input_sums_0, gate_0
+    )
+    units_blocks = scatter_plane_blocks(sums_units_0)
+    sums_units_0 = scatter_halve(units_blocks)
+    sums_attn_1 = scatter_last(sums_attn_1)
+    second_units = scatter_join(sums_units_1, True)
+    mod_0, proj_0, hidden_bias_0 = small_grads(
+        input_sums_0, middle_sums_0, gate_0, turn_sums_0, joined_bias_0, fc1_bias_0
+    )
+    mod_1, proj_1, hidden_bias_1 = small_grads(
+        input_sums_1, middle_sums_1, gate_1, turn_sums_1, joined_bias_1, fc1_bias_1
+    )
+    clips_0 = jnp.sum(onehot[:, :, None, None] * mod_0[:, None], axis=0)
     small = (
-        dmod_clips,
-        jnp.stack([first_proj, second_proj]),
-        jnp.stack([first_hidden, second_hidden]),
-    )
-    owned = jnp.sum(
-        deal(jnp.concatenate([sum_to_owner(piece, all_devices) for piece in small], axis=1)), axis=0
-    )
+        jnp.stack([clips_0, mod_1]),
+        jnp.stack([proj_0, proj_1]),
+        jnp.stack([hidden_bias_0, hidden_bias_1]),
+    )
+    dealt = jnp.concatenate([sum_to_owner(piece, all_devices) for piece in small], axis=1)
+    owned = jnp.sum(deal(dealt), axis=0)
+    sums_attn_0 = scatter_near(after(sums_attn_0, units_blocks, owned))
     own_dmod = owned[:first_end]
     b_proj_grad = owned[first_end:second_end].reshape(2, 4, own_width)
     b_fc1_grad = owned[second_end:].reshape(2, -1)
     summed_mod = from_owners(
         deal(jnp.broadcast_to(own_dmod[None], (all_devices, own_dmod.shape[0]))), (2, clip_count, 6)
     )
+    sums_units_0, sums_attn_1, sums_attn_0, summed_mod = together(
+        sums_units_0, sums_attn_1, sums_attn_0, summed_mod
+    )
+    second_attn = scatter_join(sums_attn_1)[0]
+    sums_attn_0 = scatter_planes(sums_attn_0)
+    sums_units_0 = scatter_last(sums_units_0)
+    first_units = scatter_join(sums_units_0, True)
+    first_attn = scatter_finish(sums_attn_0)
     w_ada_grad = sum(
         gated_own[clip][None, :, None, None] * summed_mod[:, clip][:, None]
         for clip in range(clip_count)
@@ -876,7 +1004,7 @@
     cond_own = lax.dynamic_slice_in_dim(cond_float, own_start, own_width, 1)
     cond_grad = jax.vjp(jax.nn.silu, cond_own)[1](silu_grad)[0]
 
-    reduced = (first_reduced, second_reduced)
+    reduced = ((first_attn, first_units), (second_attn, second_units))
     out_start = padded(joined_width)
     w_qkv_grad = jnp.stack(
         [part[0][:, :joined_width].reshape(own_rows, 3, head_width) for part in reduced]

time: 762 us -> 678 us (0.89)
  waiting for transfers between devices: 293 us -> 214 us
  local copies, waits for them, and re-layouts: 105 us -> 76.9 us
  Pallas kernels: 158 us -> 166 us
    ppermute x56 -> x59, waiting for transfers between devices: 263 us -> 172 us  [swap_by(): return lax.ppermute(values, 'dp', [(i, i ^ offset) for i in range(count)])]
    slice x26 -> x14, local copies, waits for them, and re-layouts: 34.5 us -> 15.6 us  [the longest x8 11.7 us: gather_halves(): return (near[1][:half], near[2][half:])]
    convert_element_type x8 -> x12, other arithmetic: 8.16 us -> 26.4 us  [the longest x4 8.48 us: scatter_near(): (rest_across.astype(wide) + got_along[:half].astype(wide)).astype(low)]
    all_to_all x4, waiting for transfers between devices: 18.8 us -> 35.7 us  [deal(): lax.all_to_all(values, everyone, split_axis=0, concat_axis=0, tiled=True)]
    another operation x2 -> x13, other arithmetic: 0.64 us -> 13.4 us  [the longest x6 7 us: scatter_halve(): sent = jnp.stack([block.astype(low) for block in blocks[half:]])]
    add x12 -> x6, other arithmetic: 16.1 us -> 6.55 us  [the longest x4 3.74 us: chip_sum(): return keep.astype(wide) + swap_tensor(send).astype(wide)]
    unnamed x176 -> x136, local copies, waits for them, and re-layouts: 17.1 us -> 11.8 us
    pallas_call x10 -> x12, Pallas kernels: 32.1 us -> 36.3 us  [row_kernel(): pl.pallas_call(body, grid=(groups,), in_specs=[by_rows(block, width) for...]
  transfers between devices with their start and end apart: 70 -> 73, of which waited for: 30 -> 22; matrix products, arithmetic and copies ran while one was open for 19% -> 20% of each run, Pallas kernels for 17% -> 20%
where the time goes in v3:
time: 678 us; the launch traced here: 666 us
  waiting for transfers between devices  214 us (32%)
  Pallas kernels  166 us (24%)
  starting transfers between devices  98.8 us (15%)
  local copies, waits for them, and re-layouts  76.9 us (11%)
  other arithmetic  76.1 us (11%)
  blocking collectives  31.6 us (5%)
    ppermute x59, waiting for transfers between devices, swap_by(): return lax.ppermute(values, 'dp', [(i, i ^ offset) for i in range(count)])  172 us
    ppermute x59, starting transfers between devices, swap_by(): return lax.ppermute(values, 'dp', [(i, i ^ offset) for i in range(count)])  73.6 us
    pallas_call x12, Pallas kernels, row_kernel(): pl.pallas_call(body, grid=(groups,), in_specs=[by_rows(block, width) for...  36.3 us
    all_to_all x4, waiting for transfers between devices, deal(): lax.all_to_all(values, everyone, split_axis=0, concat_axis=0, tiled=True)  35.7 us
    pallas_call x4, Pallas kernels, units_call(): pl.pallas_call(body, grid_spec=pltpu.PrefetchScalarGridSpec(num_scalar_pr...  35.7 us
    pallas_call x4, Pallas kernels, weight_grad(): pl.pallas_call(functools.partial(weight_grad_kernel, count, tuple(starts)...  30.6 us
    pallas_call x4, Pallas kernels, arrange(): pl.pallas_call(arrange_kernel, out_shape=jax.ShapeDtypeStruct((groups * 4...  24.1 us
    pallas_call x2, Pallas kernels, attention_backward(): pl.pallas_call(functools.partial(attention_back_kernel, place_count), gri...  22.1 us
  transfers between devices with their start and end apart: 73, of which 22 were waited for; matrix products, arithmetic and copies ran while one was open for 20% of the time, Pallas kernels for 20%

profile of v3, /device:TPU:0, one launch (start us, length us, event | category | flops | bytes accessed | tf_op | source)
XLA Modules:
  0.0 666.1 jit_solution(17831350164300179809)
XLA Ops:
  30.0 9.3 %collective-permute-done.1 = bf16[72,2432]{1,0:T(8,128)(2,1)} collective-permute-done((bf16[72,2432]{1,0:T(8,128)(2,1)S(1)}, bf16[72,2432]{1,0:T(8,128)(2,1)}, u32[]{:S(2)}, u32[]{:S(2)}) %collective-permute-start.1) | collective-permute-done | bytes 350240 | tf_op jit(solution)/shard_map/ppermute | solution.py:54
  53.4 16.2 %collective-permute-done.8 = bf16[72,2304]{1,0:T(8,128)(2,1)} collective-permute-done((bf16[72,2304]{1,0:T(8,128)(2,1)S(1)}, bf16[72,2304]{1,0:T(8,128)(2,1)}, u32[]{:S(2)}, u32[]{:S(2)}) %collective-permute-start.8) | collective-permute-done | bytes 331808 | tf_op jit(solution)/shard_map/ppermute | solution.py:54
  106.4 14.1 %collective-permute-done.11 = bf16[2,72,2432]{2,1,0:T(8,128)(2,1)} collective-permute-done((bf16[2,72,2432]{2,1,0:T(8,128)(2,1)}, bf16[2,72,2432]{2,1,0:T(8,128)(2,1)}, u32[]{:S(2)}, u32[]{:S(2)}) %collective-permute-start.11) | collective-permute-done | bytes 700448 | tf_op jit(solution)/shard_map/ppermute | solution.py:54
  129.1 8.4 %attention.2 = (bf16[256,1152]{1,0:T(8,128)(2,1)}, bf16[256,1792]{1,0:T(8,128)(2,1)}, bf16[256,576]{1,0:T(8,128)(2,1)}, bf16[256,1152]{1,0:T(8,128)(2,1)}) custom-call(bf16[256,1152]{1,0:T(8,128)(2,1)} %bitcast.276, f32[1,6,1152]{2,1,0:T(8,128)} %mul.253.mod_ref, bf16[1152,2432]{1,0:T(8,128)(2,1)} %bitcast.272, f32[1,1792]{1,0:T(1,128)} %broadcast_in_dim.13.bias_ref), custom_call_target="tpu_custom_call" | custom-call | flops 96731136 | bytes 536576 | tf_op jit(solution)/shard_map/attention/pallas_call | solution.py:568
  140.5 6.6 collective-permute-done.22
  164.9 32.9 %collective-permute-done.23.low_ref = bf16[2,72,2304]{2,1,0:T(8,128)(2,1)} collective-permute-done((bf16[2,72,2304]{2,1,0:T(8,128)(2,1)}, bf16[2,72,2304]{2,1,0:T(8,128)(2,1)}, u32[]{:S(2)}, u32[]{:S(2)}) %collective-permute-start.23) | collective-permute-done | bytes 663584 | tf_op jit(solution)/shard_map/ppermute | solution.py:54
  208.9 8.7 %units.2 = (bf16[512,1152]{1,0:T(8,128)(2,1)}, bf16[512,1152]{1,0:T(8,128)(2,1)}, bf16[2,128,1152]{2,1,0:T(8,128)(2,1)}, bf16[2,128,1152]{2,1,0:T(8,128)(2,1)}) custom-call(s32[3]{0:T(128)} %pad_add_fusion.place_ref, bf16[512,1152]{1,0:T(8,128)(2,1)} %copy-done.2, bf16[1152,2304]{1,0:T(8,128)(2,1)} %bitcast.264, bf16[1152,2304]{1,0:T(8,128)(2,1)} %bitcast.265, ...), custom_call_target="tpu_custom_call" | custom-call | flops 169869312 | bytes 700416 | tf_op jit(solution)/shard_map/units/pallas_call | solution.py:635
  217.8 10.9 %collective-permute-done.14 = bf16[2,72,2304]{2,1,0:T(8,128)(2,1)S(1)} collective-permute-done((bf16[2,72,2304]{2,1,0:T(8,128)(2,1)}, bf16[2,72,2304]{2,1,0:T(8,128)(2,1)S(1)}, u32[]{:S(2)}, u32[]{:S(2)}) %collective-permute-start.14) | collective-permute-done | bytes 663584 | tf_op jit(solution)/shard_map/ppermute | solution.py:54
  236.4 24.6 %collective-permute-done.17.across_ref = bf16[4,72,2304]{2,1,0:T(8,128)(2,1)} collective-permute-done((bf16[4,72,2304]{2,1,0:T(8,128)(2,1)S(1)}, bf16[4,72,2304]{2,1,0:T(8,128)(2,1)}, u32[]{:S(2)}, u32[]{:S(2)}) %collective-permute-start.17) | collective-permute-done | bytes 1327136 | tf_op jit(solution)/shard_map/ppermute | solution.py:54
  291.1 8.4 %attention.3 = (bf16[256,1152]{1,0:T(8,128)(2,1)}, bf16[256,1792]{1,0:T(8,128)(2,1)}, bf16[256,576]{1,0:T(8,128)(2,1)}, bf16[256,1152]{1,0:T(8,128)(2,1)}) custom-call(bf16[256,1152]{1,0:T(8,128)(2,1)} %bitcast.279, f32[1,6,1152]{2,1,0:T(8,128)} %squeeze.51.mod_ref, bf16[1152,2432]{1,0:T(8,128)(2,1)} %bitcast.274, f32[1,1792]{1,0:T(1,128)} %broadcast_in_dim.15.bias_ref), custom_call_target="tpu_custom_call" | custom-call | flops 96731136 | bytes 536576 | tf_op jit(solution)/shard_map/attention/pallas_call | solution.py:568
  310.6 7.5 %collective-permute-done.31.low_ref = bf16[2,72,2304]{2,1,0:T(8,128)(2,1)} collective-permute-done((bf16[2,72,2304]{2,1,0:T(8,128)(2,1)S(1)}, bf16[2,72,2304]{2,1,0:T(8,128)(2,1)}, u32[]{:S(2)}, u32[]{:S(2)}) %collective-permute-start.31) | collective-permute-done | bytes 663584 | tf_op jit(solution)/shard_map/ppermute | solution.py:54
  329.2 8.7 %units.3 = (bf16[512,1152]{1,0:T(8,128)(2,1)}, bf16[512,1152]{1,0:T(8,128)(2,1)}, bf16[2,128,1152]{2,1,0:T(8,128)(2,1)}, bf16[2,128,1152]{2,1,0:T(8,128)(2,1)}) custom-call(s32[3]{0:T(128)} %pad_add_fusion.place_ref, bf16[512,1152]{1,0:T(8,128)(2,1)} %copy-done.3, bf16[1152,2304]{1,0:T(8,128)(2,1)} %bitcast.268, bf16[1152,2304]{1,0:T(8,128)(2,1)} %bitcast.269, ...), custom_call_target="tpu_custom_call" | custom-call | flops 169869312 | bytes 700416 | tf_op jit(solution)/shard_map/units/pallas_call | solution.py:635
  337.9 9.1 %units_back.2 = (bf16[512,1152]{1,0:T(8,128)(2,1)}, bf16[2,128,1152]{2,1,0:T(8,128)(2,1)}, bf16[2,128,1152]{2,1,0:T(8,128)(2,1)}, f32[1,1152]{1,0:T(1,128)}) custom-call(s32[3]{0:T(128)} %pad_add_fusion.place_ref, bf16[512,1152]{1,0:T(8,128)(2,1)} %copy-done, bf16[1152,2304]{1,0:T(8,128)(2,1)} %bitcast.270, bf16[1152,2304]{1,0:T(8,128)(2,1)} %bitcast.271, ...), custom_call_target="tpu_custom_call" | custom-call | flops 169869312 | bytes 700416 | tf_op jit(solution)/shard_map/units_back/pallas_call | solution.py:635
  351.5 8.1 %collective-permute-done.34 = bf16[128,1152]{1,0:T(8,128)(2,1)S(1)} collective-permute-done((bf16[128,1152]{1,0:T(8,128)(2,1)S(1)}, bf16[128,1152]{1,0:T(8,128)(2,1)S(1)}, u32[]{:S(2)}, u32[]{:S(2)}) %collective-permute-start.34) | collective-permute-done | bytes 294944 | tf_op jit(solution)/shard_map/ppermute | solution.py:54
  368.2 9.0 %weight_grad.4 = (bf16[4,72,2304]{2,1,0:T(8,128)(2,1)}, bf16[4,72,2304]{2,1,0:T(8,128)(2,1)}, bf16[4,72,2304]{2,1,0:T(8,128)(2,1)}, bf16[2,72,2304]{2,1,0:T(8,128)(2,1)}, bf16[2,72,2304]{2,1,0:T(8,128)(2,1)}) custom-call(s32[3]{0:T(128)} %pad_add_fusion.place_ref, bf16[512,1152]{1,0:T(8,128)(2,1)} %copy-done.3, ...), custom_call_target="tpu_custom_call" | custom-call | flops 169869312 | bytes 774144 | tf_op jit(solution)/shard_map/weight_grad/pallas_call | solution.py:213
  379.1 11.1 %attention_back.2 = (bf16[256,1792]{1,0:T(8,128)(2,1)}, bf16[256,1152]{1,0:T(8,128)(2,1)}, f32[1,1,1792]{2,1,0:T(1,128)}) custom-call(bf16[256,1152]{1,0:T(8,128)(2,1)} %get-tuple-element.218.upstream_ref.refs_2_, bf16[1152,2432]{1,0:T(8,128)(2,1)} %bitcast.275, bf16[256,1792]{1,0:T(8,128)(2,1)} %get-tuple-element.194.joined_ref), custom_call_target="tpu_custom_call" | custom-call | flops 113246208 | bytes 538624 | tf_op jit(solution)/shard_map/attention_back/pallas_call | solution.py:592
  448.6 9.2 %units_back.3 = (bf16[512,1152]{1,0:T(8,128)(2,1)}, bf16[2,128,1152]{2,1,0:T(8,128)(2,1)}, bf16[2,128,1152]{2,1,0:T(8,128)(2,1)}, f32[1,1152]{1,0:T(1,128)}) custom-call(s32[3]{0:T(128)} %pad_add_fusion.place_ref, bf16[512,1152]{1,0:T(8,128)(2,1)} %copy-done.1, bf16[1152,2304]{1,0:T(8,128)(2,1)} %bitcast.266, bf16[1152,2304]{1,0:T(8,128)(2,1)} %bitcast.267, ...), custom_call_target="tpu_custom_call" | custom-call | flops 169869312 | bytes 700416 | tf_op jit(solution)/shard_map/units_back/pallas_call | solution.py:635
  476.2 8.6 %weight_grad.6 = (bf16[4,72,2304]{2,1,0:T(8,128)(2,1)}, bf16[4,72,2304]{2,1,0:T(8,128)(2,1)}, bf16[4,72,2304]{2,1,0:T(8,128)(2,1)}, bf16[2,72,2304]{2,1,0:T(8,128)(2,1)}, bf16[2,72,2304]{2,1,0:T(8,128)(2,1)}) custom-call(s32[3]{0:T(128)} %pad_add_fusion.place_ref, bf16[512,1152]{1,0:T(8,128)(2,1)} %copy-done.2, ...), custom_call_target="tpu_custom_call" | custom-call | flops 169869312 | bytes 774144 | tf_op jit(solution)/shard_map/weight_grad/pallas_call | solution.py:213
  498.0 7.5 %collective-permute-done.49 = bf16[2,72,2304]{2,1,0:T(8,128)(2,1)} collective-permute-done((bf16[2,72,2304]{2,1,0:T(8,128)(2,1)}, bf16[2,72,2304]{2,1,0:T(8,128)(2,1)}, u32[]{:S(2)}, u32[]{:S(2)}) %collective-permute-start.49) | collective-permute-done | bytes 663584 | tf_op jit(solution)/shard_map/ppermute | solution.py:54
  505.4 11.0 %attention_back.3 = (bf16[256,1792]{1,0:T(8,128)(2,1)}, bf16[256,1152]{1,0:T(8,128)(2,1)}, f32[1,1,1792]{2,1,0:T(1,128)}) custom-call(bf16[256,1152]{1,0:T(8,128)(2,1)} %get-tuple-element.241.upstream_ref.refs_2_, bf16[1152,2432]{1,0:T(8,128)(2,1)} %bitcast.273, bf16[256,1792]{1,0:T(8,128)(2,1)} %get-tuple-element.242.joined_ref), custom_call_target="tpu_custom_call" | custom-call | flops 113246208 | bytes 538624 | tf_op jit(solution)/shard_map/attention_back/pallas_call | solution.py:592
  546.8 8.1 %collective-permute-start.60 = (bf16[4,72,2432]{2,1,0:T(8,128)(2,1)}, bf16[4,72,2432]{2,1,0:T(8,128)(2,1)}, u32[]{:S(2)}, u32[]{:S(2)}) collective-permute-start(bf16[4,72,2432]{2,1,0:T(8,128)(2,1)} %get-tuple-element.283), channel_id=1, source_target_pairs={{0,4},{2,6},{4,0},{6,2},{8,12},{10,14},{12,8},{14,10},{16,20},{18,... | collective-permute-start | bytes 4202504 | tf_op jit(solution)/shard_map/ppermute | solution.py:54
  572.4 20.8 %all-to-all-done.4 = f32[32,1,1008]{2,1,0:T(1,128)S(1)} async-done(((f32[32,1,1008]{2,1,0:T(1,128)}), f32[32,1,1008]{2,1,0:T(1,128)S(1)}, u32[]{:S(2)}, u32[]{:S(2)}) %all-to-all-start.4) | async-done | bytes 129056 | tf_op jit(solution)/shard_map/all_to_all | solution.py:325
  608.3 8.4 %all-to-all-done.5 = f32[32,1,432]{2,1,0:T(1,128)S(1)} async-done(((f32[32,1,432]{2,1,0:T(1,128)}), f32[32,1,432]{2,1,0:T(1,128)S(1)}, u32[]{:S(2)}, u32[]{:S(2)}) %all-to-all-start.5) | async-done | bytes 55328 | tf_op jit(solution)/shard_map/all_to_all | solution.py:325
  641.0 20.4 %collective-permute-done.64 = bf16[72,2432]{1,0:T(8,128)(2,1)} collective-permute-done((bf16[72,2432]{1,0:T(8,128)(2,1)}, bf16[72,2432]{1,0:T(8,128)(2,1)}, u32[]{:S(2)}, u32[]{:S(2)}) %collective-permute-start.64) | collective-permute-done | bytes 350240 | tf_op jit(solution)/shard_map/ppermute | solution.py:54
  (514 shorter events, 375.9 us)
Async XLA Ops:
  46.1 47.7 %collective-permute-start.3 = (bf16[4,72,2432]{2,1,0:T(8,128)(2,1)S(1)}, bf16[4,72,2432]{2,1,0:T(8,128)(2,1)}, u32[]{:S(2)}, u32[]{:S(2)}) collective-permute-start(bf16[4,72,2432]{2,1,0:T(8,128)(2,1)S(1)} %pad_maximum_fusion.1.own_ref), channel_id=1, source_target_pairs={{0,2},{2,0},{4,6},{6,4},{8,10},{10,8},{12,14},{14,12},{16,18},{18,... | collective-permute-start | bytes 4202504 | tf_op jit(solution)/shard_map/ppermute | solution.py:54
  47.7 48.8 %collective-permute-start.4 = (bf16[4,72,2432]{2,1,0:T(8,128)(2,1)S(1)}, bf16[4,72,2432]{2,1,0:T(8,128)(2,1)}, u32[]{:S(2)}, u32[]{:S(2)}) collective-permute-start(bf16[4,72,2432]{2,1,0:T(8,128)(2,1)S(1)} %pad_maximum_fusion.1.own_ref), channel_id=1, source_target_pairs={{0,4},{2,6},{4,0},{6,2},{8,12},{10,14},{12,8},{14,10},{16,20},{18,... | collective-permute-start | bytes 4202504 | tf_op jit(solution)/shard_map/ppermute | solution.py:54
  99.1 51.9 %collective-permute-start.15 = (bf16[4,72,2304]{2,1,0:T(8,128)(2,1)S(1)}, bf16[4,72,2304]{2,1,0:T(8,128)(2,1)}, u32[]{:S(2)}, u32[]{:S(2)}) collective-permute-start(bf16[4,72,2304]{2,1,0:T(8,128)(2,1)S(1)} %pad_maximum_fusion.3.own_ref), channel_id=1, source_target_pairs={{0,2},{2,0},{4,6},{6,4},{8,10},{10,8},{12,14},{14,12},{16,18},{18,... | collective-permute-start | bytes 3981320 | tf_op jit(solution)/shard_map/ppermute | solution.py:54
  100.7 53.1 %collective-permute-start.16 = (bf16[4,72,2304]{2,1,0:T(8,128)(2,1)S(1)}, bf16[4,72,2304]{2,1,0:T(8,128)(2,1)}, u32[]{:S(2)}, u32[]{:S(2)}) collective-permute-start(bf16[4,72,2304]{2,1,0:T(8,128)(2,1)S(1)} %pad_maximum_fusion.3.own_ref), channel_id=1, source_target_pairs={{0,4},{2,6},{4,0},{6,2},{8,12},{10,14},{12,8},{14,10},{16,20},{18,... | collective-permute-start | bytes 3981320 | tf_op jit(solution)/shard_map/ppermute | solution.py:54
  149.8 58.1 %collective-permute-start.20 = (bf16[4,72,2432]{2,1,0:T(8,128)(2,1)}, bf16[4,72,2432]{2,1,0:T(8,128)(2,1)}, u32[]{:S(2)}, u32[]{:S(2)}) collective-permute-start(bf16[4,72,2432]{2,1,0:T(8,128)(2,1)} %pad_maximum_fusion.2.own_ref), channel_id=1, source_target_pairs={{0,2},{2,0},{4,6},{6,4},{8,10},{10,8},{12,14},{14,12},{16,18},{18,... | collective-permute-start | bytes 4202504 | tf_op jit(solution)/shard_map/ppermute | solution.py:54
  151.1 56.8 %collective-permute-start.21 = (bf16[4,72,2432]{2,1,0:T(8,128)(2,1)}, bf16[4,72,2432]{2,1,0:T(8,128)(2,1)}, u32[]{:S(2)}, u32[]{:S(2)}) collective-permute-start(bf16[4,72,2432]{2,1,0:T(8,128)(2,1)} %pad_maximum_fusion.2.own_ref), channel_id=1, source_target_pairs={{0,4},{2,6},{4,0},{6,2},{8,12},{10,14},{12,8},{14,10},{16,20},{18,... | collective-permute-start | bytes 4202504 | tf_op jit(solution)/shard_map/ppermute | solution.py:54
  153.8 44.0 %collective-permute-start.23 = (bf16[2,72,2304]{2,1,0:T(8,128)(2,1)}, bf16[2,72,2304]{2,1,0:T(8,128)(2,1)}, u32[]{:S(2)}, u32[]{:S(2)}) collective-permute-start(bf16[2,72,2304]{2,1,0:T(8,128)(2,1)} %slice.561), channel_id=1, source_target_pairs={{0,4},{2,6},{4,0},{6,2},{8,12},{10,14},{12,8},{14,10},{16,20},{18,... | collective-permute-start | bytes 1990664 | tf_op jit(solution)/shard_map/ppermute | solution.py:54
  156.2 43.2 %collective-permute-start.24 = (bf16[2,72,2304]{2,1,0:T(8,128)(2,1)S(1)}, bf16[2,72,2304]{2,1,0:T(8,128)(2,1)}, u32[]{:S(2)}, u32[]{:S(2)}) collective-permute-start(bf16[2,72,2304]{2,1,0:T(8,128)(2,1)S(1)} %slice.562), channel_id=1, source_target_pairs={{0,2},{2,0},{4,6},{6,4},{8,10},{10,8},{12,14},{14,12},{16,18},{18,... | collective-permute-start | bytes 1990664 | tf_op jit(solution)/shard_map/ppermute | solution.py:54
  162.3 43.1 %collective-permute-start.19 = (bf16[128,1152]{1,0:T(8,128)(2,1)}, bf16[128,1152]{1,0:T(8,128)(2,1)}, u32[]{:S(2)}, u32[]{:S(2)}) collective-permute-start(bf16[128,1152]{1,0:T(8,128)(2,1)} %constant_dynamic-slice_fusion.9), channel_id=1, source_target_pairs={{0,8},{2,10},{4,12},{6,14},{8,0},{10,2},{12,4},{14,6},{16,24},{18,... | collective-permute-start | bytes 884744 | tf_op jit(solution)/shard_map/ppermute | solution.py:54
  232.2 45.1 %collective-permute-start.27 = (bf16[2,72,2432]{2,1,0:T(8,128)(2,1)S(1)}, bf16[2,72,2432]{2,1,0:T(8,128)(2,1)}, u32[]{:S(2)}, u32[]{:S(2)}) collective-permute-start(bf16[2,72,2432]{2,1,0:T(8,128)(2,1)S(1)} %slice.568), channel_id=1, source_target_pairs={{0,4},{2,6},{4,0},{6,2},{8,12},{10,14},{12,8},{14,10},{16,20},{18,... | collective-permute-start | bytes 2101256 | tf_op jit(solution)/shard_map/ppermute | solution.py:54
  235.1 42.3 %collective-permute-start.28 = (bf16[2,72,2432]{2,1,0:T(8,128)(2,1)}, bf16[2,72,2432]{2,1,0:T(8,128)(2,1)}, u32[]{:S(2)}, u32[]{:S(2)}) collective-permute-start(bf16[2,72,2432]{2,1,0:T(8,128)(2,1)} %slice.569), channel_id=1, source_target_pairs={{0,2},{2,0},{4,6},{6,4},{8,10},{10,8},{12,14},{14,12},{16,18},{18,... | collective-permute-start | bytes 2101256 | tf_op jit(solution)/shard_map/ppermute | solution.py:54
  377.2 48.9 %collective-permute-start.41 = (bf16[4,72,2304]{2,1,0:T(8,128)(2,1)}, bf16[4,72,2304]{2,1,0:T(8,128)(2,1)S(1)}, u32[]{:S(2)}, u32[]{:S(2)}) collective-permute-start(bf16[4,72,2304]{2,1,0:T(8,128)(2,1)} %get-tuple-element.211), channel_id=1, source_target_pairs={{0,2},{2,0},{4,6},{6,4},{8,10},{10,8},{12,14},{14,12},{16,18},{18,... | collective-permute-start | bytes 3981320 | tf_op jit(solution)/shard_map/ppermute | solution.py:54
  377.8 48.4 %collective-permute-start.42 = (bf16[4,72,2304]{2,1,0:T(8,128)(2,1)}, bf16[4,72,2304]{2,1,0:T(8,128)(2,1)}, u32[]{:S(2)}, u32[]{:S(2)}) collective-permute-start(bf16[4,72,2304]{2,1,0:T(8,128)(2,1)} %get-tuple-element.212), channel_id=1, source_target_pairs={{0,4},{2,6},{4,0},{6,2},{8,12},{10,14},{12,8},{14,10},{16,20},{18,... | collective-permute-start | bytes 3981320 | tf_op jit(solution)/shard_map/ppermute | solution.py:54
  412.1 51.7 %collective-permute-start.45 = (bf16[4,72,2432]{2,1,0:T(8,128)(2,1)}, bf16[4,72,2432]{2,1,0:T(8,128)(2,1)}, u32[]{:S(2)}, u32[]{:S(2)}) collective-permute-start(bf16[4,72,2432]{2,1,0:T(8,128)(2,1)} %get-tuple-element.228), channel_id=1, source_target_pairs={{0,2},{2,0},{4,6},{6,4},{8,10},{10,8},{12,14},{14,12},{16,18},{18,... | collective-permute-start | bytes 4202504 | tf_op jit(solution)/shard_map/ppermute | solution.py:54
  414.0 49.7 %collective-permute-start.46 = (bf16[4,72,2432]{2,1,0:T(8,128)(2,1)}, bf16[4,72,2432]{2,1,0:T(8,128)(2,1)}, u32[]{:S(2)}, u32[]{:S(2)}) collective-permute-start(bf16[4,72,2432]{2,1,0:T(8,128)(2,1)} %get-tuple-element.229), channel_id=1, source_target_pairs={{0,4},{2,6},{4,0},{6,2},{8,12},{10,14},{12,8},{14,10},{16,20},{18,... | collective-permute-start | bytes 4202504 | tf_op jit(solution)/shard_map/ppermute | solution.py:54
  428.8 35.0 %collective-permute-start.43 = (bf16[2,72,2304]{2,1,0:T(8,128)(2,1)}, bf16[2,72,2304]{2,1,0:T(8,128)(2,1)S(1)}, u32[]{:S(2)}, u32[]{:S(2)}) collective-permute-start(bf16[2,72,2304]{2,1,0:T(8,128)(2,1)} %add_convert_fusion.7), channel_id=1, source_target_pairs={{0,2},{2,0},{4,6},{6,4},{8,10},{10,8},{12,14},{14,12},{16,18},{18,... | collective-permute-start | bytes 1990664 | tf_op jit(solution)/shard_map/ppermute | solution.py:54
  466.1 39.4 %collective-permute-start.47 = (bf16[2,72,2432]{2,1,0:T(8,128)(2,1)S(1)}, bf16[2,72,2432]{2,1,0:T(8,128)(2,1)}, u32[]{:S(2)}, u32[]{:S(2)}) collective-permute-start(bf16[2,72,2432]{2,1,0:T(8,128)(2,1)S(1)} %add_convert_fusion.3), channel_id=1, source_target_pairs={{0,2},{2,0},{4,6},{6,4},{8,10},{10,8},{12,14},{14,12},{16,18},{18,... | collective-permute-start | bytes 2101256 | tf_op jit(solution)/shard_map/ppermute | solution.py:54
  469.7 35.7 %collective-permute-start.48 = (bf16[2,72,2432]{2,1,0:T(8,128)(2,1)}, bf16[2,72,2432]{2,1,0:T(8,128)(2,1)}, u32[]{:S(2)}, u32[]{:S(2)}) collective-permute-start(bf16[2,72,2432]{2,1,0:T(8,128)(2,1)} %add_convert_fusion.2), channel_id=1, source_target_pairs={{0,4},{2,6},{4,0},{6,2},{8,12},{10,14},{12,8},{14,10},{16,20},{18,... | collective-permute-start | bytes 2101256 | tf_op jit(solution)/shard_map/ppermute | solution.py:54
  484.9 35.2 %collective-permute-start.51 = (bf16[4,72,2304]{2,1,0:T(8,128)(2,1)}, bf16[4,72,2304]{2,1,0:T(8,128)(2,1)}, u32[]{:S(2)}, u32[]{:S(2)}) collective-permute-start(bf16[4,72,2304]{2,1,0:T(8,128)(2,1)} %get-tuple-element.251), channel_id=1, source_target_pairs={{0,2},{2,0},{4,6},{6,4},{8,10},{10,8},{12,14},{14,12},{16,18},{18,... | collective-permute-start | bytes 3981320 | tf_op jit(solution)/shard_map/ppermute | solution.py:54
  520.1 34.9 %collective-permute-start.55 = (bf16[2,72,2432]{2,1,0:T(8,128)(2,1)}, bf16[2,72,2432]{2,1,0:T(8,128)(2,1)S(1)}, u32[]{:S(2)}, u32[]{:S(2)}) collective-permute-start(bf16[2,72,2432]{2,1,0:T(8,128)(2,1)} %pad_maximum_fusion.8), channel_id=1, source_target_pairs={{0,16},{2,18},{4,20},{6,22},{8,24},{10,26},{12,28},{14,30},{16,0},... | collective-permute-start | bytes 2101256 | tf_op jit(solution)/shard_map/ppermute | solution.py:54
  545.5 47.7 %collective-permute-start.59 = (bf16[4,72,2432]{2,1,0:T(8,128)(2,1)}, bf16[4,72,2432]{2,1,0:T(8,128)(2,1)}, u32[]{:S(2)}, u32[]{:S(2)}) collective-permute-start(bf16[4,72,2432]{2,1,0:T(8,128)(2,1)} %get-tuple-element.282), channel_id=1, source_target_pairs={{0,2},{2,0},{4,6},{6,4},{8,10},{10,8},{12,14},{14,12},{16,18},{18,... | collective-permute-start | bytes 4202504 | tf_op jit(solution)/shard_map/ppermute | solution.py:54
  546.8 46.5 %collective-permute-start.60 = (bf16[4,72,2432]{2,1,0:T(8,128)(2,1)}, bf16[4,72,2432]{2,1,0:T(8,128)(2,1)}, u32[]{:S(2)}, u32[]{:S(2)}) collective-permute-start(bf16[4,72,2432]{2,1,0:T(8,128)(2,1)} %get-tuple-element.283), channel_id=1, source_target_pairs={{0,4},{2,6},{4,0},{6,2},{8,12},{10,14},{12,8},{14,10},{16,20},{18,... | collective-permute-start | bytes 4202504 | tf_op jit(solution)/shard_map/ppermute | solution.py:54
  559.3 58.0 %collective-permute-start.57 = (bf16[2,72,2304]{2,1,0:T(8,128)(2,1)}, bf16[2,72,2304]{2,1,0:T(8,128)(2,1)}, u32[]{:S(2)}, u32[]{:S(2)}) collective-permute-start(bf16[2,72,2304]{2,1,0:T(8,128)(2,1)} %pad_maximum_fusion.13), channel_id=1, source_target_pairs={{0,16},{2,18},{4,20},{6,22},{8,24},{10,26},{12,28},{14,30},{16,0},... | collective-permute-start | bytes 1990664 | tf_op jit(solution)/shard_map/ppermute | solution.py:54
  560.2 57.1 %collective-permute-start.58 = (bf16[1,72,2432]{2,1,0:T(8,128)(2,1)}, bf16[1,72,2432]{2,1,0:T(8,128)(2,1)}, u32[]{:S(2)}, u32[]{:S(2)}) collective-permute-start(bf16[1,72,2432]{2,1,0:T(8,128)(2,1)} %get-tuple-element.412), channel_id=1, source_target_pairs={{0,8},{2,10},{4,12},{6,14},{8,0},{10,2},{12,4},{14,6},{16,24},{18,... | collective-permute-start | bytes 1050632 | tf_op jit(solution)/shard_map/ppermute | solution.py:54
  (111 other events, 1461.9 us)

commit v4 on v3

--- a/solution.py
+++ b/solution.py
@@ -150,20 +150,23 @@
     return (swap_by(halves[0], 2), swap_by(halves[1], 1))
 
 
-def together(*values):
-    return lax.optimization_barrier(values)
-
-
-def weight_grad_kernel(count, starts, place_ref, *refs):
+def weight_grad_kernel(count, starts, lefts, place_ref, *refs):
     pairs = len(starts)
-    operands, outs, total = refs[: 2 * pairs], refs[2 * pairs : -1], refs[-1]
+    operands, outs = refs[: pairs * (lefts + 1)], refs[pairs * (lefts + 1) : -2]
+    left_rows, total = refs[-2:]
     own, to_across, to_along, rest_across, rest_along = outs
     me, plane = place_ref[1], place_ref[2]
     rows, groups = total.shape[0] // count, count // 4
     half = groups // 2
     for index, start in enumerate(starts):
-        left, right = operands[2 * index], operands[2 * index + 1]
-        total[:, start : start + right.shape[1]] = product_left(left[...], right[...])
+        *parts, right = operands[index * (lefts + 1) : (index + 1) * (lefts + 1)]
+        if lefts == 1:
+            left = parts[0][...]
+        else:
+            for at, part in enumerate(parts):
+                left_rows[at * part.shape[0] : (at + 1) * part.shape[0]] = part[...]
+            left = left_rows[...]
+        total[:, start : start + right.shape[1]] = product_left(left, right[...])
         spare = -right.shape[1] % 128
         if spare:
             end = start + right.shape[1]
@@ -203,27 +206,28 @@
     count = lax.axis_size("dp")
     groups = count // 4
     half = groups // 2
-    width = pairs[0][0].shape[1]
+    lefts = len(pairs[0][0])
+    width = pairs[0][0][0].shape[1]
     rows = width // count
     starts, columns = [], 0
     for _, right in pairs:
         starts.append(columns)
         columns += padded(right.shape[1])
-    tokens = pairs[0][0].shape[0]
+    tokens = pairs[0][1].shape[0]
     own, to_across, to_along, rest_across, rest_along = pl.pallas_call(
-        functools.partial(weight_grad_kernel, count, tuple(starts)),
+        functools.partial(weight_grad_kernel, count, tuple(starts), lefts),
         out_shape=[
             jax.ShapeDtypeStruct((blocks, rows, columns), low)
             for blocks in (groups, groups, groups, half, half)
         ],
         in_specs=[pl.BlockSpec(memory_space=pltpu.SMEM)]
-        + [pl.BlockSpec(memory_space=pltpu.VMEM)] * (2 * len(pairs)),
-        scratch_shapes=[pltpu.VMEM((width, columns), wide)],
+        + [pl.BlockSpec(memory_space=pltpu.VMEM)] * ((lefts + 1) * len(pairs)),
+        scratch_shapes=[pltpu.VMEM((tokens, width), low), pltpu.VMEM((width, columns), wide)],
         name="weight_grad",
         cost_estimate=cost(
             2 * tokens * width * columns, 2 * width * columns + 4 * tokens * (width + columns)
         ),
-    )(place_scalars(), *[operand for pair in pairs for operand in pair])
+    )(place_scalars(), *[operand for left, right in pairs for operand in (*left, right)])
     return (own, rest_across, rest_along, to_across, to_along)
 
 
@@ -232,11 +236,16 @@
     return (own, rest_across, rest_along, swap_by(to_across, 1), swap_by(to_along, 2))
 
 
-def scatter_near(state):
+def scatter_near_sums(state):
     own, rest_across, rest_along, got_across, got_along = state
     half = rest_across.shape[0]
     rest_across = (rest_across.astype(wide) + got_along[:half].astype(wide)).astype(low)
     rest_along = (rest_along.astype(wide) + got_across[:half].astype(wide)).astype(low)
+    return (own, got_across, got_along, rest_across, rest_along)
+
+
+def scatter_near(sums):
+    own, got_across, got_along, rest_across, rest_along = sums
     return (own, got_across, got_along, swap_by(rest_across, 1), swap_by(rest_along, 2))
 
 
@@ -253,8 +262,7 @@
     return [total(relative) for relative in range(own.shape[0])]
 
 
-def scatter_planes(state):
-    blocks = scatter_plane_blocks(state)
+def scatter_planes(blocks):
     got = [
         swap_by(block.astype(low), relative << 2) for relative, block in enumerate(blocks) if relative
     ]
@@ -300,11 +308,14 @@
     )
 
 
-def pair_rows(values):
+def pair_part(values):
     half = values.shape[0] // 2
-    sent = lax.dynamic_slice_in_dim(values, lax.axis_index("tensor") * half, half, 0)
+    return lax.dynamic_slice_in_dim(values, lax.axis_index("tensor") * half, half, 0)
+
+
+def pair_rows(values, sent):
     got = swap_by(sent, 1 << PAIR)
-    return jnp.concatenate([values, lax.all_gather(got, "tensor", axis=0, tiled=True)])
+    return (values, lax.all_gather(got, "tensor", axis=0, tiled=True))
 
 
 def chip_sum(keep, send):
@@ -349,6 +360,10 @@
 
 
 COST_SHARE = 16
+
+
+def by_group(*rest):
+    return pl.BlockSpec((1,) + rest, lambda i, *_: (i // STEPS,) + (0,) * len(rest))
 
 
 def cost(flops, bytes_accessed, transcendentals=0):
@@ -357,6 +372,18 @@
         bytes_accessed=bytes_accessed // COST_SHARE,
         transcendentals=transcendentals // COST_SHARE,
     )
+
+
+STEPS = 2
+
+
+def add_sums(sums_ref, *values):
+    @pl.when(lax.rem(pl.program_id(0), STEPS) == 0)
+    def _():
+        sums_ref[...] = jnp.zeros_like(sums_ref)
+
+    for row, value in enumerate(values):
+        sums_ref[0, row : row + 1] += column_sum(value)
 
 
 def column_sum(values):
@@ -417,13 +444,17 @@
             for part in range(3)
         )
         upstream = attended_grad[:, start : start + HEAD_DIM]
-        probs = head_probs(query, keys, mask)
-        value_grad = product_left(probs.astype(low), upstream)
-        prob_grad = product_right(upstream, value)
-        centre = jnp.sum(probs * prob_grad, axis=-1, keepdims=True)
+        scores = product_right(keys, query) * score_scale
+        if mask is not None:
+            scores = jnp.where(mask, scores, -1e30)
+        exponent = jnp.exp(scores - jnp.max(scores, axis=0, keepdims=True))
+        probs = exponent * (1.0 / jnp.sum(exponent, axis=0, keepdims=True))
+        value_grad = product(probs.astype(low), upstream)
+        prob_grad = product_right(value, upstream)
+        centre = jnp.sum(probs * prob_grad, axis=0, keepdims=True)
         score_grad = (probs * (prob_grad - centre)).astype(low)
-        query_grad = product(score_grad, keys) * score_scale
-        keys_grad = product_left(score_grad, query) * score_scale
+        query_grad = product_left(score_grad, keys) * score_scale
+        keys_grad = product(score_grad, query) * score_scale
         for part, grad in enumerate((query_grad, keys_grad, value_grad)):
             grad_ref[:, part * width + start : part * width + start + HEAD_DIM] = grad.astype(low)
     spare = joined_width - 3 * width
@@ -460,7 +491,8 @@
 
 def units_kernel(
     place_ref,
-    hidden_ref,
+    own_ref,
+    other_ref,
     up_ref,
     down_ref,
     bias_ref,
@@ -470,7 +502,8 @@
     send_ref,
     partial_ref,
 ):
-    inner = product(hidden_ref[...], up_ref[...]) + bias_ref[...]
+    hidden = jnp.where(pl.program_id(0) == 0, own_ref[...], other_ref[...])
+    inner = product(hidden, up_ref[...]) + bias_ref[...]
     active, slope = gelu_parts(inner)
     slope_ref[...] = slope.astype(low)
     active = active.astype(low)
@@ -481,7 +514,8 @@
 
 def units_back_kernel(
     place_ref,
-    upstream_ref,
+    own_ref,
+    other_ref,
     up_ref,
     down_ref,
     slope_ref,
@@ -491,7 +525,8 @@
     bias_ref,
     partial_ref,
 ):
-    grad = (product(upstream_ref[...], down_ref[...]) * slope_ref[...].astype(wide)).astype(low)
+    upstream = jnp.where(pl.program_id(0) == 0, own_ref[...], other_ref[...])
+    grad = (product(upstream, down_ref[...]) * slope_ref[...].astype(wide)).astype(low)
     grad_ref[...] = grad
 
     @pl.when(pl.program_id(0) == 0)
@@ -511,12 +546,12 @@
 def turn_kernel(upstream_ref, mod_ref, grad_ref, sums_ref):
     grad = (upstream_ref[...].astype(wide) * mod_ref[0, 5:6]).astype(low)
     grad_ref[...] = grad
-    sums_ref[0, 0:1] = column_sum(grad.astype(wide))
+    add_sums(sums_ref, grad.astype(wide))
 
 
 def gate_kernel(upstream_ref, branch_ref, bias_ref, mod_ref, sums_ref):
     branch = branch_ref[...].astype(wide) + bias_ref[...]
-    sums_ref[0, 0:1] = column_sum(upstream_ref[...].astype(wide) * branch)
+    add_sums(sums_ref, upstream_ref[...].astype(wide) * branch)
 
 
 def middle_back_kernel(
@@ -540,10 +575,9 @@
     grad = (middle_grad * mod_ref[0, 2:3]).astype(low)
     grad_ref[...] = grad
     branch = mine_ref[...].astype(wide) + theirs_ref[...].astype(wide) + bias_ref[...]
-    sums_ref[0, 0:1] = column_sum(hidden_grad)
-    sums_ref[0, 1:2] = column_sum(hidden_grad * normed)
-    sums_ref[0, 2:3] = column_sum(middle_grad * branch)
-    sums_ref[0, 3:4] = column_sum(grad.astype(wide))
+    add_sums(
+        sums_ref, hidden_grad, hidden_grad * normed, middle_grad * branch, grad.astype(wide)
+    )
 
 
 def input_back_kernel(middle_ref, mine_ref, theirs_ref, x_ref, mod_ref, out_ref, sums_ref):
@@ -552,8 +586,7 @@
     out_ref[...] = (
         middle_ref[...] + layer_norm_back(normed, inverse, hidden_grad * (1.0 + mod_ref[0, 1:2]))
     ).astype(out_ref.dtype)
-    sums_ref[0, 0:1] = column_sum(hidden_grad)
-    sums_ref[0, 1:2] = column_sum(hidden_grad * normed)
+    add_sums(sums_ref, hidden_grad, hidden_grad * normed)
 
 
 def array(dtype, *shape):
@@ -608,28 +641,48 @@
     )(upstream, weight, joined)
 
 
-def row_kernel(body, groups, row_inputs, fixed_inputs, mods, outs, sums, name):
+def row_kernel(body, groups, row_inputs, fixed_inputs, mods, outs, sums, name, sent=None):
     rows, width = row_inputs[0].shape
-    block = rows // groups
+    block = rows // (groups * STEPS)
     sum_shape = [array(wide, groups, 8, width)] * sums
     moved = sum(item.size * item.dtype.itemsize for item in row_inputs)
-    return pl.pallas_call(
-        body,
-        grid=(groups,),
-        in_specs=[by_rows(block, width) for _ in row_inputs]
-        + [fixed(*item.shape) for item in fixed_inputs]
-        + [by_rows(1, 6, width)],
-        out_specs=[by_rows(block, width) for _ in outs] + [by_rows(1, 8, width)] * sums,
-        out_shape=[array(dtype, rows, width) for dtype in outs] + sum_shape,
+    first_out = len(row_inputs) + len(fixed_inputs) + 1
+    alone = sent is not None and groups == 1 and STEPS == 2
+
+    def steps(place_ref, *refs):
+        body(*refs[:-1])
+
+        @pl.when(pl.program_id(0) == place_ref[0])
+        def _():
+            refs[-1][...] = refs[first_out + sent][...]
+
+    results = pl.pallas_call(
+        steps if alone else body,
+        grid_spec=pltpu.PrefetchScalarGridSpec(
+            num_scalar_prefetch=int(alone),
+            grid=(groups * STEPS,),
+            in_specs=[by_rows(block, width) for _ in row_inputs]
+            + [fixed(*item.shape) for item in fixed_inputs]
+            + [by_group(6, width)],
+            out_specs=[by_rows(block, width) for _ in outs]
+            + [by_group(8, width)] * sums
+            + [fixed(block, width)] * alone,
+        ),
+        out_shape=[array(dtype, rows, width) for dtype in outs]
+        + sum_shape
+        + [array(low, block, width)] * alone,
         name=name,
         cost_estimate=cost(20 * rows * width, moved + 4 * rows * width * len(outs)),
-    )(*row_inputs, *fixed_inputs, mods)
+    )(*[place_scalars()] * alone, *row_inputs, *fixed_inputs, mods)
+    if sent is not None and not alone:
+        results = [*results, pair_part(results[sent])]
+    return results
 
 
 def units_call(body, rows_in, updown, extra, extra_spec, outs, out_specs, name):
-    rows, width = rows_in.shape
+    half, width = rows_in[0].shape
     units = updown.shape[1] // 2
-    half = rows // 2
+    rows = 2 * half
     halves = array(low, 2, half // 2, width)
     at = pl.BlockSpec((1, half // 2, width), lambda i, *_: (i, 0, 0))
     return pl.pallas_call(
@@ -638,7 +691,8 @@
             num_scalar_prefetch=1,
             grid=(2,),
             in_specs=[
-                by_rows(half, width),
+                fixed(half, width),
+                fixed(half, width),
                 pl.BlockSpec((width, units), lambda i, *_: (0, 0)),
                 pl.BlockSpec((width, units), lambda i, *_: (0, 1)),
                 extra_spec,
@@ -657,11 +711,11 @@
             4 * width * units + 4 * rows * width + 6 * rows * units,
             rows * units,
         ),
-    )(place_scalars(), rows_in, updown, updown, extra)
+    )(place_scalars(), *rows_in, updown, updown, extra)
 
 
 def units_forward(hidden, updown, bias):
-    rows, units = hidden.shape[0], updown.shape[1] // 2
+    rows, units = 2 * hidden[0].shape[0], updown.shape[1] // 2
     block = by_rows(rows // 2, units)
     return units_call(
         units_kernel,
@@ -690,13 +744,13 @@
     )
 
 
-def first_half(x, mods, wattn, biases, place_count):
+def first_half(x, mods, wattn, biases, place_count, *others):
     hidden, joined, attended, mine = attention_forward(x, mods, wattn, biases[0], place_count)
-    both = (mine, swap_tensor(mine))
-    middle, hidden_mlp = row_kernel(
-        middle_kernel, mods.shape[0], (x, *both), (biases[1],), mods, (wide, low), 0, "middle"
-    )
-    return (hidden, joined, attended, both, middle, hidden_mlp)
+    both = after((mine, swap_tensor(mine)), *others)
+    middle, hidden_mlp, sent = row_kernel(
+        middle_kernel, mods.shape[0], (x, *both), (biases[1],), mods, (wide, low), 0, "middle", 1
+    )
+    return (hidden, joined, attended, both, middle, (hidden_mlp, sent))
 
 
 def block_result(middle, branch, biases, mods):
@@ -706,7 +760,10 @@
 
 
 def turn(upstream, mods):
-    return row_kernel(turn_kernel, mods.shape[0], (upstream,), (), mods, (low,), 1, "turn")
+    grad, sums, sent = row_kernel(
+        turn_kernel, mods.shape[0], (upstream,), (), mods, (low,), 1, "turn", 0
+    )
+    return (grad, sent), sums
 
 
 def gate_sums(upstream, branch, biases, mods):
@@ -741,27 +798,47 @@
     )
 
 
-def small_grads(input_sums, middle_sums, gate, turn_sums, joined_bias, fc1_bias):
-    width = gate.shape[2]
-    part_width, units = width // 2, fc1_bias.shape[1]
-    mod_grad = 0.5 * jnp.concatenate(
-        [input_sums[:, :2], middle_sums[:, 2:3], middle_sums[:, :2], gate[:, :1]], axis=1
-    )
-    joined_bias = jnp.sum(joined_bias, axis=(0, 1))
-    at = lax.axis_index("tensor") * part_width
-    proj_grad = jnp.stack(
-        [
-            widen(joined_bias[:part_width], at, width),
-            widen(joined_bias[2 * part_width : 3 * part_width], at, width),
-            0.5 * jnp.sum(middle_sums[:, 3], axis=0),
-            0.5 * jnp.sum(turn_sums[:, 0], axis=0),
-        ]
-    )
-    return (mod_grad, proj_grad, widen(fc1_bias[0], unit_start(units), units * 4))
-
-
-def widen(local_part, offset, total):
-    return lax.dynamic_update_slice_in_dim(jnp.zeros((total,), wide), local_part, offset, 0)
+def pack_kernel(clips, scalars_ref, *refs):
+    out = refs[-1]
+    tensor, pair, first_frame = scalars_ref[0], scalars_ref[1], scalars_ref[2]
+    out[...] = jnp.zeros_like(out)
+    per_block = out.shape[0] // 2
+    width = out.shape[1]
+    for block in range(2):
+        inputs, middles, gate, turned, joined, fc1 = refs[6 * block : 6 * block + 6]
+        base = block * per_block
+        for group in range(gate.shape[0]):
+            clip = group if block else lax.div(first_frame + group, FRAMES)
+            if clips == 1:
+                clip = 0
+            parts = (
+                (inputs, 0), (inputs, 1), (middles, 2), (middles, 0), (middles, 1), (gate, 0)
+            )
+            for index, (ref, row) in enumerate(parts):
+                out[pl.ds(base + clip * 6 + index, 1), :] += 0.5 * ref[group, row : row + 1]
+            place = base + clips * 6
+            out[place : place + 1, :] += 0.5 * middles[group, 3:4]
+            out[place + 1 : place + 2, :] += 0.5 * turned[group, 0:1]
+            at = place + 2 + 2 * tensor
+            spare = joined.shape[2] - width
+            out[pl.ds(at, 1), :] += joined[group, :, :width]
+            out[pl.ds(at + 1, 1), :spare] += joined[group, :, width:]
+        out[pl.ds(base + clips * 6 + 6 + 2 * tensor + pair, 1), :] += fc1[...]
+
+
+def pack_sums(clips, first_frame, blocks):
+    width = blocks[0][0].shape[2]
+    rows = 2 * (6 * clips + 10)
+    scalars = jnp.stack([lax.axis_index("tensor"), my_bit(PAIR), first_frame]).astype(jnp.int32)
+    operands = [item for block in blocks for item in block]
+    return pl.pallas_call(
+        functools.partial(pack_kernel, clips),
+        out_shape=array(wide, rows, width),
+        in_specs=[pl.BlockSpec(memory_space=pltpu.SMEM)]
+        + [pl.BlockSpec(memory_space=pltpu.VMEM)] * len(operands),
+        name="pack",
+        cost_estimate=cost(rows * width, 8 * rows * width),
+    )(scalars, *operands)
 
 
 def tensor_part(values):
@@ -809,19 +886,6 @@
             )
         )
         shards.append((units_part(layer, my_bit(PAIR)), units_part(layer, 1 - my_bit(PAIR))))
-    own_attn_0 = gather_straight(shards[0])
-    near_attn_0 = gather_near(own_attn_0)
-    own_units_0 = gather_straight(after(shards[1], own_attn_0))
-    near_units_0 = gather_near(own_units_0)
-    far_attn_0 = gather_far(gather_halves(near_attn_0))
-    own_attn_1 = gather_planes(gather_pair(after(shards[2], own_units_0)))
-    near_attn_1 = gather_near(after(own_attn_1, near_attn_0))
-    own_units_1 = gather_planes(gather_pair(after(shards[3], own_attn_1)))
-    near_units_1 = gather_near(after(own_units_1, near_units_0))
-    far_units_0 = gather_far(gather_halves(near_units_0))
-    far_attn_1 = gather_far(gather_halves(near_attn_1))
-    far_units_1 = gather_far(gather_halves(near_units_1))
-
     cond_float = cond.astype(wide)
     gated_low = jax.nn.silu(cond_float).astype(low)
     gated_own = lax.dynamic_slice_in_dim(gated_low, own_start, own_width, 1).astype(wide)
@@ -840,6 +904,22 @@
     pieces = (own_mod, b_proj.astype(wide), b_fc1.astype(wide))
     packed = jnp.concatenate([piece.reshape(-1) for piece in pieces])
     dealt = deal(jnp.broadcast_to(packed[None], (all_devices, packed.shape[0])))
+
+    own_attn_0 = gather_straight(shards[0])
+    near_attn_0 = gather_near(after(own_attn_0, dealt))
+    own_units_0 = gather_straight(after(shards[1], own_attn_0))
+    pair_attn_1 = gather_pair(after(shards[2], own_attn_0, own_units_0, near_attn_0))
+    pair_units_1 = gather_pair(after(shards[3], pair_attn_1))
+    far_attn_0 = gather_far(gather_halves(near_attn_0))
+    near_units_0 = gather_near(own_units_0)
+    own_attn_1 = gather_planes(pair_attn_1)
+    own_units_1 = gather_planes(after(pair_units_1, own_attn_1, near_units_0))
+    near_attn_1 = gather_near(after(own_attn_1, near_attn_0, far_attn_0))
+    far_units_0 = gather_far(gather_halves(near_units_0))
+    near_units_1 = gather_near(after(own_units_1, near_units_0))
+    far_attn_1 = gather_far(gather_halves(near_attn_1))
+    far_units_1 = gather_far(gather_halves(near_units_1))
+    dealt = after(dealt, near_units_0)
     first_end, second_end = pieces[0].size, pieces[0].size + pieces[1].size
     modulation = from_owners(dealt[:, :first_end], (2, clip_count, 6))
     proj_full = from_owners(dealt[:, first_end:second_end], (2, 4))
@@ -877,124 +957,140 @@
 
     upstream_1 = flat(out_grad)
     mlp_grad_1, turn_sums_1 = turn(upstream_1, mods_1)
-    flat_grad_1 = pair_rows(mlp_grad_1)
+    flat_grad_1 = pair_rows(*mlp_grad_1)
 
     wattn_0 = arrange(*after((*near_attn_0, *far_attn_0), own_attn_1))
     x_0 = flat(tokens)
+    held = own_units_1
     hidden_0, joined_0, attended_0, both_0, middle_0, hidden_mlp = first_half(
-        x_0, mods_0, wattn_0, biases_0, None
-    )
-    flat_0 = pair_rows(hidden_mlp)
-    units_0 = arrange(*near_units_0, *far_units_0)
+        x_0, mods_0, wattn_0, biases_0, None, held
+    )
+    flat_0 = pair_rows(*hidden_mlp)
+    units_0 = arrange(*after((*near_units_0, *far_units_0), near_attn_1, own_units_1))
     slope_0, active_0, keep, send = units_forward(
-        after(flat_0, near_attn_1, flat_grad_1), units_0, biases_0[3]
+        after(flat_0, far_attn_1, flat_grad_1), units_0, biases_0[3]
     )
     branch_0 = pair_sum(chip_sum(keep, send))
-    result_0 = own_places(
-        block_result(after(middle_0, near_units_1), branch_0, biases_0, mods_0), frames_dev
-    )
-    x_1 = flat(lax.all_to_all(result_0, "dp", split_axis=2, concat_axis=0, tiled=True))
+    result_0 = own_places(block_result(middle_0, branch_0, biases_0, mods_0), frames_dev)
+    arrived = lax.all_to_all(result_0, "dp", split_axis=2, concat_axis=0, tiled=True)
+    x_1 = flat(after(arrived, near_units_1))
 
     wattn_1 = arrange(*near_attn_1, *far_attn_1)
     hidden_1, joined_1, attended_1, both_1, middle_1, hidden_mlp = first_half(
         x_1, mods_1, wattn_1, biases_1, own_place_count
     )
-    flat_1 = pair_rows(hidden_mlp)
+    flat_1 = pair_rows(*hidden_mlp)
     units_1 = arrange(*near_units_1, *far_units_1)
     slope_1, active_1, keep_1, send_1 = units_forward(flat_1, units_1, biases_1[3])
 
     inner_grad_1, keep, send, fc1_bias_1 = units_backward(flat_grad_1, units_1, slope_1)
     chip = chip_sum(keep, send)
     hidden_grad = pair_sum(chip)
-    sums_units_1 = scatter_start(
-        weight_grad(after(((flat_1, inner_grad_1), (flat_grad_1, active_1)), chip))
-    )
-    middle_grad, attn_grad, middle_sums_1 = middle_back(
+    middle_grad, attn_grad_1, middle_sums_1 = middle_back(
         upstream_1, hidden_grad, middle_1, both_1, biases_1, mods_1
     )
-    joined_grad, mine_grad, joined_bias_1 = attention_backward(
-        attn_grad, wattn_1, joined_1, mods_1.shape[0], own_place_count
+    joined_grad_1, mine_grad, joined_bias_1 = attention_backward(
+        attn_grad_1, wattn_1, joined_1, mods_1.shape[0], own_place_count
     )
     x_grad_1, input_sums_1 = input_back(middle_grad, mine_grad, x_1, mods_1, low)
     sent_back = own_places(x_grad_1, all_frames)
     arrived_back = lax.all_to_all(sent_back, "dp", split_axis=0, concat_axis=2, tiled=True)
-    sums_attn_1 = scatter_start(
-        weight_grad(after(((hidden_1, joined_grad), (attn_grad, attended_1)), sent_back))
-    )
-    sums_units_1 = scatter_near(after(sums_units_1, sums_attn_1[0]))
-
-    branch_1 = pair_sum(chip_sum(*after((keep_1, send_1), attn_grad)))
-    output = own_places(block_result(middle_1, branch_1, biases_1, mods_1), all_frames)
-    gate_1 = gate_sums(upstream_1, branch_1, biases_1, mods_1)
+    units_pairs = ((flat_1, inner_grad_1), (flat_grad_1, active_1))
+    units_pairs = after(units_pairs, chip)
+    start_units_1 = scatter_start(weight_grad(units_pairs))
 
     upstream_0 = flat(arrived_back)
     mlp_grad_0, turn_sums_0 = turn(upstream_0, mods_0)
-    flat_grad_0 = pair_rows(mlp_grad_0)
-    inner_grad_0, keep, send, fc1_bias_0 = units_backward(flat_grad_0, units_0, slope_0)
+    part_0 = mlp_grad_0[1]
+    attn_pairs = (((hidden_1,), joined_grad_1), ((attn_grad_1,), attended_1))
+    attn_pairs = after(attn_pairs, sent_back)
+    start_attn_1 = scatter_start(weight_grad(attn_pairs))
+    near_sums = scatter_near_sums(after(start_units_1, start_attn_1[0]))
+    near_units_grad_1 = scatter_near(near_sums)
+    flat_grad_0 = pair_rows(*mlp_grad_0)
+    inner_grad_0, keep, send, fc1_bias_0 = units_backward(
+        flat_grad_0, units_0, slope_0
+    )
     chip = chip_sum(keep, send)
     hidden_grad = pair_sum(chip)
-    sums_units_1, sums_attn_1, chip = together(sums_units_1, sums_attn_1, chip)
-    sums_attn_1 = scatter_near(sums_attn_1)
-    units_blocks = scatter_plane_blocks(sums_units_1)
-    inner_grad_0 = after(inner_grad_0, chip, units_blocks)
-    sums_units_1 = scatter_halve(units_blocks)
-    sums_units_0 = scatter_start(weight_grad(((flat_0, inner_grad_0), (flat_grad_0, active_0))))
     middle_grad, attn_grad, middle_sums_0 = middle_back(
         upstream_0, hidden_grad, middle_0, both_0, biases_0, mods_0
     )
-    sums_attn_1, sums_units_1, attn_grad = together(sums_attn_1, sums_units_1, attn_grad)
-    sums_attn_1 = scatter_halve(scatter_plane_blocks(sums_attn_1))
-    sums_units_1 = scatter_last(sums_units_1)
+    blocks_units_1 = scatter_plane_blocks(near_units_grad_1)
+    half_units_1 = scatter_halve(blocks_units_1)
+    near_sums = scatter_near_sums(after(start_attn_1, chip))
+    near_attn_grad_1 = scatter_near(near_sums)
+    units_pairs = ((flat_0, inner_grad_0), (flat_grad_0, active_0))
+    units_pairs = after(units_pairs, chip, blocks_units_1, near_sums)
+    start_units_0 = scatter_start(weight_grad(units_pairs))
+    blocks_attn_1 = scatter_plane_blocks(after(near_attn_grad_1, attn_grad))
+    half_attn_1 = scatter_halve(blocks_attn_1)
+    held = after(attn_grad, blocks_attn_1)
     joined_grad, mine_grad, joined_bias_0 = attention_backward(
-        attn_grad, wattn_0, joined_0, mods_0.shape[0], None
-    )
-    sums_units_0, joined_grad = together(sums_units_0, joined_grad)
-    sums_units_0 = scatter_near(sums_units_0)
-    sums_attn_0 = scatter_start(weight_grad(((hidden_0, joined_grad), (attn_grad, attended_0))))
-    x_grad_0, input_sums_0 = input_back(middle_grad, mine_grad, x_0, mods_0, wide)
+        held, wattn_0, joined_0, mods_0.shape[0], None
+    )
+    attn_pairs = (((hidden_0,), joined_grad), ((attn_grad,), attended_0))
+    parts = weight_grad(attn_pairs)
+    held = after(parts, start_units_0, half_units_1, half_attn_1)
+    start_attn_0 = scatter_start(held)
+    near_sums = scatter_near_sums(after(start_units_0, parts[0]))
+    near_units_grad_0 = scatter_near(near_sums)
+    x_grad_0, input_sums_0 = input_back(
+        after(middle_grad, parts[0]), mine_grad, x_0, mods_0, wide
+    )
     tokens_grad = own_places(x_grad_0, frames_dev)
     gate_0 = gate_sums(upstream_0, branch_0, biases_0, mods_0)
-    sums_units_0, sums_attn_1, sums_units_1, input_sums_0, gate_0 = together(
-        sums_units_0, sums_attn_1, sums_units_1, input_sums_0, gate_0
-    )
-    units_blocks = scatter_plane_blocks(sums_units_0)
-    sums_units_0 = scatter_halve(units_blocks)
-    sums_attn_1 = scatter_last(sums_attn_1)
-    second_units = scatter_join(sums_units_1, True)
-    mod_0, proj_0, hidden_bias_0 = small_grads(
-        input_sums_0, middle_sums_0, gate_0, turn_sums_0, joined_bias_0, fc1_bias_0
-    )
-    mod_1, proj_1, hidden_bias_1 = small_grads(
-        input_sums_1, middle_sums_1, gate_1, turn_sums_1, joined_bias_1, fc1_bias_1
-    )
-    clips_0 = jnp.sum(onehot[:, :, None, None] * mod_0[:, None], axis=0)
-    small = (
-        jnp.stack([clips_0, mod_1]),
-        jnp.stack([proj_0, proj_1]),
-        jnp.stack([hidden_bias_0, hidden_bias_1]),
-    )
-    dealt = jnp.concatenate([sum_to_owner(piece, all_devices) for piece in small], axis=1)
-    owned = jnp.sum(deal(dealt), axis=0)
-    sums_attn_0 = scatter_near(after(sums_attn_0, units_blocks, owned))
-    own_dmod = owned[:first_end]
-    b_proj_grad = owned[first_end:second_end].reshape(2, 4, own_width)
-    b_fc1_grad = owned[second_end:].reshape(2, -1)
-    summed_mod = from_owners(
-        deal(jnp.broadcast_to(own_dmod[None], (all_devices, own_dmod.shape[0]))), (2, clip_count, 6)
-    )
-    sums_units_0, sums_attn_1, sums_attn_0, summed_mod = together(
-        sums_units_0, sums_attn_1, sums_attn_0, summed_mod
-    )
-    second_attn = scatter_join(sums_attn_1)[0]
-    sums_attn_0 = scatter_planes(sums_attn_0)
-    sums_units_0 = scatter_last(sums_units_0)
-    first_units = scatter_join(sums_units_0, True)
+    last_units_1 = scatter_last(after(half_units_1, parts[0]))
+    blocks_units_0 = scatter_plane_blocks(after(near_units_grad_0, x_grad_0, last_units_1, gate_0))
+    half_units_0 = scatter_halve(blocks_units_0)
+    last_attn_1 = scatter_last(after(half_attn_1, x_grad_0))
+    second_units = scatter_join(last_units_1, True)
+
+    held = after((keep_1, send_1), attn_grad_1, sent_back)
+    branch_1 = pair_sum(chip_sum(*held))
+    output = own_places(block_result(middle_1, branch_1, biases_1, mods_1), all_frames)
+    gate_1 = gate_sums(after(upstream_1, parts[0]), branch_1, biases_1, mods_1)
+
+    input_sums_0 = after(input_sums_0, blocks_units_0, half_attn_1)
+    packed_sums = pack_sums(
+        clip_count,
+        lax.axis_index("dp") * frames_dev,
+        (
+            (input_sums_0, middle_sums_0, gate_0, turn_sums_0, joined_bias_0, fc1_bias_0),
+            (input_sums_1, middle_sums_1, gate_1, turn_sums_1, joined_bias_1, fc1_bias_1),
+        ),
+    )
+    owned = jnp.sum(deal(packed_sums.reshape(all_devices, -1)), axis=0)
+    near_sums = scatter_near_sums(after(start_attn_0, blocks_units_0, owned))
+    near_attn_grad_0 = scatter_near(near_sums)
+    held = after(owned, near_sums)
+    everything = deal(jnp.broadcast_to(held[None], (all_devices, owned.shape[0])))
+    held = after(near_attn_grad_0, everything, last_attn_1, half_units_0)
+    sums_attn_0 = scatter_planes(scatter_plane_blocks(held))
+    held = after(half_units_0, near_attn_grad_0, everything)
+    first_units = scatter_join(scatter_last(held), True)
+    second_attn = scatter_join(after(last_attn_1, near_attn_grad_0, everything))[0]
     first_attn = scatter_finish(sums_attn_0)
+    everything = after(everything, sums_attn_0[0]).reshape(2, -1, width)
+    mod_rows = 6 * clip_count
+    summed_mod = everything[:, :mod_rows].reshape(2, clip_count, 6, width)
+    b_ada_grad = lax.dynamic_slice_in_dim(jnp.sum(summed_mod, axis=1), own_start, own_width, 2)
+    columns = everything[:, mod_rows + 2 : mod_rows + 6].reshape(2, 2, 2, width)[..., :head_width]
+    proj_rows = jnp.concatenate(
+        [
+            jnp.concatenate([columns[:, 0], columns[:, 1]], axis=-1),
+            everything[:, mod_rows : mod_rows + 2],
+        ],
+        axis=1,
+    )
+    b_proj_grad = lax.dynamic_slice_in_dim(proj_rows, own_start, own_width, 2)
+    fc1_rows = everything[:, mod_rows + 6 :].reshape(2, -1)
+    own_units = fc1_rows.shape[1] // all_devices
+    b_fc1_grad = lax.dynamic_slice_in_dim(fc1_rows, flat_index * own_units, own_units, 1)
     w_ada_grad = sum(
         gated_own[clip][None, :, None, None] * summed_mod[:, clip][:, None]
         for clip in range(clip_count)
     )
-    b_ada_grad = jnp.sum(own_dmod.reshape(2, clip_count, 6, own_width), axis=1)
     silu_grad = jnp.stack(
         [
             jnp.sum(summed_mod[:, clip][:, None] * w_ada_wide, axis=(0, 2, 3))

time: 678 us -> 629 us (0.928)
  the two profiles are of different devices: /device:TPU:0 before, /device:TPU:10 now
where the time goes in v4:
time: 629 us; the launch traced here: 618 us
  waiting for transfers between devices  186 us (30%)
  Pallas kernels  164 us (26%)
  starting transfers between devices  104 us (17%)
  other arithmetic  76.6 us (12%)
  local copies, waits for them, and re-layouts  52.3 us (8%)
  blocking collectives  32.7 us (5%)
    ppermute x59, waiting for transfers between devices, swap_by(): return lax.ppermute(values, 'dp', [(i, i ^ offset) for i in range(count)])  128 us
    ppermute x59, starting transfers between devices, swap_by(): return lax.ppermute(values, 'dp', [(i, i ^ offset) for i in range(count)])  68.2 us
    all_to_all x4, waiting for transfers between devices, deal(): lax.all_to_all(values, everyone, split_axis=0, concat_axis=0, tiled=True)  48.7 us
    pallas_call x4, Pallas kernels, units_call(): pl.pallas_call(body, grid_spec=pltpu.PrefetchScalarGridSpec(num_scalar_pr...  36.5 us
    pallas_call x12, Pallas kernels, row_kernel(): pl.pallas_call(steps if alone else body, grid_spec=pltpu.PrefetchScalarGr...  35.7 us
    pallas_call x4, Pallas kernels, weight_grad(): pl.pallas_call(functools.partial(weight_grad_kernel, count, tuple(starts)...  30.3 us
    pallas_call x4, Pallas kernels, arrange(): pl.pallas_call(arrange_kernel, out_shape=jax.ShapeDtypeStruct((groups * 4...  24.1 us
    all_to_all x4, starting transfers between devices, deal(): lax.all_to_all(values, everyone, split_axis=0, concat_axis=0, tiled=True)  23.2 us
  transfers between devices with their start and end apart: 73, of which 29 were waited for; matrix products, arithmetic and copies ran while one was open for 17% of the time, Pallas kernels for 21%

profile of v4, /device:TPU:10, one launch (start us, length us, event | category | flops | bytes accessed | tf_op | source)
XLA Modules:
  0.0 618.3 jit_solution(3880461877139984091)
XLA Ops:
  11.2 6.9 %all-to-all-start = ((f32[32,1,432]{2,1,0:T(1,128)}), f32[32,1,432]{2,1,0:T(1,128)S(1)}, u32[]{:S(2)}, u32[]{:S(2)}) async-start(f32[32,1,432]{2,1,0:T(1,128)} %all_to_all.54), calls=%async_computation | async-start | bytes 131072 | tf_op jit(solution)/shard_map/all_to_all | solution.py:336
  20.1 19.3 %all-to-all-done = f32[32,1,432]{2,1,0:T(1,128)S(1)} async-done(((f32[32,1,432]{2,1,0:T(1,128)}), f32[32,1,432]{2,1,0:T(1,128)S(1)}, u32[]{:S(2)}, u32[]{:S(2)}) %all-to-all-start) | async-done | bytes 55328 | tf_op jit(solution)/shard_map/all_to_all | solution.py:336
  59.8 17.8 %collective-permute-done.4 = bf16[72,2304]{1,0:T(8,128)(2,1)S(1)} collective-permute-done((bf16[72,2304]{1,0:T(8,128)(2,1)S(1)}, bf16[72,2304]{1,0:T(8,128)(2,1)S(1)}, u32[]{:S(2)}, u32[]{:S(2)}) %collective-permute-start.4) | collective-permute-done | bytes 331808 | tf_op jit(solution)/shard_map/ppermute | solution.py:54
  77.7 8.7 %collective-permute-done.5 = bf16[72,2304]{1,0:T(8,128)(2,1)} collective-permute-done((bf16[72,2304]{1,0:T(8,128)(2,1)S(1)}, bf16[72,2304]{1,0:T(8,128)(2,1)}, u32[]{:S(2)}, u32[]{:S(2)}) %collective-permute-start.5) | collective-permute-done | bytes 331808 | tf_op jit(solution)/shard_map/ppermute | solution.py:54
  90.8 8.6 %collective-permute-done.12 = bf16[72,2432]{1,0:T(8,128)(2,1)S(1)} collective-permute-done((bf16[72,2432]{1,0:T(8,128)(2,1)S(1)}, bf16[72,2432]{1,0:T(8,128)(2,1)S(1)}, u32[]{:S(2)}, u32[]{:S(2)}) %collective-permute-start.12) | collective-permute-done | bytes 350240 | tf_op jit(solution)/shard_map/ppermute | solution.py:54
  110.2 9.8 %collective-permute-done.7.along_ref = bf16[4,72,2304]{2,1,0:T(8,128)(2,1)} collective-permute-done((bf16[4,72,2304]{2,1,0:T(8,128)(2,1)S(1)}, bf16[4,72,2304]{2,1,0:T(8,128)(2,1)}, u32[]{:S(2)}, u32[]{:S(2)}) %collective-permute-start.7) | collective-permute-done | bytes 1327136 | tf_op jit(solution)/shard_map/ppermute | solution.py:54
  121.9 7.9 %collective-permute-done.13 = bf16[2,72,2432]{2,1,0:T(8,128)(2,1)S(1)} collective-permute-done((bf16[2,72,2432]{2,1,0:T(8,128)(2,1)}, bf16[2,72,2432]{2,1,0:T(8,128)(2,1)S(1)}, u32[]{:S(2)}, u32[]{:S(2)}) %collective-permute-start.13) | collective-permute-done | bytes 700448 | tf_op jit(solution)/shard_map/ppermute | solution.py:54
  150.7 8.4 %attention.2 = (bf16[256,1152]{1,0:T(8,128)(2,1)}, bf16[256,1792]{1,0:T(8,128)(2,1)}, bf16[256,576]{1,0:T(8,128)(2,1)}, bf16[256,1152]{1,0:T(8,128)(2,1)}) custom-call(bf16[256,1152]{1,0:T(8,128)(2,1)} %bitcast.268, f32[1,6,1152]{2,1,0:T(8,128)} %mul.132.mod_ref.refs_4_.refs_1_, bf16[1152,2432]{1,0:T(8,128)(2,1)} %bitcast.264, ...), custom_call_target="tpu_custom_call" | custom-call | flops 96731136 | bytes 536576 | tf_op jit(solution)/shard_map/attention/pallas_call | solution.py:601
  205.6 8.9 %units.2 = (bf16[512,1152]{1,0:T(8,128)(2,1)}, bf16[512,1152]{1,0:T(8,128)(2,1)}, bf16[2,128,1152]{2,1,0:T(8,128)(2,1)}, bf16[2,128,1152]{2,1,0:T(8,128)(2,1)}) custom-call(s32[3]{0:T(128)} %pad_add_fusion.place_ref, bf16[256,1152]{1,0:T(8,128)(2,1)} %get-tuple-element.291.own_ref.refs_0_, bf16[256,1152]{1,0:T(8,128)(2,1)} %all_gather.37.other_ref.refs_1_, ...), custom_call_target="tpu_custom_call" | custom-call | flops 169869312 | bytes 700416 | tf_op jit(solution)/shard_map/units/pallas_call | solution.py:688
  257.3 8.5 %attention.3 = (bf16[256,1152]{1,0:T(8,128)(2,1)}, bf16[256,1792]{1,0:T(8,128)(2,1)}, bf16[256,576]{1,0:T(8,128)(2,1)}, bf16[256,1152]{1,0:T(8,128)(2,1)}) custom-call(bf16[256,1152]{1,0:T(8,128)(2,1)} %bitcast.271, f32[1,6,1152]{2,1,0:T(8,128)} %squeeze.57.refs_1_.mod_ref.refs_4_, bf16[1152,2432]{1,0:T(8,128)(2,1)} %bitcast.266, ...), custom_call_target="tpu_custom_call" | custom-call | flops 96731136 | bytes 536576 | tf_op jit(solution)/shard_map/attention/pallas_call | solution.py:601
  276.1 7.1 %collective-permute-done.32.high_ref = bf16[2,72,2304]{2,1,0:T(8,128)(2,1)S(1)} collective-permute-done((bf16[2,72,2304]{2,1,0:T(8,128)(2,1)S(1)}, bf16[2,72,2304]{2,1,0:T(8,128)(2,1)S(1)}, u32[]{:S(2)}, u32[]{:S(2)}) %collective-permute-start.32) | collective-permute-done | bytes 663584 | tf_op jit(solution)/shard_map/ppermute | solution.py:54
  293.6 8.9 %units.3 = (bf16[512,1152]{1,0:T(8,128)(2,1)}, bf16[512,1152]{1,0:T(8,128)(2,1)}, bf16[2,128,1152]{2,1,0:T(8,128)(2,1)}, bf16[2,128,1152]{2,1,0:T(8,128)(2,1)}) custom-call(s32[3]{0:T(128)} %pad_add_fusion.place_ref, bf16[256,1152]{1,0:T(8,128)(2,1)} %get-tuple-element.277.own_ref.refs_0_, bf16[256,1152]{1,0:T(8,128)(2,1)} %all_gather.42.other_ref.refs_1_, ...), custom_call_target="tpu_custom_call" | custom-call | flops 169869312 | bytes 700416 | tf_op jit(solution)/shard_map/units/pallas_call | solution.py:688
  302.5 9.3 %units_back.2 = (bf16[512,1152]{1,0:T(8,128)(2,1)}, bf16[2,128,1152]{2,1,0:T(8,128)(2,1)}, bf16[2,128,1152]{2,1,0:T(8,128)(2,1)}, f32[1,1152]{1,0:T(1,128)}) custom-call(s32[3]{0:T(128)} %pad_add_fusion.place_ref, bf16[256,1152]{1,0:T(8,128)(2,1)} %get-tuple-element.280.own_ref.refs_3_, bf16[256,1152]{1,0:T(8,128)(2,1)} %all_gather.39.other_ref.refs_4_, ...), custom_call_target="tpu_custom_call" | custom-call | flops 169869312 | bytes 700416 | tf_op jit(solution)/shard_map/units_back/pallas_call | solution.py:688
  317.1 8.6 %weight_grad.6 = (bf16[4,72,2304]{2,1,0:T(8,128)(2,1)}, bf16[4,72,2304]{2,1,0:T(8,128)(2,1)}, bf16[4,72,2304]{2,1,0:T(8,128)(2,1)}, bf16[2,72,2304]{2,1,0:T(8,128)(2,1)}, bf16[2,72,2304]{2,1,0:T(8,128)(2,1)}) custom-call(s32[3]{0:T(128)} %pad_add_fusion.place_ref, bf16[256,1152]{1,0:T(8,128)(2,1)} %get-tuple-element.277.own_ref.refs_0_, ...), custom_call_target="tpu_custom_call" | custom-call | flops 169869312 | bytes 774144 | tf_op jit(solution)/shard_map/weight_grad/pallas_call | solution.py:217
  334.6 9.7 %attention_back.2 = (bf16[256,1792]{1,0:T(8,128)(2,1)}, bf16[256,1152]{1,0:T(8,128)(2,1)}, f32[1,1,1792]{2,1,0:T(1,128)}) custom-call(bf16[256,1152]{1,0:T(8,128)(2,1)} %get-tuple-element.249.upstream_ref.refs_2_, bf16[1152,2432]{1,0:T(8,128)(2,1)} %bitcast.267, bf16[256,1792]{1,0:T(8,128)(2,1)} %get-tuple-element.231.joined_ref), custom_call_target="tpu_custom_call" | custom-call | flops 113246208 | bytes 538624 | tf_op jit(solution)/shard_map/attention_back/pallas_call | solution.py:625
  388.5 9.3 %units_back.3 = (bf16[512,1152]{1,0:T(8,128)(2,1)}, bf16[2,128,1152]{2,1,0:T(8,128)(2,1)}, bf16[2,128,1152]{2,1,0:T(8,128)(2,1)}, f32[1,1152]{1,0:T(1,128)}) custom-call(s32[3]{0:T(128)} %pad_add_fusion.place_ref, bf16[256,1152]{1,0:T(8,128)(2,1)} %get-tuple-element.294.own_ref.refs_3_, bf16[256,1152]{1,0:T(8,128)(2,1)} %all_gather.46.other_ref.refs_4_, ...), custom_call_target="tpu_custom_call" | custom-call | flops 169869312 | bytes 700416 | tf_op jit(solution)/shard_map/units_back/pallas_call | solution.py:688
  405.4 7.1 %collective-permute-done.53 = bf16[2,72,2304]{2,1,0:T(8,128)(2,1)} collective-permute-done((bf16[2,72,2304]{2,1,0:T(8,128)(2,1)}, bf16[2,72,2304]{2,1,0:T(8,128)(2,1)}, u32[]{:S(2)}, u32[]{:S(2)}) %collective-permute-start.53) | collective-permute-done | bytes 663584 | tf_op jit(solution)/shard_map/ppermute | solution.py:54
  427.4 8.6 %weight_grad.7 = (bf16[4,72,2304]{2,1,0:T(8,128)(2,1)}, bf16[4,72,2304]{2,1,0:T(8,128)(2,1)}, bf16[4,72,2304]{2,1,0:T(8,128)(2,1)}, bf16[2,72,2304]{2,1,0:T(8,128)(2,1)}, bf16[2,72,2304]{2,1,0:T(8,128)(2,1)}) custom-call(s32[3]{0:T(128)} %pad_add_fusion.place_ref, bf16[256,1152]{1,0:T(8,128)(2,1)} %get-tuple-element.291.own_ref.refs_0_, ...), custom_call_target="tpu_custom_call" | custom-call | flops 169869312 | bytes 774144 | tf_op jit(solution)/shard_map/weight_grad/pallas_call | solution.py:217
  448.0 9.7 %attention_back.3 = (bf16[256,1792]{1,0:T(8,128)(2,1)}, bf16[256,1152]{1,0:T(8,128)(2,1)}, f32[1,1,1792]{2,1,0:T(1,128)}) custom-call(bf16[256,1152]{1,0:T(8,128)(2,1)} %get-tuple-element.264.upstream_ref.refs_2_, bf16[1152,2432]{1,0:T(8,128)(2,1)} %bitcast.265, bf16[256,1792]{1,0:T(8,128)(2,1)} %get-tuple-element.265.joined_ref), custom_call_target="tpu_custom_call" | custom-call | flops 113246208 | bytes 538624 | tf_op jit(solution)/shard_map/attention_back/pallas_call | solution.py:625
  471.1 9.5 %collective-permute-done.55 = bf16[1,72,2304]{2,1,0:T(8,128)(2,1)} collective-permute-done((bf16[1,72,2304]{2,1,0:T(8,128)(2,1)}, bf16[1,72,2304]{2,1,0:T(8,128)(2,1)}, u32[]{:S(2)}, u32[]{:S(2)}) %collective-permute-start.55) | collective-permute-done | bytes 331808 | tf_op jit(solution)/shard_map/ppermute | solution.py:54
  523.9 16.7 %all-to-all-done.4 = f32[32,1,1152]{2,1,0:T(1,128)} async-done(((f32[32,1,1152]{2,1,0:T(1,128)}), f32[32,1,1152]{2,1,0:T(1,128)}, u32[]{:S(2)}, u32[]{:S(2)}) %all-to-all-start.4) | async-done | bytes 147488 | tf_op jit(solution)/shard_map/all_to_all | solution.py:336
  558.9 8.5 %all-to-all-done.5 = f32[32,1,1152]{2,1,0:T(1,128)S(1)} async-done(((f32[32,1,1152]{2,1,0:T(1,128)}), f32[32,1,1152]{2,1,0:T(1,128)S(1)}, u32[]{:S(2)}, u32[]{:S(2)}) %all-to-all-start.5) | async-done | bytes 147488 | tf_op jit(solution)/shard_map/all_to_all | solution.py:336
  587.5 10.2 %collective-permute-done.64 = bf16[72,2432]{1,0:T(8,128)(2,1)} collective-permute-done((bf16[72,2432]{1,0:T(8,128)(2,1)}, bf16[72,2432]{1,0:T(8,128)(2,1)}, u32[]{:S(2)}, u32[]{:S(2)}) %collective-permute-start.64) | collective-permute-done | bytes 350240 | tf_op jit(solution)/shard_map/ppermute | solution.py:54
  597.7 8.9 %collective-permute-done.65 = bf16[72,2432]{1,0:T(8,128)(2,1)} collective-permute-done((bf16[72,2432]{1,0:T(8,128)(2,1)}, bf16[72,2432]{1,0:T(8,128)(2,1)}, u32[]{:S(2)}, u32[]{:S(2)}) %collective-permute-start.65) | collective-permute-done | bytes 350240 | tf_op jit(solution)/shard_map/ppermute | solution.py:54
  (423 shorter events, 379.1 us)
Async XLA Ops:
  4.6 42.0 %collective-permute-start.1 = (bf16[72,2432]{1,0:T(8,128)(2,1)}, bf16[72,2432]{1,0:T(8,128)(2,1)}, u32[]{:S(2)}, u32[]{:S(2)}) collective-permute-start(bf16[72,2432]{1,0:T(8,128)(2,1)} %get-tuple-element.478), channel_id=1, source_target_pairs={{0,16},{2,18},{4,20},{6,22},{8,24},{10,26},{12,28},{14,30},{16,0},... | collective-permute-start | bytes 1050632 | tf_op jit(solution)/shard_map/ppermute | solution.py:54
  7.1 39.4 %collective-permute-start = (bf16[72,2432]{1,0:T(8,128)(2,1)}, bf16[72,2432]{1,0:T(8,128)(2,1)}, u32[]{:S(2)}, u32[]{:S(2)}) collective-permute-start(bf16[72,2432]{1,0:T(8,128)(2,1)} %get-tuple-element.478), channel_id=1, source_target_pairs={{0,8},{2,10},{4,12},{6,14},{8,0},{10,2},{12,4},{14,6},{16,24},{18,... | collective-permute-start | bytes 1050632 | tf_op jit(solution)/shard_map/ppermute | solution.py:54
  7.6 39.0 %collective-permute-start.2 = (bf16[72,2432]{1,0:T(8,128)(2,1)}, bf16[72,2432]{1,0:T(8,128)(2,1)}, u32[]{:S(2)}, u32[]{:S(2)}) collective-permute-start(bf16[72,2432]{1,0:T(8,128)(2,1)} %get-tuple-element.478), channel_id=1, source_target_pairs={{0,24},{2,26},{4,28},{6,30},{8,16},{10,18},{12,20},{14,22},{16,8},... | collective-permute-start | bytes 1050632 | tf_op jit(solution)/shard_map/ppermute | solution.py:54
  52.4 37.6 %collective-permute-start.9 = (bf16[4,72,2432]{2,1,0:T(8,128)(2,1)S(1)}, bf16[4,72,2432]{2,1,0:T(8,128)(2,1)}, u32[]{:S(2)}, u32[]{:S(2)}) collective-permute-start(bf16[4,72,2432]{2,1,0:T(8,128)(2,1)S(1)} %pad_maximum_fusion.1.own_ref), channel_id=1, source_target_pairs={{0,4},{2,6},{4,0},{6,2},{8,12},{10,14},{12,8},{14,10},{16,20},{18,... | collective-permute-start | bytes 4202504 | tf_op jit(solution)/shard_map/ppermute | solution.py:54
  53.8 36.2 %collective-permute-start.8 = (bf16[4,72,2432]{2,1,0:T(8,128)(2,1)S(1)}, bf16[4,72,2432]{2,1,0:T(8,128)(2,1)}, u32[]{:S(2)}, u32[]{:S(2)}) collective-permute-start(bf16[4,72,2432]{2,1,0:T(8,128)(2,1)S(1)} %pad_maximum_fusion.1.own_ref), channel_id=1, source_target_pairs={{0,2},{2,0},{4,6},{6,4},{8,10},{10,8},{12,14},{14,12},{16,18},{18,... | collective-permute-start | bytes 4202504 | tf_op jit(solution)/shard_map/ppermute | solution.py:54
  87.9 32.2 %collective-permute-start.7 = (bf16[4,72,2304]{2,1,0:T(8,128)(2,1)S(1)}, bf16[4,72,2304]{2,1,0:T(8,128)(2,1)}, u32[]{:S(2)}, u32[]{:S(2)}) collective-permute-start(bf16[4,72,2304]{2,1,0:T(8,128)(2,1)S(1)} %pad_maximum_fusion.3.own_ref), channel_id=1, source_target_pairs={{0,4},{2,6},{4,0},{6,2},{8,12},{10,14},{12,8},{14,10},{16,20},{18,... | collective-permute-start | bytes 3981320 | tf_op jit(solution)/shard_map/ppermute | solution.py:54
  134.5 39.2 %collective-permute-start.20 = (bf16[4,72,2432]{2,1,0:T(8,128)(2,1)S(1)}, bf16[4,72,2432]{2,1,0:T(8,128)(2,1)S(1)}, u32[]{:S(2)}, u32[]{:S(2)}) collective-permute-start(bf16[4,72,2432]{2,1,0:T(8,128)(2,1)S(1)} %pad_maximum_fusion.2.own_ref), channel_id=1, source_target_pairs={{0,4},{2,6},{4,0},{6,2},{8,12},{10,14},{12,8},{14,10},{16,20},{18,... | collective-permute-start | bytes 4202504 | tf_op jit(solution)/shard_map/ppermute | solution.py:54
  135.7 40.0 %collective-permute-start.18 = (bf16[4,72,2432]{2,1,0:T(8,128)(2,1)S(1)}, bf16[4,72,2432]{2,1,0:T(8,128)(2,1)}, u32[]{:S(2)}, u32[]{:S(2)}) collective-permute-start(bf16[4,72,2432]{2,1,0:T(8,128)(2,1)S(1)} %pad_maximum_fusion.2.own_ref), channel_id=1, source_target_pairs={{0,2},{2,0},{4,6},{6,4},{8,10},{10,8},{12,14},{14,12},{16,18},{18,... | collective-permute-start | bytes 4202504 | tf_op jit(solution)/shard_map/ppermute | solution.py:54
  139.1 38.9 %collective-permute-start.16 = (bf16[2,72,2304]{2,1,0:T(8,128)(2,1)S(1)}, bf16[2,72,2304]{2,1,0:T(8,128)(2,1)}, u32[]{:S(2)}, u32[]{:S(2)}) collective-permute-start(bf16[2,72,2304]{2,1,0:T(8,128)(2,1)S(1)} %pad_maximum_fusion.10), channel_id=1, source_target_pairs={{0,16},{2,18},{4,20},{6,22},{8,24},{10,26},{12,28},{14,30},{16,0},... | collective-permute-start | bytes 1990664 | tf_op jit(solution)/shard_map/ppermute | solution.py:54
  218.4 35.8 %collective-permute-start.28 = (bf16[4,72,2304]{2,1,0:T(8,128)(2,1)}, bf16[4,72,2304]{2,1,0:T(8,128)(2,1)S(1)}, u32[]{:S(2)}, u32[]{:S(2)}) collective-permute-start(bf16[4,72,2304]{2,1,0:T(8,128)(2,1)} %constant_dynamic-update-slice_fusion.own_ref), channel_id=1, source_target_pairs={{0,4},{2,6},{4,0},{6,2},{8,12},{10,14},{12,8},{14,10},{16,20},{18,... | collective-permute-start | bytes 3981320 | tf_op jit(solution)/shard_map/ppermute | solution.py:54
  219.4 34.8 %collective-permute-start.27 = (bf16[4,72,2304]{2,1,0:T(8,128)(2,1)}, bf16[4,72,2304]{2,1,0:T(8,128)(2,1)}, u32[]{:S(2)}, u32[]{:S(2)}) collective-permute-start(bf16[4,72,2304]{2,1,0:T(8,128)(2,1)} %constant_dynamic-update-slice_fusion.own_ref), channel_id=1, source_target_pairs={{0,2},{2,0},{4,6},{6,4},{8,10},{10,8},{12,14},{14,12},{16,18},{18,... | collective-permute-start | bytes 3981320 | tf_op jit(solution)/shard_map/ppermute | solution.py:54
  325.7 40.9 %collective-permute-start.46 = (bf16[4,72,2304]{2,1,0:T(8,128)(2,1)}, bf16[4,72,2304]{2,1,0:T(8,128)(2,1)}, u32[]{:S(2)}, u32[]{:S(2)}) collective-permute-start(bf16[4,72,2304]{2,1,0:T(8,128)(2,1)} %get-tuple-element.286), channel_id=1, source_target_pairs={{0,2},{2,0},{4,6},{6,4},{8,10},{10,8},{12,14},{14,12},{16,18},{18,... | collective-permute-start | bytes 3981320 | tf_op jit(solution)/shard_map/ppermute | solution.py:54
  326.9 39.8 %collective-permute-start.47 = (bf16[4,72,2304]{2,1,0:T(8,128)(2,1)}, bf16[4,72,2304]{2,1,0:T(8,128)(2,1)}, u32[]{:S(2)}, u32[]{:S(2)}) collective-permute-start(bf16[4,72,2304]{2,1,0:T(8,128)(2,1)} %get-tuple-element.287), channel_id=1, source_target_pairs={{0,4},{2,6},{4,0},{6,2},{8,12},{10,14},{12,8},{14,10},{16,20},{18,... | collective-permute-start | bytes 3981320 | tf_op jit(solution)/shard_map/ppermute | solution.py:54
  364.6 52.9 %collective-permute-start.41 = (bf16[4,72,2432]{2,1,0:T(8,128)(2,1)}, bf16[4,72,2432]{2,1,0:T(8,128)(2,1)S(1)}, u32[]{:S(2)}, u32[]{:S(2)}) collective-permute-start(bf16[4,72,2432]{2,1,0:T(8,128)(2,1)} %get-tuple-element.254), channel_id=1, source_target_pairs={{0,2},{2,0},{4,6},{6,4},{8,10},{10,8},{12,14},{14,12},{16,18},{18,... | collective-permute-start | bytes 4202504 | tf_op jit(solution)/shard_map/ppermute | solution.py:54
  365.2 52.4 %collective-permute-start.42 = (bf16[4,72,2432]{2,1,0:T(8,128)(2,1)}, bf16[4,72,2432]{2,1,0:T(8,128)(2,1)}, u32[]{:S(2)}, u32[]{:S(2)}) collective-permute-start(bf16[4,72,2432]{2,1,0:T(8,128)(2,1)} %get-tuple-element.255), channel_id=1, source_target_pairs={{0,4},{2,6},{4,0},{6,2},{8,12},{10,14},{12,8},{14,10},{16,20},{18,... | collective-permute-start | bytes 4202504 | tf_op jit(solution)/shard_map/ppermute | solution.py:54
  368.7 43.8 %collective-permute-start.53 = (bf16[2,72,2304]{2,1,0:T(8,128)(2,1)}, bf16[2,72,2304]{2,1,0:T(8,128)(2,1)}, u32[]{:S(2)}, u32[]{:S(2)}) collective-permute-start(bf16[2,72,2304]{2,1,0:T(8,128)(2,1)} %add_convert_fusion.4), channel_id=1, source_target_pairs={{0,4},{2,6},{4,0},{6,2},{8,12},{10,14},{12,8},{14,10},{16,20},{18,... | collective-permute-start | bytes 1990664 | tf_op jit(solution)/shard_map/ppermute | solution.py:54
  425.0 39.3 %collective-permute-start.54 = (bf16[2,72,2304]{2,1,0:T(8,128)(2,1)}, bf16[2,72,2304]{2,1,0:T(8,128)(2,1)}, u32[]{:S(2)}, u32[]{:S(2)}) collective-permute-start(bf16[2,72,2304]{2,1,0:T(8,128)(2,1)} %pad_maximum_fusion.11), channel_id=1, source_target_pairs={{0,16},{2,18},{4,20},{6,22},{8,24},{10,26},{12,28},{14,30},{16,0},... | collective-permute-start | bytes 1990664 | tf_op jit(solution)/shard_map/ppermute | solution.py:54
  436.0 46.9 %collective-permute-start.49 = (bf16[4,72,2304]{2,1,0:T(8,128)(2,1)}, bf16[4,72,2304]{2,1,0:T(8,128)(2,1)}, u32[]{:S(2)}, u32[]{:S(2)}) collective-permute-start(bf16[4,72,2304]{2,1,0:T(8,128)(2,1)} %get-tuple-element.300), channel_id=1, source_target_pairs={{0,2},{2,0},{4,6},{6,4},{8,10},{10,8},{12,14},{14,12},{16,18},{18,... | collective-permute-start | bytes 3981320 | tf_op jit(solution)/shard_map/ppermute | solution.py:54
  440.1 42.7 %collective-permute-start.50 = (bf16[4,72,2304]{2,1,0:T(8,128)(2,1)}, bf16[4,72,2304]{2,1,0:T(8,128)(2,1)}, u32[]{:S(2)}, u32[]{:S(2)}) collective-permute-start(bf16[4,72,2304]{2,1,0:T(8,128)(2,1)} %get-tuple-element.301), channel_id=1, source_target_pairs={{0,4},{2,6},{4,0},{6,2},{8,12},{10,14},{12,8},{14,10},{16,20},{18,... | collective-permute-start | bytes 3981320 | tf_op jit(solution)/shard_map/ppermute | solution.py:54
  457.7 33.3 %collective-permute-start.45 = (bf16[256,1152]{1,0:T(8,128)(2,1)}, bf16[256,1152]{1,0:T(8,128)(2,1)}, u32[]{:S(2)}, u32[]{:S(2)}) collective-permute-start(bf16[256,1152]{1,0:T(8,128)(2,1)} %get-tuple-element.270.mine_ref), channel_id=1, source_target_pairs={{0,1},{1,0},{2,3},{3,2},{4,5},{5,4},{6,7},{7,6},{8,9},{9,8},{10,11... | collective-permute-start | bytes 1769480 | tf_op jit(solution)/shard_map/ppermute | solution.py:298
  499.7 42.0 %collective-permute-start.57 = (bf16[4,72,2432]{2,1,0:T(8,128)(2,1)}, bf16[4,72,2432]{2,1,0:T(8,128)(2,1)}, u32[]{:S(2)}, u32[]{:S(2)}) collective-permute-start(bf16[4,72,2432]{2,1,0:T(8,128)(2,1)} %get-tuple-element.337), channel_id=1, source_target_pairs={{0,2},{2,0},{4,6},{6,4},{8,10},{10,8},{12,14},{14,12},{16,18},{18,... | collective-permute-start | bytes 4202504 | tf_op jit(solution)/shard_map/ppermute | solution.py:54
  501.1 40.5 %collective-permute-start.58 = (bf16[4,72,2432]{2,1,0:T(8,128)(2,1)}, bf16[4,72,2432]{2,1,0:T(8,128)(2,1)}, u32[]{:S(2)}, u32[]{:S(2)}) collective-permute-start(bf16[4,72,2432]{2,1,0:T(8,128)(2,1)} %get-tuple-element.338), channel_id=1, source_target_pairs={{0,4},{2,6},{4,0},{6,2},{8,12},{10,14},{12,8},{14,10},{16,20},{18,... | collective-permute-start | bytes 4202504 | tf_op jit(solution)/shard_map/ppermute | solution.py:54
  521.4 46.1 %collective-permute-start.62 = (bf16[2,72,2304]{2,1,0:T(8,128)(2,1)}, bf16[2,72,2304]{2,1,0:T(8,128)(2,1)}, u32[]{:S(2)}, u32[]{:S(2)}) collective-permute-start(bf16[2,72,2304]{2,1,0:T(8,128)(2,1)} %pad_maximum_fusion.12), channel_id=1, source_target_pairs={{0,16},{2,18},{4,20},{6,22},{8,24},{10,26},{12,28},{14,30},{16,0},... | collective-permute-start | bytes 1990664 | tf_op jit(solution)/shard_map/ppermute | solution.py:54
  573.7 32.9 %collective-permute-start.65 = (bf16[72,2432]{1,0:T(8,128)(2,1)}, bf16[72,2432]{1,0:T(8,128)(2,1)}, u32[]{:S(2)}, u32[]{:S(2)}) collective-permute-start(bf16[72,2432]{1,0:T(8,128)(2,1)} %get-tuple-element.445), channel_id=1, source_target_pairs={{0,24},{2,26},{4,28},{6,30},{8,16},{10,18},{12,20},{14,22},{16,8},... | collective-permute-start | bytes 1050632 | tf_op jit(solution)/shard_map/ppermute | solution.py:54
  (97 other events, 1305.7 us)
